TPU v7x, 32 devices: a whole 2x2x4 slice. The times are simulated.
32 devices in a mesh: mem: 4 (over x, core), lat: 8 (over z, y).
Axes of the slice: x: 2, y: 2, z: 4, core: 2. Of those that a mesh axis runs over, the one named last changes fastest.
Arguments:
- ensemble: float32 [256, 16, 512], P('mem', 'lat'), may hold values from -6 to 6
- diffusivity: float32 [16, 512], P('lat'), may hold values from 0.02 to 0.2
- north_wind: float32 [16, 512], P('lat'), may hold values from -0.25 to 0.25
- observed_blocks: int32 [8, 4, 4], P('lat'), may hold values from 0 to 7
- eastern_average_flags: int32 [8, 4, 512], P('lat'), may hold values 0 or 1
- observed_values: float32 [8, 4, 512], P('lat', 'mem'), may hold values from -6 to 6
- observed_error: float32 [8, 4, 512], P('lat', 'mem'), may hold values from 0.5 to 4
Outputs:
- analysis: float32 [256, 16, 512], P('mem', 'lat')
Inputs may be any that keep to these rules, and one draw needn't show every extreme that they name: `observed_blocks`: block i covers a band's flattened cells i * 128 to (i + 1) * 128 - 1; blocks may repeat.
All inputs are finite; a program needn't handle non-finite values. No bound on the sum of `eastern_average_flags` on one device may be relied on, other than what follows from the above.
Results may differ from a plain program's by a relative error of at most 0.0003.
Values sent between devices are 32-bit elements; how exact they have to be, the bound alone decides.
No kernel may reach another device: no remote copies, remote signals or barrier semaphores. Data moves between devices by JAX's collectives and lax.ppermute only.
A program may use at most 64 MiB of HBM per device.

v0:
```python
import jax
import jax.numpy as jnp
from jax import lax
from jax.sharding import PartitionSpec as P

OBS = 512
BLOCK = 128
NEWTON = 4


ADVECTION = 0.1
HIGHEST = lax.Precision.HIGHEST


def with_halo(block, sides, width):
    for axis, dim in sides:
        count = lax.axis_size(axis)
        forward = [(i, i + 1) for i in range(count - 1)]
        backward = [(target, source) for source, target in forward]
        low = lax.ppermute(
            lax.slice_in_dim(block, block.shape[dim] - width, None, axis=dim), axis, forward
        )
        high = lax.ppermute(lax.slice_in_dim(block, 0, width, axis=dim), axis, backward)
        block = jnp.concatenate([low, block, high], axis=dim)
    return block


def advance(padded, diffusivity, north_wind):
    centre = padded[:, 1:-1, :]
    northern = padded[:, :-2, :]
    equatorward_side = padded[:, 2:, :]
    eastern = jnp.roll(centre, -1, axis=2)
    western_neighbour = jnp.roll(centre, 1, axis=2)
    return (
        centre
        - ADVECTION * centre * (eastern - western_neighbour)
        - north_wind * (equatorward_side - northern)
        + diffusivity * (eastern + western_neighbour + northern + equatorward_side - 4.0 * centre)
    )


def contract_first(left, right):
    return lax.dot_general(
        left, right, (((0,), (0,)), ((), ())), precision=HIGHEST, preferred_element_type=jnp.float32
    )


def patch_gain(cell_values, seen_values, values, errors):
    sample_states = cell_values.shape[0]
    cell_offset = cell_values - jnp.mean(cell_values, axis=0)
    seen_mean = jnp.mean(seen_values, axis=0)
    seen_offset = seen_values - seen_mean
    covariance = contract_first(seen_offset, seen_offset) / (sample_states - 1.0) + jnp.diag(errors)
    row_scale = jnp.sum(jnp.abs(covariance), axis=1)
    inverse = jnp.diag(1.0 / row_scale)
    for sweep in range(NEWTON):
        product = jnp.dot(
            covariance, inverse, precision=HIGHEST, preferred_element_type=jnp.float32
        )
        inverse = 2.0 * inverse - jnp.dot(
            inverse, product, precision=HIGHEST, preferred_element_type=jnp.float32
        )
    cross_cov = contract_first(cell_offset, seen_offset) / (sample_states - 1.0)
    gain = jnp.dot(cross_cov, inverse, precision=HIGHEST, preferred_element_type=jnp.float32)
    innovation = values - seen_mean
    return (gain, innovation, seen_mean)


def body(
    ensemble,
    diffusivity,
    north_wind,
    observed_blocks,
    eastern_average_flags,
    observed_values,
    observed_error,
):
    local_members, row_count, meridian_total = ensemble.shape
    patch_count = lax.axis_size("mem")
    cell_count = row_count * meridian_total // patch_count
    coefficients = jnp.stack([diffusivity, north_wind])
    coef_rims = with_halo(coefficients, (("lat", 1),), 1)
    widened = with_halo(ensemble, (("lat", 1),), 2)
    variable_layers = advance(advance(widened, coef_rims[0], coef_rims[1]), diffusivity, north_wind)
    block_tiles = variable_layers.reshape(local_members, row_count * meridian_total // BLOCK, BLOCK)
    east_tiles = jnp.roll(variable_layers, -1, axis=2).reshape(
        local_members, row_count * meridian_total // BLOCK, BLOCK
    )
    chosen = observed_blocks[0].reshape(-1)
    direct = jnp.take(block_tiles, chosen, axis=1).reshape(local_members, patch_count, OBS)
    shifted = jnp.take(east_tiles, chosen, axis=1).reshape(local_members, patch_count, OBS)
    observed = jnp.where(eastern_average_flags[0][None] == 1, 0.5 * (direct + shifted), direct)
    owned = variable_layers.reshape(local_members, patch_count, cell_count)
    cell_values, seen_values = (
        lax.all_to_all(owned, "mem", split_axis=1, concat_axis=0, tiled=True),
        lax.all_to_all(observed, "mem", split_axis=1, concat_axis=0, tiled=True),
    )
    cell_values = cell_values[:, 0, :]
    seen_values = seen_values[:, 0, :]
    gain, innovation, seen_mean = patch_gain(
        cell_values, seen_values, observed_values[0, 0], observed_error[0, 0]
    )
    weights = innovation[None, :] - 0.5 * (seen_values - seen_mean[None, :])
    update = lax.dot_general(
        weights,
        gain,
        (((1,), (1,)), ((), ())),
        precision=HIGHEST,
        preferred_element_type=jnp.float32,
    )
    analysed = (cell_values + update)[:, None, :]
    returned = lax.all_to_all(analysed, "mem", split_axis=0, concat_axis=1, tiled=True)
    return returned.reshape(local_members, row_count, meridian_total)


def solution(mesh):
    return jax.shard_map(
        body,
        mesh=mesh,
        in_specs=(
            P("mem", "lat", None),
            P("lat", None),
            P("lat", None),
            P("lat", None, None),
            P("lat", None, None),
            P("lat", "mem", None),
            P("lat", "mem", None),
        ),
        out_specs=P("mem", "lat", None),
        check_vma=False,
    )
```

profile of v0, /device:TPU:0, one launch (start us, length us, event | category | flops | bytes accessed | tf_op | source)
XLA Modules:
  0.0 85.1 jit_solution(7209250416968997480)
XLA Ops:
  0.0 4.9 %collective-permute-start = (f32[64,2,512]{2,1,0:T(2,128)}, f32[64,2,512]{2,1,0:T(2,128)S(1)}, u32[]{:S(2)}, u32[]{:S(2)}) collective-permute-start(f32[64,2,512]{2,1,0:T(2,128)} %param.9), channel_id=1, source_target_pairs={{0,1},{1,2},{2,3},{3,4},{4,5},{5,6},{6,7},{8,9},{9,10},{10,11},{11... | collective-permute-start | bytes 786440 | tf_op jit(solution)/shard_map/ppermute | solution.py:20
  4.9 1.3 %collective-permute-start.1 = (f32[64,2,512]{2,1,0:T(2,128)}, f32[64,2,512]{2,1,0:T(2,128)S(1)}, u32[]{:S(2)}, u32[]{:S(2)}) collective-permute-start(f32[64,2,512]{2,1,0:T(2,128)} %param.9), channel_id=1, source_target_pairs={{1,0},{2,1},{3,2},{4,3},{5,4},{6,5},{7,6},{9,8},{10,9},{11,10},{12... | collective-permute-start | bytes 786440 | tf_op jit(solution)/shard_map/ppermute | solution.py:23
  7.0 4.5 %collective-permute-start.2 = (f32[2,1,512]{2,1,0:T(1,128)S(1)}, f32[2,1,512]{2,1,0:T(1,128)S(1)}, u32[]{:S(2)}, u32[]{:S(2)}) collective-permute-start(f32[2,1,512]{2,1,0:T(1,128)S(1)} %get-tuple-element.14), channel_id=1, source_target_pairs={{0,1},{1,2},{2,3},{3,4},{4,5},{5,6},{6,7},{8,9},{9,10},{10,11},{11... | collective-permute-start | bytes 12296 | tf_op jit(solution)/shard_map/ppermute | solution.py:20
  11.6 1.3 %collective-permute-start.3 = (f32[2,1,512]{2,1,0:T(1,128)S(1)}, f32[2,1,512]{2,1,0:T(1,128)S(1)}, u32[]{:S(2)}, u32[]{:S(2)}) collective-permute-start(f32[2,1,512]{2,1,0:T(1,128)S(1)} %get-tuple-element.15), channel_id=1, source_target_pairs={{1,0},{2,1},{3,2},{4,3},{5,4},{6,5},{7,6},{9,8},{10,9},{11,10},{12... | collective-permute-start | bytes 12296 | tf_op jit(solution)/shard_map/ppermute | solution.py:23
  13.0 3.5 %collective-permute-done.2 = f32[2,1,512]{2,1,0:T(1,128)S(1)} collective-permute-done((f32[2,1,512]{2,1,0:T(1,128)S(1)}, f32[2,1,512]{2,1,0:T(1,128)S(1)}, u32[]{:S(2)}, u32[]{:S(2)}) %collective-permute-start.2) | collective-permute-done | bytes 4128 | tf_op jit(solution)/shard_map/ppermute | solution.py:20
  16.5 1.0 %collective-permute-done.3 = f32[2,1,512]{2,1,0:T(1,128)S(1)} collective-permute-done((f32[2,1,512]{2,1,0:T(1,128)S(1)}, f32[2,1,512]{2,1,0:T(1,128)S(1)}, u32[]{:S(2)}, u32[]{:S(2)}) %collective-permute-start.3) | collective-permute-done | bytes 4128 | tf_op jit(solution)/shard_map/ppermute | solution.py:23
  17.5 1.3 %pad_maximum_fusion = f32[64,6,512]{2,1,0:T(8,128)S(1)} fusion(f32[64,2,512]{2,1,0:T(2,128)S(1)} %collective-permute-done.1, f32[64,2,512]{2,1,0:T(2,128)} %param.9, f32[64,2,512]{2,1,0:T(2,128)S(1)} %collective-permute-done), kind=kLoop, calls=%fused_computation.18 | loop fusion | flops 393216 | bytes 1572864 | tf_op jit(solution)/shard_map/concatenate | solution.py:24
  19.8 1.3 %multiply_add_fusion = f32[64,4,512]{2,1,0:T(4,128)S(1)} fusion(f32[64,2,512]{2,1,0:T(2,128)S(1)} %copy-done, f32[64,2,512]{2,1,0:T(2,128)S(1)} %collective-permute-done, f32[64,2,512]{2,1,0:T(2,128)S(1)} %collective-permute-done.1, f32[64,4,511]{2,1,0:T(4,128)S(1)} %get-tuple-element.7, f32[64,4,511]{2,1,0:T(4,128)S(1)} %get-tuple-element.6, ...), kind=kLoop, calls=%fused_computation.42 | loop fusion | flops 2883584 | bytes 2897920 | tf_op jit(solution)/shard_map/add | solution.py:35
  27.0 3.4 %all-to-all-start = ((f32[64,4,256]{2,0,1:T(8,128)}), f32[64,4,256]{2,0,1:T(8,128)S(1)}, u32[]{:S(2)}, u32[]{:S(2)}) async-start(f32[64,4,256]{2,0,1:T(8,128)} %copy.36), calls=%async_computation | async-start | bytes 524288 | tf_op jit(solution)/shard_map/all_to_all | solution.py:95
  30.6 1.0 %copy.41 = f32[64,4,512]{2,0,1:T(8,128)} copy(f32[64,4,512]{2,1,0:T(4,128)S(1)} %multiply_select_fusion) | data formatting | bytes 1048576 | tf_op jit(solution)/shard_map/jit(_where)/select_n | solution.py:92
  31.6 4.8 %all-to-all-done = f32[64,4,256]{2,0,1:T(8,128)S(1)} async-done(((f32[64,4,256]{2,0,1:T(8,128)}), f32[64,4,256]{2,0,1:T(8,128)S(1)}, u32[]{:S(2)}, u32[]{:S(2)}) %all-to-all-start) | async-done | bytes 262176 | tf_op jit(solution)/shard_map/all_to_all | solution.py:95
  36.4 3.6 %all-to-all-start.1 = ((f32[64,4,512]{2,0,1:T(8,128)}), f32[64,4,512]{2,0,1:T(8,128)S(1)}, u32[]{:S(2)}, u32[]{:S(2)}) async-start(f32[64,4,512]{2,0,1:T(8,128)} %copy.41), calls=%async_computation.1 | async-start | bytes 1048576 | tf_op jit(solution)/shard_map/all_to_all | solution.py:96
  40.1 8.5 %all-to-all-done.1 = f32[64,4,512]{2,0,1:T(8,128)S(1)} async-done(((f32[64,4,512]{2,0,1:T(8,128)}), f32[64,4,512]{2,0,1:T(8,128)S(1)}, u32[]{:S(2)}, u32[]{:S(2)}) %all-to-all-start.1) | async-done | bytes 524320 | tf_op jit(solution)/shard_map/all_to_all | solution.py:96
  50.0 1.2 %abs_reduce_fusion = (f32[512]{0:T(512)S(1)}, f32[512,512]{0,1:T(8,128)S(1)}) fusion(f32[512]{0:T(512)S(1)} %bitcast.94, f32[64,4,512]{2,0,1:T(8,128)S(1)} %all-to-all-done.1, f32[512]{0:T(512)S(1)} %get-tuple-element.17), kind=kOutput, calls=%fused_computation.19 | convolution fusion | flops 807009792 | bytes 1579008 | tf_op jit(solution)/shard_map/dot_general | solution.py:43
  51.2 3.5 %fusion.2 = f32[512,512]{1,0:T(8,128)S(1)} fusion(f32[512,512]{0,1:T(8,128)S(1)} %get-tuple-element.21, f32[512]{0:T(512)S(1)} %broadcast_divide_fusion), kind=kOutput, calls=%fused_computation.4 | convolution fusion | flops 1611137024 | bytes 2099200 | tf_op jit(solution)/shard_map/dot_general | solution.py:57
  54.7 1.9 %fusion.4 = f32[512,512]{0,1:T(8,128)S(1)} fusion(f32[512,512]{1,0:T(8,128)S(1)} %fusion.2, f32[512]{0:T(512)S(1)} %broadcast_divide_fusion), kind=kOutput, calls=%fused_computation.7 | convolution fusion | flops 1612185600 | bytes 2099200 | tf_op jit(solution)/shard_map/dot_general | solution.py:60
  56.6 3.5 %fusion.32 = f32[512,512]{1,0:T(8,128)S(1)} fusion(f32[512,512]{0,1:T(8,128)S(1)} %get-tuple-element.21, f32[512,512]{0,1:T(8,128)S(1)} %fusion.4), kind=kOutput, calls=%fused_computation.72 | convolution fusion | flops 1610612736 | bytes 3145728 | tf_op jit(solution)/shard_map/dot_general | solution.py:57
  60.1 1.9 %convolution_subtract_fusion.2 = f32[512,512]{0,1:T(8,128)S(1)} fusion(f32[512,512]{0,1:T(8,128)S(1)} %fusion.4, f32[512,512]{1,0:T(8,128)S(1)} %fusion.32), kind=kOutput, calls=%fused_computation.10 | convolution fusion | flops 1611137024 | bytes 3145728 | tf_op jit(solution)/shard_map/dot_general | solution.py:60
  62.0 3.7 %fusion.33 = f32[512,512]{1,0:T(8,128)S(1)} fusion(f32[512,512]{0,1:T(8,128)S(1)} %get-tuple-element.21, f32[512,512]{0,1:T(8,128)S(1)} %convolution_subtract_fusion.2), kind=kOutput, calls=%fused_computation.73 | convolution fusion | flops 1610612736 | bytes 3145728 | tf_op jit(solution)/shard_map/dot_general | solution.py:57
  65.7 1.9 %convolution_subtract_fusion.1 = f32[512,512]{0,1:T(8,128)S(1)} fusion(f32[512,512]{0,1:T(8,128)S(1)} %convolution_subtract_fusion.2, f32[512,512]{1,0:T(8,128)S(1)} %fusion.33), kind=kOutput, calls=%fused_computation.9 | convolution fusion | flops 1611137024 | bytes 3145728 | tf_op jit(solution)/shard_map/dot_general | solution.py:60
  67.5 3.5 %fusion.34 = f32[512,512]{1,0:T(8,128)S(1)} fusion(f32[512,512]{0,1:T(8,128)S(1)} %get-tuple-element.21, f32[512,512]{0,1:T(8,128)S(1)} %convolution_subtract_fusion.1), kind=kOutput, calls=%fused_computation.74 | convolution fusion | flops 1610612736 | bytes 3145728 | tf_op jit(solution)/shard_map/dot_general | solution.py:57
  71.0 1.9 %convolution_subtract_fusion = f32[512,512]{0,1:T(8,128)S(1)} fusion(f32[512,512]{0,1:T(8,128)S(1)} %convolution_subtract_fusion.1, f32[512,512]{1,0:T(8,128)S(1)} %fusion.34), kind=kOutput, calls=%fused_computation.8 | convolution fusion | flops 1611137024 | bytes 3145728 | tf_op jit(solution)/shard_map/dot_general | solution.py:60
  73.6 1.1 %fusion.35 = f32[256,512]{1,0:T(8,128)S(1)} fusion(f32[256,512]{1,0:T(8,128)S(1)} %fusion.9, f32[512,512]{0,1:T(8,128)S(1)} %convolution_subtract_fusion), kind=kOutput, calls=%fused_computation.75 | convolution fusion | flops 805306368 | bytes 2097152 | tf_op jit(solution)/shard_map/dot_general | solution.py:64
  75.6 8.4 %all_to_all.45 = f32[256,1,256]{2,1,0:T(1,128)S(1)} all-to-all(f32[256,1,256]{2,1,0:T(1,128)S(1)} %copy.46), channel_id=1, replica_groups=mesh['mem'=4,'lat'=8] {'mem'}, dimensions={0} | all-to-all | bytes 524288 | tf_op jit(solution)/shard_map/all_to_all | solution.py:112
  (56 shorter events, 12.0 us)
Async XLA Ops:
  0.0 17.5 %collective-permute-start = (f32[64,2,512]{2,1,0:T(2,128)}, f32[64,2,512]{2,1,0:T(2,128)S(1)}, u32[]{:S(2)}, u32[]{:S(2)}) collective-permute-start(f32[64,2,512]{2,1,0:T(2,128)} %param.9), channel_id=1, source_target_pairs={{0,1},{1,2},{2,3},{3,4},{4,5},{5,6},{6,7},{8,9},{9,10},{10,11},{11... | collective-permute-start | bytes 786440 | tf_op jit(solution)/shard_map/ppermute | solution.py:20
  4.9 12.6 %collective-permute-start.1 = (f32[64,2,512]{2,1,0:T(2,128)}, f32[64,2,512]{2,1,0:T(2,128)S(1)}, u32[]{:S(2)}, u32[]{:S(2)}) collective-permute-start(f32[64,2,512]{2,1,0:T(2,128)} %param.9), channel_id=1, source_target_pairs={{1,0},{2,1},{3,2},{4,3},{5,4},{6,5},{7,6},{9,8},{10,9},{11,10},{12... | collective-permute-start | bytes 786440 | tf_op jit(solution)/shard_map/ppermute | solution.py:23
  6.2 6.7 %copy-start.4 = (s32[1,4,4]{2,1,0:T(4,128)S(1)}, s32[1,4,4]{2,1,0:T(4,128)}, u32[]{:S(2)}) copy-start(s32[1,4,4]{2,1,0:T(4,128)} %param.12) | copy-start | bytes 196
  7.0 6.0 %copy-start.3 = (s32[1,4,512]{2,1,0:T(4,128)S(1)}, s32[1,4,512]{2,1,0:T(4,128)}, u32[]{:S(2)}) copy-start(s32[1,4,512]{2,1,0:T(4,128)} %param.13) | copy-start | bytes 24580
  7.0 9.5 %collective-permute-start.2 = (f32[2,1,512]{2,1,0:T(1,128)S(1)}, f32[2,1,512]{2,1,0:T(1,128)S(1)}, u32[]{:S(2)}, u32[]{:S(2)}) collective-permute-start(f32[2,1,512]{2,1,0:T(1,128)S(1)} %get-tuple-element.14), channel_id=1, source_target_pairs={{0,1},{1,2},{2,3},{3,4},{4,5},{5,6},{6,7},{8,9},{9,10},{10,11},{11... | collective-permute-start | bytes 12296 | tf_op jit(solution)/shard_map/ppermute | solution.py:20
  11.6 5.9 %collective-permute-start.3 = (f32[2,1,512]{2,1,0:T(1,128)S(1)}, f32[2,1,512]{2,1,0:T(1,128)S(1)}, u32[]{:S(2)}, u32[]{:S(2)}) collective-permute-start(f32[2,1,512]{2,1,0:T(1,128)S(1)} %get-tuple-element.15), channel_id=1, source_target_pairs={{1,0},{2,1},{3,2},{4,3},{5,4},{6,5},{7,6},{9,8},{10,9},{11,10},{12... | collective-permute-start | bytes 12296 | tf_op jit(solution)/shard_map/ppermute | solution.py:23
  13.0 4.5 %copy-start.2 = (f32[2,512]{1,0:T(2,128)S(1)}, f32[2,512]{1,0:T(2,128)}, u32[]{:S(2)}) copy-start(f32[2,512]{1,0:T(2,128)} %param.11) | copy-start | bytes 12292
  13.0 4.5 %copy-start.1 = (f32[2,512]{1,0:T(2,128)S(1)}, f32[2,512]{1,0:T(2,128)}, u32[]{:S(2)}) copy-start(f32[2,512]{1,0:T(2,128)} %param.10) | copy-start | bytes 12292
  18.8 1.0 %copy-start = (f32[64,2,512]{2,1,0:T(2,128)S(1)}, f32[64,2,512]{2,1,0:T(2,128)}, u32[]{:S(2)}) copy-start(f32[64,2,512]{2,1,0:T(2,128)} %param.9) | copy-start | bytes 786436
  27.0 9.4 %all-to-all-start = ((f32[64,4,256]{2,0,1:T(8,128)}), f32[64,4,256]{2,0,1:T(8,128)S(1)}, u32[]{:S(2)}, u32[]{:S(2)}) async-start(f32[64,4,256]{2,0,1:T(8,128)} %copy.36), calls=%async_computation | async-start | bytes 524288 | tf_op jit(solution)/shard_map/all_to_all | solution.py:95
  36.4 12.3 %all-to-all-start.1 = ((f32[64,4,512]{2,0,1:T(8,128)}), f32[64,4,512]{2,0,1:T(8,128)S(1)}, u32[]{:S(2)}, u32[]{:S(2)}) async-start(f32[64,4,512]{2,0,1:T(8,128)} %copy.41), calls=%async_computation.1 | async-start | bytes 1048576 | tf_op jit(solution)/shard_map/all_to_all | solution.py:96
  48.7 0.7 copy-start.5
  49.3 0.7 copy-start.6
where the time goes:
time: 85.7 us; the launch traced here: 85.1 us
  matrix products  25.2 us (29%)
  starting transfers between devices  19.1 us (22%)
  waiting for transfers between devices  17.8 us (21%)
  local copies, waits for them, and re-layouts  9.31 us (11%)
  blocking collectives  8.39 us (10%)
  other arithmetic  4.96 us (6%)
    dot_general x4, matrix products, patch_gain(): jnp.dot(covariance, inverse, precision=HIGHEST, preferred_element_type=jn...  14.1 us
    ppermute x2, starting transfers between devices, with_halo(): lax.ppermute(lax.slice_in_dim(block, block.shape[dim] - width, None, axis...  9.45 us
    all_to_all x1, waiting for transfers between devices, body(): lax.all_to_all(observed, 'mem', split_axis=1, concat_axis=0, tiled=True)  8.54 us
    all_to_all x1, blocking collectives, body(): lax.all_to_all(analysed, 'mem', split_axis=0, concat_axis=1, tiled=True)  8.39 us
    dot_general x4, matrix products, patch_gain(): jnp.dot(inverse, product, precision=HIGHEST, preferred_element_type=jnp.f...  7.55 us
    all_to_all x1, waiting for transfers between devices, body(): lax.all_to_all(owned, 'mem', split_axis=1, concat_axis=0, tiled=True)  4.83 us
    all_to_all x1, starting transfers between devices, body(): lax.all_to_all(observed, 'mem', split_axis=1, concat_axis=0, tiled=True)  3.65 us
    ppermute x2, waiting for transfers between devices, with_halo(): lax.ppermute(lax.slice_in_dim(block, block.shape[dim] - width, None, axis...  3.46 us
  transfers between devices with their start and end apart: 6, of which 4 were waited for; matrix products, arithmetic and copies ran while one was open for 2% of the time, Pallas kernels for 0%

commit v1 on v0

v1 whole, which is shorter than its diff:
```python
import functools

import jax
import jax.numpy as jnp
from jax import lax
from jax.experimental import pallas as pl
from jax.experimental.pallas import tpu as pltpu
from jax.sharding import PartitionSpec as P

NEWTON = 4
ADVECTION = 0.1
F32 = jnp.float32
BF16 = jnp.bfloat16
VMEM = pl.BlockSpec(memory_space=pltpu.VMEM)
SMEM = pl.BlockSpec(memory_space=pltpu.SMEM)


def xor_pairs(count, bit):
    return [(i, i ^ bit) for i in range(count)]


def step(rows, diffusivity, north_wind):
    out = []
    for r in range(1, len(rows) - 1):
        north, centre, south = rows[r - 1], rows[r], rows[r + 1]
        last = centre.shape[1] - 1
        eastern = pltpu.roll(centre, last, 1)
        western = pltpu.roll(centre, 1, 1)
        out.append(
            centre
            - ADVECTION * centre * (eastern - western)
            - north_wind[r - 1] * (south - north)
            + diffusivity[r - 1] * (eastern + western + north + south - 4.0 * centre)
        )
    return out


def forecast_kernel(first, count, lead, own, dif, wind, near, far, coef_near, coef_far, out):
    even = lax.rem(lax.axis_index("lat"), 2) == 0
    rows, longitudes = own.shape[1], own.shape[2]
    edge = near.shape[1]

    def pick(a, b):
        return jnp.where(even, a, b)

    def members(ref, r):
        return ref[lead : lead + count, r, :]

    low = [pick(members(far, r), members(near, r)) for r in (edge - 2, edge - 1)]
    high = [pick(members(near, r), members(far, r)) for r in (0, 1)]
    here = [own[first : first + count, r, :] for r in range(rows)]

    def coefficient(which, ref):
        before = pick(coef_far[which : which + 1, edge - 1, :], coef_near[which : which + 1, edge - 1, :])
        after = pick(coef_near[which : which + 1, 0, :], coef_far[which : which + 1, 0, :])
        return [before] + [ref[r : r + 1, :] for r in range(rows)] + [after]

    d, w = coefficient(0, dif), coefficient(1, wind)
    once = step(low + here + high, d, w)
    twice = step(once, d[1:-1], w[1:-1])
    for r in range(rows):
        out[:, r * longitudes : (r + 1) * longitudes] = twice[r]


def split(x):
    high = x.astype(BF16)
    return high, (x - high.astype(F32)).astype(BF16)


def dot3(a, b, dims=(((1,), (0,)), ((), ()))):
    mul = functools.partial(lax.dot_general, dimension_numbers=dims, preferred_element_type=F32)
    return mul(a[0], b[0]) + (mul(a[0], b[1]) + mul(a[1], b[0]))


def gain_kernel(groups, pieces, tops, longitudes, blocks, flags, values, errors, *refs):
    parts = refs[: groups * pieces]
    outs = refs[groups * pieces : -2]
    seen, cells = refs[-2:]
    patch = lax.axis_index("mem")
    total, observations = seen.shape
    own_cells = cells.shape[1]
    block_count = blocks.shape[1]
    width = observations // block_count
    row_blocks = longitudes // width
    flag = flags[pl.ds(patch, 1), :]
    lane = lax.broadcasted_iota(jnp.int32, (1, width), 1)
    for i in range(block_count):
        c = blocks[patch, i]
        row = lax.div(c, row_blocks)
        n = row * row_blocks + lax.rem(c - row * row_blocks + 1, row_blocks)
        averaged = flag[:, i * width : (i + 1) * width] == 1
        at = 0
        for part in parts:
            size = part.shape[0]
            direct = part[:, pl.ds(pl.multiple_of(c * width, width), width)]
            beyond = part[:, pl.ds(pl.multiple_of(n * width, width), width)]
            east = jnp.where(
                lane == width - 1, pltpu.roll(beyond, width - 1, 1), pltpu.roll(direct, width - 1, 1)
            )
            seen[at : at + size, i * width : (i + 1) * width] = jnp.where(
                averaged, 0.5 * (direct + east), direct
            )
            at += size
    at = 0
    for part in parts:
        size = part.shape[0]
        cells[at : at + size, :] = part[:, pl.ds(pl.multiple_of(patch * own_cells, own_cells), own_cells)]
        at += size
    scale = 1.0 / (total - 1.0)
    raw = seen[...]
    seen_mean = jnp.sum(raw, axis=0, keepdims=True) * (1.0 / total)
    offset = raw - seen_mean
    off = split(offset)
    turned = split(offset.T)
    covariance = dot3(turned, off) * scale
    down = lax.broadcasted_iota(jnp.int32, covariance.shape, 0)
    across = lax.broadcasted_iota(jnp.int32, covariance.shape, 1)
    covariance = covariance + jnp.where(down == across, errors[...], 0.0)
    inverse_scale = 1.0 / jnp.sum(jnp.abs(covariance), axis=0, keepdims=True)
    start = ((values[...] - seen_mean) - 0.5 * offset) * inverse_scale
    b1 = covariance * inverse_scale
    s1 = split(b1)
    b2 = 2.0 * b1 - dot3(s1, s1)
    s2 = split(b2)
    b4 = 2.0 * b2 - dot3(s2, s2)
    s4 = split(b4)
    q = start
    for _ in range(3):
        q = start + (q - dot3(split(q), s4))
    q = 2.0 * q - dot3(split(q), s2)
    q = 2.0 * q - dot3(split(q), s1)
    mix = dot3(split(q), off, (((1,), (1,)), ((), ()))) * scale
    state = cells[...]
    shift = state - jnp.sum(state, axis=0, keepdims=True) * (1.0 / total)
    analysed = state + dot3(split(mix), split(shift))
    size = total // groups
    for out, wanted in zip(outs, tops):
        for at, j in enumerate(wanted):
            out[at * size : (at + 1) * size, :] = analysed[j * size : (j + 1) * size, :]


def place_kernel(masks, where, longitudes, *refs):
    sources, out = refs[:-1], refs[-1]
    here = lax.axis_index("mem")
    local = out.shape[0]
    width = sources[0].shape[1]
    found = [sources[where[m][0]][where[m][1] * local : (where[m][1] + 1) * local, :] for m in masks]
    for patch in range(len(masks)):
        value = found[0]
        for m, candidate in zip(masks[1:], found[1:]):
            value = jnp.where((here ^ m) == patch, candidate, value)
        row, column = divmod(patch * width, longitudes)
        out[:, row, column : column + width] = value


def body(
    ensemble,
    diffusivity,
    north_wind,
    observed_blocks,
    eastern_average_flags,
    observed_values,
    observed_error,
):
    local, rows, longitudes = ensemble.shape
    lats, mems = lax.axis_size("lat"), lax.axis_size("mem")
    observations = observed_values.shape[-1]
    cell_count = rows * longitudes
    own_cells = cell_count // mems
    total = local * mems
    near_pairs = xor_pairs(lats, 1)
    far_pairs = [(i, i + 2) for i in range(0, lats - 2, 2)] + [(i, i - 2) for i in range(3, lats, 2)]

    def edges(block):
        if block.shape[1] == 2:
            return block
        return jnp.concatenate([block[:, :2], block[:, -2:]], axis=1)

    pieces = 2
    count = local // pieces
    bits = [1 << k for k in reversed(range(mems.bit_length() - 1))]
    coefficients = edges(jnp.stack([diffusivity, north_wind]))
    near, far = [], []
    for k in range(pieces):
        own = edges(ensemble[k * count : (k + 1) * count])
        if k == 0:
            own = jnp.concatenate([coefficients, own], axis=0)
        near.append(lax.ppermute(own, "lat", near_pairs))
    for k in range(pieces):
        far.append(lax.ppermute(near[k], "lat", far_pairs))
    parts = [[] for _ in range(pieces)]
    for k in range(pieces):
        band = pl.pallas_call(
            functools.partial(forecast_kernel, k * count, count, 2 if k == 0 else 0),
            out_shape=jax.ShapeDtypeStruct((count, cell_count), F32),
            in_specs=[VMEM] * 7,
            out_specs=VMEM,
            cost_estimate=pl.CostEstimate(flops=2000000, bytes_accessed=2000000, transcendentals=0),
            name="forecast",
        )(ensemble, diffusivity, north_wind, near[k], far[k], near[0], far[0])
        held = [band]
        for bit in bits:
            held = held + [lax.ppermute(a, "mem", xor_pairs(mems, bit)) for a in held]
        parts[k] = held
    masks = [0]
    for bit in bits:
        masks = masks + [m ^ bit for m in masks]

    tops = [[j for j, m in enumerate(masks) if (m & bit) and m < 2 * bit] for bit in bits]
    tops.append([0])
    flat = [parts[k][j] for j in range(mems) for k in range(pieces)]
    shapes = [jax.ShapeDtypeStruct((len(t) * local, own_cells), F32) for t in tops]
    outs = pl.pallas_call(
        functools.partial(gain_kernel, mems, pieces, tops, longitudes),
        out_shape=shapes,
        in_specs=[SMEM] + [VMEM] * (3 + len(flat)),
        out_specs=[VMEM] * len(shapes),
        scratch_shapes=[pltpu.VMEM((total, observations), F32), pltpu.VMEM((total, own_cells), F32)],
        cost_estimate=pl.CostEstimate(flops=5000000000, bytes_accessed=4000000, transcendentals=0),
        name="gain",
    )(observed_blocks[0], eastern_average_flags[0], observed_values[0], observed_error[0], *flat)
    carried = [(outs[-1], [(0, 0)])]
    for bit, sent, top in zip(bits, outs, tops):
        moving = [(a, g) for a, g in carried if any(left & bit for left, _ in g)]
        moving.append((sent, [(masks[j], 0) for j in top]))
        stay = [(a, [(left if not left & bit else -1, pm) for left, pm in g]) for a, g in carried]
        came = [
            (
                lax.ppermute(a, "mem", xor_pairs(mems, bit)),
                [(left ^ bit if left > 0 and left & bit else -1, pm ^ bit) for left, pm in g],
            )
            for a, g in moving
        ]
        carried = stay + came
    where = {}
    for index, (_, g) in enumerate(carried):
        for at, (left, pm) in enumerate(g):
            if left == 0:
                where[pm] = (index, at)
    return pl.pallas_call(
        functools.partial(place_kernel, masks, where, longitudes),
        out_shape=jax.ShapeDtypeStruct((local, rows, longitudes), F32),
        in_specs=[VMEM] * len(carried),
        out_specs=VMEM,
        cost_estimate=pl.CostEstimate(flops=100000, bytes_accessed=600000, transcendentals=0),
        name="place",
    )(*[a for a, _ in carried])


def solution(mesh):
    return jax.shard_map(
        body,
        mesh=mesh,
        in_specs=(
            P("mem", "lat", None),
            P("lat", None),
            P("lat", None),
            P("lat", None, None),
            P("lat", None, None),
            P("lat", "mem", None),
            P("lat", "mem", None),
        ),
        out_specs=P("mem", "lat", None),
        check_vma=False,
    )
```

time: 85.7 us -> 50.3 us (0.59)
  matrix products: 25.2 us -> 0 us
  Pallas kernels: 0 us -> 14.7 us
  blocking collectives: 8.39 us -> 0 us
  local copies, waits for them, and re-layouts: 9.31 us -> 4.32 us
  starting transfers between devices: 19.1 us -> 14.2 us
  other arithmetic: 4.96 us -> 0.06 us
  waiting for transfers between devices: 17.8 us -> 16.6 us
    dot_general x12 -> x0, matrix products: 25.2 us -> none  [the longest x4 14.1 us: patch_gain(): jnp.dot(covariance, inverse, precision=HIGHEST, preferred_element_type=jn...]
    pallas_call x0 -> x4, Pallas kernels: none -> 14.7 us  [the longest x1 8.15 us: body(): pl.pallas_call(functools.partial(gain_kernel, mems, pieces, tops, longitu...]
    all_to_all x2 -> x0, waiting for transfers between devices: 13.4 us -> none  [the longest x1 8.54 us: body(): lax.all_to_all(observed, 'mem', split_axis=1, concat_axis=0, tiled=True)]
    ppermute x4 -> x13, waiting for transfers between devices: 4.43 us -> 16.6 us  [the longest x3 6.34 us: body(): lax.ppermute(a, 'mem', xor_pairs(mems, bit))]
    all_to_all x1 -> x0, blocking collectives: 8.39 us -> none  [body(): lax.all_to_all(analysed, 'mem', split_axis=0, concat_axis=1, tiled=True)]
    all_to_all x2 -> x0, starting transfers between devices: 7.06 us -> none  [the longest x1 3.65 us: body(): lax.all_to_all(observed, 'mem', split_axis=1, concat_axis=0, tiled=True)]
    reshape x9 -> x0, local copies, waits for them, and re-layouts: 2.83 us -> none  [the longest x2 1.01 us: body(): owned = variable_layers.reshape(local_members, patch_count, cell_count)]
    add x2 -> x0, other arithmetic: 2.17 us -> none  [advance(): centre - ADVECTION * centre * (eastern - western_neighbour)]
  transfers between devices with their start and end apart: 6 -> 13, of which waited for: 4 -> 7; matrix products, arithmetic and copies ran while one was open for 2% -> 0% of each run, Pallas kernels for 0% -> 9%
where the time goes in v1:
time: 50.3 us; the launch traced here: 50 us
  waiting for transfers between devices  16.6 us (33%)
  Pallas kernels  14.7 us (29%)
  starting transfers between devices  14.2 us (28%)
  local copies, waits for them, and re-layouts  4.32 us (9%)
    pallas_call x1, Pallas kernels, body(): pl.pallas_call(functools.partial(gain_kernel, mems, pieces, tops, longitu...  8.15 us
    ppermute x2, starting transfers between devices, body(): far.append(lax.ppermute(near[k], 'lat', far_pairs))  7.46 us
    ppermute x3, waiting for transfers between devices, body(): lax.ppermute(a, 'mem', xor_pairs(mems, bit))  6.34 us
    ppermute x6, waiting for transfers between devices, body(): held = held + [lax.ppermute(a, 'mem', xor_pairs(mems, bit)) for a in held]  5.42 us
    pallas_call x2, Pallas kernels, body(): pl.pallas_call(functools.partial(forecast_kernel, k * count, count, 2 if...  4.72 us
    ppermute x2, waiting for transfers between devices, body(): near.append(lax.ppermute(own, 'lat', near_pairs))  4.45 us
    unnamed x32, local copies, waits for them, and re-layouts  3.32 us
    ppermute x2, starting transfers between devices, body(): near.append(lax.ppermute(own, 'lat', near_pairs))  3.14 us
  transfers between devices with their start and end apart: 13, of which 7 were waited for; matrix products, arithmetic and copies ran while one was open for 0% of the time, Pallas kernels for 9%

profile of v1, /device:TPU:0, one launch (start us, length us, event | category | flops | bytes accessed | tf_op | source)
XLA Modules:
  0.0 50.0 jit_solution(12456385208178580552)
XLA Ops:
  0.0 1.0 %fusion = (f32[32,2,512]{2,1,0:T(2,128)S(1)}, f32[32,2,512]{2,1,0:T(2,128)S(1)}) fusion(f32[64,2,512]{2,1,0:T(2,128)} %own.3), kind=kLoop, calls=%fused_computation.1 | loop fusion | bytes 524288 | tf_op jit(solution)/shard_map/slice | solution.py:185
  1.0 0.7 %copy-done.8 = f32[2,512]{1,0:T(2,128)S(1)} copy-done((f32[2,512]{1,0:T(2,128)S(1)}, f32[2,512]{1,0:T(2,128)}, u32[]{:S(2)}) %copy-start.8) | copy-done | bytes 4120
  1.8 3.1 %collective-permute-start = (f32[34,2,512]{2,1,0:T(2,128)S(1)}, f32[34,2,512]{2,1,0:T(2,128)S(1)}, u32[]{:S(2)}, u32[]{:S(2)}) collective-permute-start(f32[34,2,512]{2,1,0:T(2,128)S(1)} %pad_maximum_fusion), channel_id=1, source_target_pairs={{0,1},{1,0},{2,3},{3,2},{4,5},{5,4},{6,7},{7,6},{8,9},{9,8},{10,11... | collective-permute-start | bytes 417800 | tf_op jit(solution)/shard_map/ppermute | solution.py:188
  4.9 4.4 %collective-permute-done.near.coef_near = f32[34,2,512]{2,1,0:T(2,128)S(1)} collective-permute-done((f32[34,2,512]{2,1,0:T(2,128)S(1)}, f32[34,2,512]{2,1,0:T(2,128)S(1)}, u32[]{:S(2)}, u32[]{:S(2)}) %collective-permute-start) | collective-permute-done | bytes 139296 | tf_op jit(solution)/shard_map/ppermute | solution.py:188
  9.3 4.0 %collective-permute-start.1 = (f32[34,2,512]{2,1,0:T(2,128)S(1)}, f32[34,2,512]{2,1,0:T(2,128)S(1)}, u32[]{:S(2)}, u32[]{:S(2)}) collective-permute-start(f32[34,2,512]{2,1,0:T(2,128)S(1)} %collective-permute-done.near.coef_near), channel_id=1, source_target_pairs={{0,2},{2,4},{4,6},{3,1},{5,3},{7,5},{8,10},{10,12},{12,14},{11,9},... | collective-permute-start | bytes 417800 | tf_op jit(solution)/shard_map/ppermute | solution.py:190
  13.4 3.5 %collective-permute-start.3 = (f32[32,2,512]{2,1,0:T(2,128)S(1)}, f32[32,2,512]{2,1,0:T(2,128)S(1)}, u32[]{:S(2)}, u32[]{:S(2)}) collective-permute-start(f32[32,2,512]{2,1,0:T(2,128)S(1)} %collective-permute-done.2.near), channel_id=1, source_target_pairs={{0,2},{2,4},{4,6},{3,1},{5,3},{7,5},{8,10},{10,12},{12,14},{11,9},... | collective-permute-start | bytes 393224 | tf_op jit(solution)/shard_map/ppermute | solution.py:190
  17.3 0.7 %copy-done.1 = f32[34,2,512]{2,1,0:T(2,128)} copy-done((f32[34,2,512]{2,1,0:T(2,128)}, f32[34,2,512]{2,1,0:T(2,128)S(1)}, u32[]{:S(2)}) %copy-start.1) | copy-done | bytes 139288
  17.9 2.4 %forecast.2.refs_0_ = f32[32,1024]{1,0:T(8,128)} custom-call(f32[64,2,512]{2,1,0:T(2,128)} %own.3, f32[2,512]{1,0:T(2,128)} %dif.3, f32[2,512]{1,0:T(2,128)} %wind.3, f32[34,2,512]{2,1,0:T(2,128)} %copy-done, f32[34,2,512]{2,1,0:T(2,128)} %copy-done.1, f32[34,2,512]{2,1,0:T(2,128)} %copy-done, f32[34,2,512]{2,1,0:T(2,128)} %copy-done.1), custom_call_target="tpu_custom_call" | custom-call | flops 2000000 | bytes 2000000 | tf_op jit(solution)/shard_map/forecast/pallas_call | solution.py:193
  20.3 1.5 %collective-permute-start.4 = (f32[32,1024]{1,0:T(8,128)}, f32[32,1024]{1,0:T(8,128)S(1)}, u32[]{:S(2)}, u32[]{:S(2)}) collective-permute-start(f32[32,1024]{1,0:T(8,128)} %forecast.2.refs_0_), channel_id=1, source_target_pairs={{0,16},{8,24},{16,0},{24,8},{1,17},{9,25},{17,1},{25,9},{2,18},{10... | collective-permute-start | bytes 393224 | tf_op jit(solution)/shard_map/ppermute | solution.py:203
  21.8 0.6 %copy-done.4 = f32[32,2,512]{2,1,0:T(2,128)} copy-done((f32[32,2,512]{2,1,0:T(2,128)}, f32[32,2,512]{2,1,0:T(2,128)S(1)}, u32[]{:S(2)}) %copy-start.4) | copy-done | bytes 131096
  22.4 2.4 %forecast.3.refs_1_ = f32[32,1024]{1,0:T(8,128)} custom-call(f32[64,2,512]{2,1,0:T(2,128)} %own.3, f32[2,512]{1,0:T(2,128)} %dif.3, f32[2,512]{1,0:T(2,128)} %wind.3, f32[32,2,512]{2,1,0:T(2,128)} %copy-done.2, f32[32,2,512]{2,1,0:T(2,128)} %copy-done.4, f32[34,2,512]{2,1,0:T(2,128)} %copy-done, f32[34,2,512]{2,1,0:T(2,128)} %copy-done.1), custom_call_target="tpu_custom_call" | custom-call | flops 2000000 | bytes 2000000 | tf_op jit(solution)/shard_map/forecast/pallas_call | solution.py:193
  24.8 0.5 %collective-permute-start.5 = (f32[32,1024]{1,0:T(8,128)}, f32[32,1024]{1,0:T(8,128)S(1)}, u32[]{:S(2)}, u32[]{:S(2)}) collective-permute-start(f32[32,1024]{1,0:T(8,128)} %forecast.3.refs_1_), channel_id=1, source_target_pairs={{0,16},{8,24},{16,0},{24,8},{1,17},{9,25},{17,1},{25,9},{2,18},{10... | collective-permute-start | bytes 393224 | tf_op jit(solution)/shard_map/ppermute | solution.py:203
  25.3 0.5 %collective-permute-start.7 = (f32[32,1024]{1,0:T(8,128)}, f32[32,1024]{1,0:T(8,128)S(1)}, u32[]{:S(2)}, u32[]{:S(2)}) collective-permute-start(f32[32,1024]{1,0:T(8,128)} %forecast.3.refs_1_), channel_id=1, source_target_pairs={{0,8},{8,0},{16,24},{24,16},{1,9},{9,1},{17,25},{25,17},{2,10},{10... | collective-permute-start | bytes 393224 | tf_op jit(solution)/shard_map/ppermute | solution.py:203
  25.8 0.9 %collective-permute-done.4.refs_2_ = f32[32,1024]{1,0:T(8,128)S(1)} collective-permute-done((f32[32,1024]{1,0:T(8,128)}, f32[32,1024]{1,0:T(8,128)S(1)}, u32[]{:S(2)}, u32[]{:S(2)}) %collective-permute-start.4) | collective-permute-done | bytes 131104 | tf_op jit(solution)/shard_map/ppermute | solution.py:203
  26.7 3.2 %collective-permute-done.5.refs_3_ = f32[32,1024]{1,0:T(8,128)S(1)} collective-permute-done((f32[32,1024]{1,0:T(8,128)}, f32[32,1024]{1,0:T(8,128)S(1)}, u32[]{:S(2)}, u32[]{:S(2)}) %collective-permute-start.5) | collective-permute-done | bytes 131104 | tf_op jit(solution)/shard_map/ppermute | solution.py:203
  30.0 1.3 %collective-permute-done.9.refs_7_ = f32[32,1024]{1,0:T(8,128)S(1)} collective-permute-done((f32[32,1024]{1,0:T(8,128)S(1)}, f32[32,1024]{1,0:T(8,128)S(1)}, u32[]{:S(2)}, u32[]{:S(2)}) %collective-permute-start.9) | collective-permute-done | bytes 131104 | tf_op jit(solution)/shard_map/ppermute | solution.py:203
  31.3 0.6 %copy-done.15 = f32[32,1024]{1,0:T(8,128)} copy-done((f32[32,1024]{1,0:T(8,128)}, f32[32,1024]{1,0:T(8,128)S(1)}, u32[]{:S(2)}) %copy-start.15) | copy-done | bytes 131096
  32.0 8.1 %gain.1 = (f32[128,256]{1,0:T(8,128)}, f32[64,256]{1,0:T(8,128)}, f32[64,256]{1,0:T(8,128)}) custom-call(s32[4,4]{1,0:T(4,128)} %bitcast.9, s32[4,512]{1,0:T(4,128)} %bitcast.8, f32[1,512]{1,0:T(1,128)} %bitcast.10, f32[1,512]{1,0:T(1,128)} %bitcast.11, f32[32,1024]{1,0:T(8,128)} %forecast.2.refs_0_, f32[32,1024]{1,0:T(8,128)} %forecast.3.refs_1_, ...), custom_call_target="tpu_custom_call" | custom-call | flops 5000000000 | bytes 4000000 | tf_op jit(solution)/shard_map/gain/pallas_call | solution.py:213
  40.1 0.5 %collective-permute-start.10 = (f32[128,256]{1,0:T(8,128)}, f32[128,256]{1,0:T(8,128)S(1)}, u32[]{:S(2)}, u32[]{:S(2)}) collective-permute-start(f32[128,256]{1,0:T(8,128)} %get-tuple-element.9), channel_id=1, source_target_pairs={{0,16},{8,24},{16,0},{24,8},{1,17},{9,25},{17,1},{25,9},{2,18},{10... | collective-permute-start | bytes 393224 | tf_op jit(solution)/shard_map/ppermute | solution.py:229
  40.7 5.2 %collective-permute-done.10.refs_1_ = f32[128,256]{1,0:T(8,128)S(1)} collective-permute-done((f32[128,256]{1,0:T(8,128)}, f32[128,256]{1,0:T(8,128)S(1)}, u32[]{:S(2)}, u32[]{:S(2)}) %collective-permute-start.10) | collective-permute-done | bytes 131104 | tf_op jit(solution)/shard_map/ppermute | solution.py:229
  45.9 0.5 %collective-permute-start.12 = (f32[64,256]{1,0:T(8,128)}, f32[64,256]{1,0:T(8,128)S(1)}, u32[]{:S(2)}, u32[]{:S(2)}) collective-permute-start(f32[64,256]{1,0:T(8,128)} %get-tuple-element.10), channel_id=1, source_target_pairs={{0,8},{8,0},{16,24},{24,16},{1,9},{9,1},{17,25},{25,17},{2,10},{10... | collective-permute-start | bytes 196616 | tf_op jit(solution)/shard_map/ppermute | solution.py:229
  46.4 1.1 %collective-permute-done.12.refs_3_ = f32[64,256]{1,0:T(8,128)S(1)} collective-permute-done((f32[64,256]{1,0:T(8,128)}, f32[64,256]{1,0:T(8,128)S(1)}, u32[]{:S(2)}, u32[]{:S(2)}) %collective-permute-start.12) | collective-permute-done | bytes 65568 | tf_op jit(solution)/shard_map/ppermute | solution.py:229
  47.5 0.6 %copy-done.7 = f32[64,256]{1,0:T(8,128)} copy-done((f32[64,256]{1,0:T(8,128)}, f32[64,256]{1,0:T(8,128)S(1)}, u32[]{:S(2)}) %copy-start.7) | copy-done | bytes 65560
  48.2 1.8 %place.1 = f32[64,2,512]{2,1,0:T(2,128)} custom-call(f32[64,256]{1,0:T(8,128)} %get-tuple-element.8.refs_0_, f32[128,256]{1,0:T(8,128)} %copy-done.3, f32[128,256]{1,0:T(8,128)} %copy-done.5, f32[64,256]{1,0:T(8,128)} %copy-done.7), custom_call_target="tpu_custom_call" | custom-call | flops 100000 | bytes 600000 | tf_op jit(solution)/shard_map/place/pallas_call | solution.py:240
  (40 shorter events, 0.7 us)
Async XLA Ops:
  0.0 1.0 %copy-start.9 = (f32[2,512]{1,0:T(2,128)S(1)}, f32[2,512]{1,0:T(2,128)}, u32[]{:S(2)}) copy-start(f32[2,512]{1,0:T(2,128)} %wind.3) | copy-start | bytes 12292
  1.0 0.7 %copy-start.8 = (f32[2,512]{1,0:T(2,128)S(1)}, f32[2,512]{1,0:T(2,128)}, u32[]{:S(2)}) copy-start(f32[2,512]{1,0:T(2,128)} %dif.3) | copy-start | bytes 12292
  1.8 7.6 %collective-permute-start = (f32[34,2,512]{2,1,0:T(2,128)S(1)}, f32[34,2,512]{2,1,0:T(2,128)S(1)}, u32[]{:S(2)}, u32[]{:S(2)}) collective-permute-start(f32[34,2,512]{2,1,0:T(2,128)S(1)} %pad_maximum_fusion), channel_id=1, source_target_pairs={{0,1},{1,0},{2,3},{3,2},{4,5},{5,4},{6,7},{7,6},{8,9},{9,8},{10,11... | collective-permute-start | bytes 417800 | tf_op jit(solution)/shard_map/ppermute | solution.py:188
  4.8 8.5 %collective-permute-start.2 = (f32[32,2,512]{2,1,0:T(2,128)S(1)}, f32[32,2,512]{2,1,0:T(2,128)S(1)}, u32[]{:S(2)}, u32[]{:S(2)}) collective-permute-start(f32[32,2,512]{2,1,0:T(2,128)S(1)} %get-tuple-element.11), channel_id=1, source_target_pairs={{0,1},{1,0},{2,3},{3,2},{4,5},{5,4},{6,7},{7,6},{8,9},{9,8},{10,11... | collective-permute-start | bytes 393224 | tf_op jit(solution)/shard_map/ppermute | solution.py:188
  9.3 7.9 %copy-start = (f32[34,2,512]{2,1,0:T(2,128)}, f32[34,2,512]{2,1,0:T(2,128)S(1)}, u32[]{:S(2)}) copy-start(f32[34,2,512]{2,1,0:T(2,128)S(1)} %collective-permute-done.near.coef_near) | copy-start | bytes 417796
  9.3 7.9 %collective-permute-start.1 = (f32[34,2,512]{2,1,0:T(2,128)S(1)}, f32[34,2,512]{2,1,0:T(2,128)S(1)}, u32[]{:S(2)}, u32[]{:S(2)}) collective-permute-start(f32[34,2,512]{2,1,0:T(2,128)S(1)} %collective-permute-done.near.coef_near), channel_id=1, source_target_pairs={{0,2},{2,4},{4,6},{3,1},{5,3},{7,5},{8,10},{10,12},{12,14},{11,9},... | collective-permute-start | bytes 417800 | tf_op jit(solution)/shard_map/ppermute | solution.py:190
  13.3 6.9 %copy-start.2 = (f32[32,2,512]{2,1,0:T(2,128)}, f32[32,2,512]{2,1,0:T(2,128)S(1)}, u32[]{:S(2)}) copy-start(f32[32,2,512]{2,1,0:T(2,128)S(1)} %collective-permute-done.2.near) | copy-start | bytes 393220
  13.4 8.4 %collective-permute-start.3 = (f32[32,2,512]{2,1,0:T(2,128)S(1)}, f32[32,2,512]{2,1,0:T(2,128)S(1)}, u32[]{:S(2)}, u32[]{:S(2)}) collective-permute-start(f32[32,2,512]{2,1,0:T(2,128)S(1)} %collective-permute-done.2.near), channel_id=1, source_target_pairs={{0,2},{2,4},{4,6},{3,1},{5,3},{7,5},{8,10},{10,12},{12,14},{11,9},... | collective-permute-start | bytes 393224 | tf_op jit(solution)/shard_map/ppermute | solution.py:190
  20.3 5.0 %copy-start.6 = (f32[32,1024]{1,0:T(8,128)S(1)}, f32[32,1024]{1,0:T(8,128)}, u32[]{:S(2)}) copy-start(f32[32,1024]{1,0:T(8,128)} %forecast.2.refs_0_) | copy-start | bytes 393220
  20.3 6.4 %collective-permute-start.4 = (f32[32,1024]{1,0:T(8,128)}, f32[32,1024]{1,0:T(8,128)S(1)}, u32[]{:S(2)}, u32[]{:S(2)}) collective-permute-start(f32[32,1024]{1,0:T(8,128)} %forecast.2.refs_0_), channel_id=1, source_target_pairs={{0,16},{8,24},{16,0},{24,8},{1,17},{9,25},{17,1},{25,9},{2,18},{10... | collective-permute-start | bytes 393224 | tf_op jit(solution)/shard_map/ppermute | solution.py:203
  24.8 5.2 %collective-permute-start.5 = (f32[32,1024]{1,0:T(8,128)}, f32[32,1024]{1,0:T(8,128)S(1)}, u32[]{:S(2)}, u32[]{:S(2)}) collective-permute-start(f32[32,1024]{1,0:T(8,128)} %forecast.3.refs_1_), channel_id=1, source_target_pairs={{0,16},{8,24},{16,0},{24,8},{1,17},{9,25},{17,1},{25,9},{2,18},{10... | collective-permute-start | bytes 393224 | tf_op jit(solution)/shard_map/ppermute | solution.py:203
  25.3 4.6 %collective-permute-start.6 = (f32[32,1024]{1,0:T(8,128)S(1)}, f32[32,1024]{1,0:T(8,128)S(1)}, u32[]{:S(2)}, u32[]{:S(2)}) collective-permute-start(f32[32,1024]{1,0:T(8,128)S(1)} %copy-done.6), channel_id=1, source_target_pairs={{0,8},{8,0},{16,24},{24,16},{1,9},{9,1},{17,25},{25,17},{2,10},{10... | collective-permute-start | bytes 393224 | tf_op jit(solution)/shard_map/ppermute | solution.py:203
  25.3 4.7 %collective-permute-start.7 = (f32[32,1024]{1,0:T(8,128)}, f32[32,1024]{1,0:T(8,128)S(1)}, u32[]{:S(2)}, u32[]{:S(2)}) collective-permute-start(f32[32,1024]{1,0:T(8,128)} %forecast.3.refs_1_), channel_id=1, source_target_pairs={{0,8},{8,0},{16,24},{24,16},{1,9},{9,1},{17,25},{25,17},{2,10},{10... | collective-permute-start | bytes 393224 | tf_op jit(solution)/shard_map/ppermute | solution.py:203
  26.7 4.6 %copy-start.10 = (f32[32,1024]{1,0:T(8,128)}, f32[32,1024]{1,0:T(8,128)S(1)}, u32[]{:S(2)}) copy-start(f32[32,1024]{1,0:T(8,128)S(1)} %collective-permute-done.4.refs_2_) | copy-start | bytes 393220
  26.7 3.3 %collective-permute-start.8 = (f32[32,1024]{1,0:T(8,128)S(1)}, f32[32,1024]{1,0:T(8,128)S(1)}, u32[]{:S(2)}, u32[]{:S(2)}) collective-permute-start(f32[32,1024]{1,0:T(8,128)S(1)} %collective-permute-done.4.refs_2_), channel_id=1, source_target_pairs={{0,8},{8,0},{16,24},{24,16},{1,9},{9,1},{17,25},{25,17},{2,10},{10... | collective-permute-start | bytes 393224 | tf_op jit(solution)/shard_map/ppermute | solution.py:203
  30.0 1.4 %copy-start.11 = (f32[32,1024]{1,0:T(8,128)}, f32[32,1024]{1,0:T(8,128)S(1)}, u32[]{:S(2)}) copy-start(f32[32,1024]{1,0:T(8,128)S(1)} %collective-permute-done.5.refs_3_) | copy-start | bytes 393220
  30.0 1.3 %collective-permute-start.9 = (f32[32,1024]{1,0:T(8,128)S(1)}, f32[32,1024]{1,0:T(8,128)S(1)}, u32[]{:S(2)}, u32[]{:S(2)}) collective-permute-start(f32[32,1024]{1,0:T(8,128)S(1)} %collective-permute-done.5.refs_3_), channel_id=1, source_target_pairs={{0,8},{8,0},{16,24},{24,16},{1,9},{9,1},{17,25},{25,17},{2,10},{10... | collective-permute-start | bytes 393224 | tf_op jit(solution)/shard_map/ppermute | solution.py:203
  30.0 1.3 %copy-start.12 = (f32[32,1024]{1,0:T(8,128)}, f32[32,1024]{1,0:T(8,128)S(1)}, u32[]{:S(2)}) copy-start(f32[32,1024]{1,0:T(8,128)S(1)} %collective-permute-done.6.refs_4_) | copy-start | bytes 393220
  30.0 1.3 %copy-start.13 = (f32[32,1024]{1,0:T(8,128)}, f32[32,1024]{1,0:T(8,128)S(1)}, u32[]{:S(2)}) copy-start(f32[32,1024]{1,0:T(8,128)S(1)} %collective-permute-done.7.refs_5_) | copy-start | bytes 393220
  30.0 1.3 %copy-start.14 = (f32[32,1024]{1,0:T(8,128)}, f32[32,1024]{1,0:T(8,128)S(1)}, u32[]{:S(2)}) copy-start(f32[32,1024]{1,0:T(8,128)S(1)} %collective-permute-done.8.refs_6_) | copy-start | bytes 393220
  40.1 5.8 %collective-permute-start.10 = (f32[128,256]{1,0:T(8,128)}, f32[128,256]{1,0:T(8,128)S(1)}, u32[]{:S(2)}, u32[]{:S(2)}) collective-permute-start(f32[128,256]{1,0:T(8,128)} %get-tuple-element.9), channel_id=1, source_target_pairs={{0,16},{8,24},{16,0},{24,8},{1,17},{9,25},{17,1},{25,9},{2,18},{10... | collective-permute-start | bytes 393224 | tf_op jit(solution)/shard_map/ppermute | solution.py:229
  45.9 1.6 %copy-start.3 = (f32[128,256]{1,0:T(8,128)}, f32[128,256]{1,0:T(8,128)S(1)}, u32[]{:S(2)}) copy-start(f32[128,256]{1,0:T(8,128)S(1)} %collective-permute-done.10.refs_1_) | copy-start | bytes 393220
  45.9 1.6 %collective-permute-start.11 = (f32[128,256]{1,0:T(8,128)S(1)}, f32[128,256]{1,0:T(8,128)S(1)}, u32[]{:S(2)}, u32[]{:S(2)}) collective-permute-start(f32[128,256]{1,0:T(8,128)S(1)} %collective-permute-done.10.refs_1_), channel_id=1, source_target_pairs={{0,8},{8,0},{16,24},{24,16},{1,9},{9,1},{17,25},{25,17},{2,10},{10... | collective-permute-start | bytes 393224 | tf_op jit(solution)/shard_map/ppermute | solution.py:229
  45.9 1.6 %collective-permute-start.12 = (f32[64,256]{1,0:T(8,128)}, f32[64,256]{1,0:T(8,128)S(1)}, u32[]{:S(2)}, u32[]{:S(2)}) collective-permute-start(f32[64,256]{1,0:T(8,128)} %get-tuple-element.10), channel_id=1, source_target_pairs={{0,8},{8,0},{16,24},{24,16},{1,9},{9,1},{17,25},{25,17},{2,10},{10... | collective-permute-start | bytes 196616 | tf_op jit(solution)/shard_map/ppermute | solution.py:229
  (5 other events, 3.3 us)

commit v2 on v1

--- a/solution.py
+++ b/solution.py
@@ -196,6 +196,7 @@
             in_specs=[VMEM] * 7,
             out_specs=VMEM,
             cost_estimate=pl.CostEstimate(flops=2000000, bytes_accessed=2000000, transcendentals=0),
+            compiler_params=pltpu.CompilerParams(vmem_limit_bytes=8 << 20),
             name="forecast",
         )(ensemble, diffusivity, north_wind, near[k], far[k], near[0], far[0])
         held = [band]
@@ -217,6 +218,7 @@
         out_specs=[VMEM] * len(shapes),
         scratch_shapes=[pltpu.VMEM((total, observations), F32), pltpu.VMEM((total, own_cells), F32)],
         cost_estimate=pl.CostEstimate(flops=5000000000, bytes_accessed=4000000, transcendentals=0),
+        compiler_params=pltpu.CompilerParams(vmem_limit_bytes=24 << 20),
         name="gain",
     )(observed_blocks[0], eastern_average_flags[0], observed_values[0], observed_error[0], *flat)
     carried = [(outs[-1], [(0, 0)])]
@@ -243,6 +245,7 @@
         in_specs=[VMEM] * len(carried),
         out_specs=VMEM,
         cost_estimate=pl.CostEstimate(flops=100000, bytes_accessed=600000, transcendentals=0),
+        compiler_params=pltpu.CompilerParams(vmem_limit_bytes=8 << 20),
         name="place",
     )(*[a for a, _ in carried])
 

time: 50.3 us -> 41.1 us (0.82)
  Pallas kernels: 14.7 us -> 8.6 us
  local copies, waits for them, and re-layouts: 4.32 us -> 1.71 us
  waiting for transfers between devices: 16.6 us -> 14.3 us
  starting transfers between devices: 14.2 us -> 16.2 us
    pallas_call x2, Pallas kernels: 4.72 us -> 1.09 us  [body(): pl.pallas_call(functools.partial(forecast_kernel, k * count, count, 2 if...]
    unnamed x32 -> x14, local copies, waits for them, and re-layouts: 3.32 us -> 0.7 us
    pallas_call x1, Pallas kernels: 8.15 us -> 6.69 us  [body(): pl.pallas_call(functools.partial(gain_kernel, mems, pieces, tops, longitu...]
    ppermute x3, waiting for transfers between devices: 6.34 us -> 5.06 us  [body(): lax.ppermute(a, 'mem', xor_pairs(mems, bit))]
    ppermute x6, waiting for transfers between devices: 5.42 us -> 4.36 us  [body(): held = held + [lax.ppermute(a, 'mem', xor_pairs(mems, bit)) for a in held]]
    ppermute x6, starting transfers between devices: 2.54 us -> 3.57 us  [body(): held = held + [lax.ppermute(a, 'mem', xor_pairs(mems, bit)) for a in held]]
    pallas_call x1, Pallas kernels: 1.82 us -> 0.82 us  [body(): pl.pallas_call(functools.partial(place_kernel, masks, where, longitudes),...]
    ppermute x3, starting transfers between devices: 1.05 us -> 2 us  [body(): lax.ppermute(a, 'mem', xor_pairs(mems, bit))]
  transfers between devices with their start and end apart: 13 -> 13, of which waited for: 7 -> 7; matrix products, arithmetic and copies ran while one was open for 0% -> 0% of each run, Pallas kernels for 9% -> 3%
where the time goes in v2:
time: 41.1 us; the launch traced here: 40.9 us
  starting transfers between devices  16.2 us (39%)
  waiting for transfers between devices  14.3 us (35%)
  Pallas kernels  8.6 us (21%)
  local copies, waits for them, and re-layouts  1.71 us (4%)
    ppermute x2, starting transfers between devices, body(): far.append(lax.ppermute(near[k], 'lat', far_pairs))  7.46 us
    pallas_call x1, Pallas kernels, body(): pl.pallas_call(functools.partial(gain_kernel, mems, pieces, tops, longitu...  6.69 us
    ppermute x3, waiting for transfers between devices, body(): lax.ppermute(a, 'mem', xor_pairs(mems, bit))  5.06 us
    ppermute x2, waiting for transfers between devices, body(): near.append(lax.ppermute(own, 'lat', near_pairs))  4.45 us
    ppermute x6, waiting for transfers between devices, body(): held = held + [lax.ppermute(a, 'mem', xor_pairs(mems, bit)) for a in held]  4.36 us
    ppermute x6, starting transfers between devices, body(): held = held + [lax.ppermute(a, 'mem', xor_pairs(mems, bit)) for a in held]  3.57 us
    ppermute x2, starting transfers between devices, body(): near.append(lax.ppermute(own, 'lat', near_pairs))  3.14 us
    ppermute x3, starting transfers between devices, body(): lax.ppermute(a, 'mem', xor_pairs(mems, bit))  2 us
  transfers between devices with their start and end apart: 13, of which 7 were waited for; matrix products, arithmetic and copies ran while one was open for 0% of the time, Pallas kernels for 3%

profile of v2, /device:TPU:0, one launch (start us, length us, event | category | flops | bytes accessed | tf_op | source)
XLA Modules:
  0.0 40.9 jit_solution(1939823142420193347)
XLA Ops:
  0.0 1.0 %fusion = (f32[32,2,512]{2,1,0:T(2,128)S(1)}, f32[32,2,512]{2,1,0:T(2,128)S(1)}) fusion(f32[64,2,512]{2,1,0:T(2,128)} %own.3), kind=kLoop, calls=%fused_computation.1 | loop fusion | bytes 524288 | tf_op jit(solution)/shard_map/slice | solution.py:185
  1.1 0.1 pad_maximum_fusion
  1.1 3.1 %collective-permute-start = (f32[34,2,512]{2,1,0:T(2,128)S(1)}, f32[34,2,512]{2,1,0:T(2,128)S(1)}, u32[]{:S(2)}, u32[]{:S(2)}) collective-permute-start(f32[34,2,512]{2,1,0:T(2,128)S(1)} %pad_maximum_fusion), channel_id=1, source_target_pairs={{0,1},{1,0},{2,3},{3,2},{4,5},{5,4},{6,7},{7,6},{8,9},{9,8},{10,11... | collective-permute-start | bytes 417800 | tf_op jit(solution)/shard_map/ppermute | solution.py:188
  4.2 0.1 collective-permute-start.2
  4.3 4.4 %collective-permute-done.near.coef_near = f32[34,2,512]{2,1,0:T(2,128)S(1)} collective-permute-done((f32[34,2,512]{2,1,0:T(2,128)S(1)}, f32[34,2,512]{2,1,0:T(2,128)S(1)}, u32[]{:S(2)}, u32[]{:S(2)}) %collective-permute-start) | collective-permute-done | bytes 139296 | tf_op jit(solution)/shard_map/ppermute | solution.py:188
  8.7 4.0 %collective-permute-start.1 = (f32[34,2,512]{2,1,0:T(2,128)S(1)}, f32[34,2,512]{2,1,0:T(2,128)S(1)}, u32[]{:S(2)}, u32[]{:S(2)}) collective-permute-start(f32[34,2,512]{2,1,0:T(2,128)S(1)} %collective-permute-done.near.coef_near), channel_id=1, source_target_pairs={{0,2},{2,4},{4,6},{3,1},{5,3},{7,5},{8,10},{10,12},{12,14},{11,9},... | collective-permute-start | bytes 417800 | tf_op jit(solution)/shard_map/ppermute | solution.py:190
  12.7 3.5 %collective-permute-start.3 = (f32[32,2,512]{2,1,0:T(2,128)S(1)}, f32[32,2,512]{2,1,0:T(2,128)S(1)}, u32[]{:S(2)}, u32[]{:S(2)}) collective-permute-start(f32[32,2,512]{2,1,0:T(2,128)S(1)} %collective-permute-done.2.near), channel_id=1, source_target_pairs={{0,2},{2,4},{4,6},{3,1},{5,3},{7,5},{8,10},{10,12},{12,14},{11,9},... | collective-permute-start | bytes 393224 | tf_op jit(solution)/shard_map/ppermute | solution.py:190
  16.2 0.4 %collective-permute-done.1.far.coef_far = f32[34,2,512]{2,1,0:T(2,128)S(1)} collective-permute-done((f32[34,2,512]{2,1,0:T(2,128)S(1)}, f32[34,2,512]{2,1,0:T(2,128)S(1)}, u32[]{:S(2)}, u32[]{:S(2)}) %collective-permute-start.1) | collective-permute-done | bytes 139296 | tf_op jit(solution)/shard_map/ppermute | solution.py:190
  16.6 0.5 %forecast.2.refs_0_ = f32[32,1024]{1,0:T(8,128)S(1)} custom-call(f32[64,2,512]{2,1,0:T(2,128)S(1)} %copy-done, f32[2,512]{1,0:T(2,128)S(1)} %copy-done.1, f32[2,512]{1,0:T(2,128)S(1)} %copy-done.2, f32[34,2,512]{2,1,0:T(2,128)S(1)} %collective-permute-done.near.coef_near, f32[34,2,512]{2,1,0:T(2,128)S(1)} %collective-permute-done.1.far.coef_far, ...), custom_call_target="tpu_custom_call" | custom-call | flops 2000000 | bytes 2000000 | tf_op jit(solution)/shard_map/forecast/pallas_call | solution.py:193
  17.2 0.0 copy-start.3
  17.2 1.6 %collective-permute-start.4 = (f32[32,1024]{1,0:T(8,128)S(1)}, f32[32,1024]{1,0:T(8,128)S(1)}, u32[]{:S(2)}, u32[]{:S(2)}) collective-permute-start(f32[32,1024]{1,0:T(8,128)S(1)} %forecast.2.refs_0_), channel_id=1, source_target_pairs={{0,16},{8,24},{16,0},{24,8},{1,17},{9,25},{17,1},{25,9},{2,18},{10... | collective-permute-start | bytes 393224 | tf_op jit(solution)/shard_map/ppermute | solution.py:204
  18.8 0.5 %forecast.3.refs_1_ = f32[32,1024]{1,0:T(8,128)S(1)} custom-call(f32[64,2,512]{2,1,0:T(2,128)S(1)} %copy-done, f32[2,512]{1,0:T(2,128)S(1)} %copy-done.1, f32[2,512]{1,0:T(2,128)S(1)} %copy-done.2, f32[32,2,512]{2,1,0:T(2,128)S(1)} %collective-permute-done.2.near, f32[32,2,512]{2,1,0:T(2,128)S(1)} %collective-permute-done.3.far, ...), custom_call_target="tpu_custom_call" | custom-call | flops 2000000 | bytes 2000000 | tf_op jit(solution)/shard_map/forecast/pallas_call | solution.py:193
  19.3 1.5 %collective-permute-start.5 = (f32[32,1024]{1,0:T(8,128)S(1)}, f32[32,1024]{1,0:T(8,128)S(1)}, u32[]{:S(2)}, u32[]{:S(2)}) collective-permute-start(f32[32,1024]{1,0:T(8,128)S(1)} %forecast.3.refs_1_), channel_id=1, source_target_pairs={{0,16},{8,24},{16,0},{24,8},{1,17},{9,25},{17,1},{25,9},{2,18},{10... | collective-permute-start | bytes 393224 | tf_op jit(solution)/shard_map/ppermute | solution.py:204
  20.8 0.5 %collective-permute-start.7 = (f32[32,1024]{1,0:T(8,128)S(1)}, f32[32,1024]{1,0:T(8,128)S(1)}, u32[]{:S(2)}, u32[]{:S(2)}) collective-permute-start(f32[32,1024]{1,0:T(8,128)S(1)} %forecast.3.refs_1_), channel_id=1, source_target_pairs={{0,8},{8,0},{16,24},{24,16},{1,9},{9,1},{17,25},{25,17},{2,10},{10... | collective-permute-start | bytes 393224 | tf_op jit(solution)/shard_map/ppermute | solution.py:204
  21.3 1.5 %collective-permute-done.4.refs_2_ = f32[32,1024]{1,0:T(8,128)S(1)} collective-permute-done((f32[32,1024]{1,0:T(8,128)S(1)}, f32[32,1024]{1,0:T(8,128)S(1)}, u32[]{:S(2)}, u32[]{:S(2)}) %collective-permute-start.4) | collective-permute-done | bytes 131104 | tf_op jit(solution)/shard_map/ppermute | solution.py:204
  22.8 1.5 %collective-permute-done.5.refs_3_ = f32[32,1024]{1,0:T(8,128)S(1)} collective-permute-done((f32[32,1024]{1,0:T(8,128)S(1)}, f32[32,1024]{1,0:T(8,128)S(1)}, u32[]{:S(2)}, u32[]{:S(2)}) %collective-permute-start.5) | collective-permute-done | bytes 131104 | tf_op jit(solution)/shard_map/ppermute | solution.py:204
  24.4 1.3 %collective-permute-done.9.refs_7_ = f32[32,1024]{1,0:T(8,128)S(1)} collective-permute-done((f32[32,1024]{1,0:T(8,128)S(1)}, f32[32,1024]{1,0:T(8,128)S(1)}, u32[]{:S(2)}, u32[]{:S(2)}) %collective-permute-start.9) | collective-permute-done | bytes 131104 | tf_op jit(solution)/shard_map/ppermute | solution.py:204
  25.7 0.7 %copy-done.4 = s32[1,4,4]{2,1,0:T(4,128)S(1)} copy-done((s32[1,4,4]{2,1,0:T(4,128)S(1)}, s32[1,4,4]{2,1,0:T(4,128)}, u32[]{:S(2)}) %copy-start.4) | copy-done | bytes 88
  26.4 6.7 %gain.1 = (f32[128,256]{1,0:T(8,128)S(1)}, f32[64,256]{1,0:T(8,128)S(1)}, f32[64,256]{1,0:T(8,128)S(1)}) custom-call(s32[4,4]{1,0:T(4,128)S(1)} %bitcast.9, s32[4,512]{1,0:T(4,128)S(1)} %bitcast.8, f32[1,512]{1,0:T(1,128)S(1)} %bitcast.10, f32[1,512]{1,0:T(1,128)S(1)} %bitcast.11, f32[32,1024]{1,0:T(8,128)S(1)} %forecast.2.refs_0_, ...), custom_call_target="tpu_custom_call" | custom-call | flops 5000000000 | bytes 4000000 | tf_op jit(solution)/shard_map/gain/pallas_call | solution.py:214
  33.1 1.5 %collective-permute-start.10 = (f32[128,256]{1,0:T(8,128)S(1)}, f32[128,256]{1,0:T(8,128)S(1)}, u32[]{:S(2)}, u32[]{:S(2)}) collective-permute-start(f32[128,256]{1,0:T(8,128)S(1)} %get-tuple-element.9), channel_id=1, source_target_pairs={{0,16},{8,24},{16,0},{24,8},{1,17},{9,25},{17,1},{25,9},{2,18},{10... | collective-permute-start | bytes 393224 | tf_op jit(solution)/shard_map/ppermute | solution.py:231
  34.6 4.1 %collective-permute-done.10.refs_1_ = f32[128,256]{1,0:T(8,128)S(1)} collective-permute-done((f32[128,256]{1,0:T(8,128)S(1)}, f32[128,256]{1,0:T(8,128)S(1)}, u32[]{:S(2)}, u32[]{:S(2)}) %collective-permute-start.10) | collective-permute-done | bytes 131104 | tf_op jit(solution)/shard_map/ppermute | solution.py:231
  38.7 0.5 %collective-permute-start.12 = (f32[64,256]{1,0:T(8,128)S(1)}, f32[64,256]{1,0:T(8,128)S(1)}, u32[]{:S(2)}, u32[]{:S(2)}) collective-permute-start(f32[64,256]{1,0:T(8,128)S(1)} %get-tuple-element.10), channel_id=1, source_target_pairs={{0,8},{8,0},{16,24},{24,16},{1,9},{9,1},{17,25},{25,17},{2,10},{10... | collective-permute-start | bytes 196616 | tf_op jit(solution)/shard_map/ppermute | solution.py:231
  39.2 0.9 %collective-permute-done.12.refs_3_ = f32[64,256]{1,0:T(8,128)S(1)} collective-permute-done((f32[64,256]{1,0:T(8,128)S(1)}, f32[64,256]{1,0:T(8,128)S(1)}, u32[]{:S(2)}, u32[]{:S(2)}) %collective-permute-start.12) | collective-permute-done | bytes 65568 | tf_op jit(solution)/shard_map/ppermute | solution.py:231
  40.1 0.8 %place.1 = f32[64,2,512]{2,1,0:T(2,128)} custom-call(f32[64,256]{1,0:T(8,128)S(1)} %get-tuple-element.8.refs_0_, f32[128,256]{1,0:T(8,128)S(1)} %collective-permute-done.10.refs_1_, f32[128,256]{1,0:T(8,128)S(1)} %collective-permute-done.11.refs_2_, f32[64,256]{1,0:T(8,128)S(1)} %collective-permute-done.12.refs_3_), custom_call_target="tpu_custom_call" | custom-call | flops 100000 | bytes 600000 | tf_op jit(solution)/shard_map/place/pallas_call | solution.py:242
  (22 shorter events, 0.1 us)
Async XLA Ops:
  0.0 1.0 %copy-start.1 = (f32[2,512]{1,0:T(2,128)S(1)}, f32[2,512]{1,0:T(2,128)}, u32[]{:S(2)}) copy-start(f32[2,512]{1,0:T(2,128)} %dif.3) | copy-start | bytes 12292
  0.0 1.0 %copy-start.2 = (f32[2,512]{1,0:T(2,128)S(1)}, f32[2,512]{1,0:T(2,128)}, u32[]{:S(2)}) copy-start(f32[2,512]{1,0:T(2,128)} %wind.3) | copy-start | bytes 12292
  1.0 15.6 %copy-start = (f32[64,2,512]{2,1,0:T(2,128)S(1)}, f32[64,2,512]{2,1,0:T(2,128)}, u32[]{:S(2)}) copy-start(f32[64,2,512]{2,1,0:T(2,128)} %own.3) | copy-start | bytes 786436
  1.1 7.6 %collective-permute-start = (f32[34,2,512]{2,1,0:T(2,128)S(1)}, f32[34,2,512]{2,1,0:T(2,128)S(1)}, u32[]{:S(2)}, u32[]{:S(2)}) collective-permute-start(f32[34,2,512]{2,1,0:T(2,128)S(1)} %pad_maximum_fusion), channel_id=1, source_target_pairs={{0,1},{1,0},{2,3},{3,2},{4,5},{5,4},{6,7},{7,6},{8,9},{9,8},{10,11... | collective-permute-start | bytes 417800 | tf_op jit(solution)/shard_map/ppermute | solution.py:188
  4.2 8.5 %collective-permute-start.2 = (f32[32,2,512]{2,1,0:T(2,128)S(1)}, f32[32,2,512]{2,1,0:T(2,128)S(1)}, u32[]{:S(2)}, u32[]{:S(2)}) collective-permute-start(f32[32,2,512]{2,1,0:T(2,128)S(1)} %get-tuple-element.11), channel_id=1, source_target_pairs={{0,1},{1,0},{2,3},{3,2},{4,5},{5,4},{6,7},{7,6},{8,9},{9,8},{10,11... | collective-permute-start | bytes 393224 | tf_op jit(solution)/shard_map/ppermute | solution.py:188
  8.7 7.9 %collective-permute-start.1 = (f32[34,2,512]{2,1,0:T(2,128)S(1)}, f32[34,2,512]{2,1,0:T(2,128)S(1)}, u32[]{:S(2)}, u32[]{:S(2)}) collective-permute-start(f32[34,2,512]{2,1,0:T(2,128)S(1)} %collective-permute-done.near.coef_near), channel_id=1, source_target_pairs={{0,2},{2,4},{4,6},{3,1},{5,3},{7,5},{8,10},{10,12},{12,14},{11,9},... | collective-permute-start | bytes 417800 | tf_op jit(solution)/shard_map/ppermute | solution.py:190
  12.7 6.0 %collective-permute-start.3 = (f32[32,2,512]{2,1,0:T(2,128)S(1)}, f32[32,2,512]{2,1,0:T(2,128)S(1)}, u32[]{:S(2)}, u32[]{:S(2)}) collective-permute-start(f32[32,2,512]{2,1,0:T(2,128)S(1)} %collective-permute-done.2.near), channel_id=1, source_target_pairs={{0,2},{2,4},{4,6},{3,1},{5,3},{7,5},{8,10},{10,12},{12,14},{11,9},... | collective-permute-start | bytes 393224 | tf_op jit(solution)/shard_map/ppermute | solution.py:190
  17.2 8.5 %copy-start.3 = (s32[1,4,512]{2,1,0:T(4,128)S(1)}, s32[1,4,512]{2,1,0:T(4,128)}, u32[]{:S(2)}) copy-start(s32[1,4,512]{2,1,0:T(4,128)} %param.11) | copy-start | bytes 24580
  17.2 5.6 %collective-permute-start.4 = (f32[32,1024]{1,0:T(8,128)S(1)}, f32[32,1024]{1,0:T(8,128)S(1)}, u32[]{:S(2)}, u32[]{:S(2)}) collective-permute-start(f32[32,1024]{1,0:T(8,128)S(1)} %forecast.2.refs_0_), channel_id=1, source_target_pairs={{0,16},{8,24},{16,0},{24,8},{1,17},{9,25},{17,1},{25,9},{2,18},{10... | collective-permute-start | bytes 393224 | tf_op jit(solution)/shard_map/ppermute | solution.py:204
  18.8 6.9 %copy-start.5 = (f32[1,1,512]{2,1,0:T(1,128)S(1)}, f32[1,1,512]{2,1,0:T(1,128)}, u32[]{:S(2)}) copy-start(f32[1,1,512]{2,1,0:T(1,128)} %param.12) | copy-start | bytes 6148
  18.8 6.9 %copy-start.6 = (f32[1,1,512]{2,1,0:T(1,128)S(1)}, f32[1,1,512]{2,1,0:T(1,128)}, u32[]{:S(2)}) copy-start(f32[1,1,512]{2,1,0:T(1,128)} %param.13) | copy-start | bytes 6148
  19.3 5.0 %collective-permute-start.5 = (f32[32,1024]{1,0:T(8,128)S(1)}, f32[32,1024]{1,0:T(8,128)S(1)}, u32[]{:S(2)}, u32[]{:S(2)}) collective-permute-start(f32[32,1024]{1,0:T(8,128)S(1)} %forecast.3.refs_1_), channel_id=1, source_target_pairs={{0,16},{8,24},{16,0},{24,8},{1,17},{9,25},{17,1},{25,9},{2,18},{10... | collective-permute-start | bytes 393224 | tf_op jit(solution)/shard_map/ppermute | solution.py:204
  20.8 3.5 %collective-permute-start.6 = (f32[32,1024]{1,0:T(8,128)S(1)}, f32[32,1024]{1,0:T(8,128)S(1)}, u32[]{:S(2)}, u32[]{:S(2)}) collective-permute-start(f32[32,1024]{1,0:T(8,128)S(1)} %forecast.2.refs_0_), channel_id=1, source_target_pairs={{0,8},{8,0},{16,24},{24,16},{1,9},{9,1},{17,25},{25,17},{2,10},{10... | collective-permute-start | bytes 393224 | tf_op jit(solution)/shard_map/ppermute | solution.py:204
  20.8 3.5 %collective-permute-start.7 = (f32[32,1024]{1,0:T(8,128)S(1)}, f32[32,1024]{1,0:T(8,128)S(1)}, u32[]{:S(2)}, u32[]{:S(2)}) collective-permute-start(f32[32,1024]{1,0:T(8,128)S(1)} %forecast.3.refs_1_), channel_id=1, source_target_pairs={{0,8},{8,0},{16,24},{24,16},{1,9},{9,1},{17,25},{25,17},{2,10},{10... | collective-permute-start | bytes 393224 | tf_op jit(solution)/shard_map/ppermute | solution.py:204
  22.8 1.6 %collective-permute-start.8 = (f32[32,1024]{1,0:T(8,128)S(1)}, f32[32,1024]{1,0:T(8,128)S(1)}, u32[]{:S(2)}, u32[]{:S(2)}) collective-permute-start(f32[32,1024]{1,0:T(8,128)S(1)} %collective-permute-done.4.refs_2_), channel_id=1, source_target_pairs={{0,8},{8,0},{16,24},{24,16},{1,9},{9,1},{17,25},{25,17},{2,10},{10... | collective-permute-start | bytes 393224 | tf_op jit(solution)/shard_map/ppermute | solution.py:204
  24.3 1.3 %collective-permute-start.9 = (f32[32,1024]{1,0:T(8,128)S(1)}, f32[32,1024]{1,0:T(8,128)S(1)}, u32[]{:S(2)}, u32[]{:S(2)}) collective-permute-start(f32[32,1024]{1,0:T(8,128)S(1)} %collective-permute-done.5.refs_3_), channel_id=1, source_target_pairs={{0,8},{8,0},{16,24},{24,16},{1,9},{9,1},{17,25},{25,17},{2,10},{10... | collective-permute-start | bytes 393224 | tf_op jit(solution)/shard_map/ppermute | solution.py:204
  25.7 0.7 %copy-start.4 = (s32[1,4,4]{2,1,0:T(4,128)S(1)}, s32[1,4,4]{2,1,0:T(4,128)}, u32[]{:S(2)}) copy-start(s32[1,4,4]{2,1,0:T(4,128)} %param.10) | copy-start | bytes 196
  33.1 5.6 %collective-permute-start.10 = (f32[128,256]{1,0:T(8,128)S(1)}, f32[128,256]{1,0:T(8,128)S(1)}, u32[]{:S(2)}, u32[]{:S(2)}) collective-permute-start(f32[128,256]{1,0:T(8,128)S(1)} %get-tuple-element.9), channel_id=1, source_target_pairs={{0,16},{8,24},{16,0},{24,8},{1,17},{9,25},{17,1},{25,9},{2,18},{10... | collective-permute-start | bytes 393224 | tf_op jit(solution)/shard_map/ppermute | solution.py:231
  38.7 1.4 %collective-permute-start.11 = (f32[128,256]{1,0:T(8,128)S(1)}, f32[128,256]{1,0:T(8,128)S(1)}, u32[]{:S(2)}, u32[]{:S(2)}) collective-permute-start(f32[128,256]{1,0:T(8,128)S(1)} %collective-permute-done.10.refs_1_), channel_id=1, source_target_pairs={{0,8},{8,0},{16,24},{24,16},{1,9},{9,1},{17,25},{25,17},{2,10},{10... | collective-permute-start | bytes 393224 | tf_op jit(solution)/shard_map/ppermute | solution.py:231
  38.7 1.4 %collective-permute-start.12 = (f32[64,256]{1,0:T(8,128)S(1)}, f32[64,256]{1,0:T(8,128)S(1)}, u32[]{:S(2)}, u32[]{:S(2)}) collective-permute-start(f32[64,256]{1,0:T(8,128)S(1)} %get-tuple-element.10), channel_id=1, source_target_pairs={{0,8},{8,0},{16,24},{24,16},{1,9},{9,1},{17,25},{25,17},{2,10},{10... | collective-permute-start | bytes 196616 | tf_op jit(solution)/shard_map/ppermute | solution.py:231

commit v3 on v2

--- a/solution.py
+++ b/solution.py
@@ -17,6 +17,13 @@
 
 def xor_pairs(count, bit):
     return [(i, i ^ bit) for i in range(count)]
+
+
+def piece_counts(local):
+    unit = 8 if local % 8 == 0 else 1
+    whole = local // unit
+    first = (whole + 1) // 2
+    return [n * unit for n in (first, whole - first) if n]
 
 
 def step(rows, diffusivity, north_wind):
@@ -35,8 +42,11 @@
     return out
 
 
-def forecast_kernel(first, count, lead, own, dif, wind, near, far, coef_near, coef_far, out):
-    even = lax.rem(lax.axis_index("lat"), 2) == 0
+def forecast_kernel(lats, first, count, lead, own, dif, wind, near, far, coef_near, coef_far, *tables_and_out):
+    out = tables_and_out[-1]
+    place = lax.axis_index("lat")
+    even = lax.rem(place, 2) == 0
+    inner = (place > 0) & (place < lats - 1)
     rows, longitudes = own.shape[1], own.shape[2]
     edge = near.shape[1]
 
@@ -46,13 +56,16 @@
     def members(ref, r):
         return ref[lead : lead + count, r, :]
 
-    low = [pick(members(far, r), members(near, r)) for r in (edge - 2, edge - 1)]
-    high = [pick(members(near, r), members(far, r)) for r in (0, 1)]
+    def beyond(x):
+        return jnp.where(inner, x, 0.0)
+
+    low = [pick(beyond(members(far, r)), members(near, r)) for r in (edge - 2, edge - 1)]
+    high = [pick(members(near, r), beyond(members(far, r))) for r in (0, 1)]
     here = [own[first : first + count, r, :] for r in range(rows)]
 
     def coefficient(which, ref):
-        before = pick(coef_far[which : which + 1, edge - 1, :], coef_near[which : which + 1, edge - 1, :])
-        after = pick(coef_near[which : which + 1, 0, :], coef_far[which : which + 1, 0, :])
+        before = pick(beyond(coef_far[which : which + 1, edge - 1, :]), coef_near[which : which + 1, edge - 1, :])
+        after = pick(coef_near[which : which + 1, 0, :], beyond(coef_far[which : which + 1, 0, :]))
         return [before] + [ref[r : r + 1, :] for r in range(rows)] + [after]
 
     d, w = coefficient(0, dif), coefficient(1, wind)
@@ -72,7 +85,7 @@
     return mul(a[0], b[0]) + (mul(a[0], b[1]) + mul(a[1], b[0]))
 
 
-def gain_kernel(groups, pieces, tops, longitudes, blocks, flags, values, errors, *refs):
+def gain_kernel(groups, pieces, longitudes, blocks, flags, values, errors, *refs):
     parts = refs[: groups * pieces]
     outs = refs[groups * pieces : -2]
     seen, cells = refs[-2:]
@@ -134,17 +147,15 @@
     shift = state - jnp.sum(state, axis=0, keepdims=True) * (1.0 / total)
     analysed = state + dot3(split(mix), split(shift))
     size = total // groups
-    for out, wanted in zip(outs, tops):
-        for at, j in enumerate(wanted):
-            out[at * size : (at + 1) * size, :] = analysed[j * size : (j + 1) * size, :]
-
-
-def place_kernel(masks, where, longitudes, *refs):
+    for j, out in enumerate(outs):
+        out[...] = analysed[j * size : (j + 1) * size, :]
+
+
+def place_kernel(masks, longitudes, *refs):
     sources, out = refs[:-1], refs[-1]
     here = lax.axis_index("mem")
-    local = out.shape[0]
     width = sources[0].shape[1]
-    found = [sources[where[m][0]][where[m][1] * local : (where[m][1] + 1) * local, :] for m in masks]
+    found = [source[...] for source in sources]
     for patch in range(len(masks)):
         value = found[0]
         for m, candidate in zip(masks[1:], found[1:]):
@@ -170,35 +181,38 @@
     total = local * mems
     near_pairs = xor_pairs(lats, 1)
     far_pairs = [(i, i + 2) for i in range(0, lats - 2, 2)] + [(i, i - 2) for i in range(3, lats, 2)]
+    far_pairs += [(lats - 2, lats - 1), (1, 0)]
 
     def edges(block):
         if block.shape[1] == 2:
             return block
         return jnp.concatenate([block[:, :2], block[:, -2:]], axis=1)
 
-    pieces = 2
-    count = local // pieces
+    counts = piece_counts(local)
+    pieces = len(counts)
+    firsts = [sum(counts[:k]) for k in range(pieces)]
     bits = [1 << k for k in reversed(range(mems.bit_length() - 1))]
     coefficients = edges(jnp.stack([diffusivity, north_wind]))
     near, far = [], []
     for k in range(pieces):
-        own = edges(ensemble[k * count : (k + 1) * count])
+        own = edges(ensemble[firsts[k] : firsts[k] + counts[k]])
         if k == 0:
             own = jnp.concatenate([coefficients, own], axis=0)
         near.append(lax.ppermute(own, "lat", near_pairs))
     for k in range(pieces):
         far.append(lax.ppermute(near[k], "lat", far_pairs))
+    tables = observed_blocks[0], eastern_average_flags[0], observed_values[0], observed_error[0]
     parts = [[] for _ in range(pieces)]
     for k in range(pieces):
         band = pl.pallas_call(
-            functools.partial(forecast_kernel, k * count, count, 2 if k == 0 else 0),
-            out_shape=jax.ShapeDtypeStruct((count, cell_count), F32),
-            in_specs=[VMEM] * 7,
+            functools.partial(forecast_kernel, lats, firsts[k], counts[k], 2 if k == 0 else 0),
+            out_shape=jax.ShapeDtypeStruct((counts[k], cell_count), F32),
+            in_specs=[VMEM] * (7 + len(tables)),
             out_specs=VMEM,
             cost_estimate=pl.CostEstimate(flops=2000000, bytes_accessed=2000000, transcendentals=0),
             compiler_params=pltpu.CompilerParams(vmem_limit_bytes=8 << 20),
             name="forecast",
-        )(ensemble, diffusivity, north_wind, near[k], far[k], near[0], far[0])
+        )(ensemble, diffusivity, north_wind, near[k], far[k], near[0], far[0], *tables)
         held = [band]
         for bit in bits:
             held = held + [lax.ppermute(a, "mem", xor_pairs(mems, bit)) for a in held]
@@ -207,12 +221,10 @@
     for bit in bits:
         masks = masks + [m ^ bit for m in masks]
 
-    tops = [[j for j, m in enumerate(masks) if (m & bit) and m < 2 * bit] for bit in bits]
-    tops.append([0])
     flat = [parts[k][j] for j in range(mems) for k in range(pieces)]
-    shapes = [jax.ShapeDtypeStruct((len(t) * local, own_cells), F32) for t in tops]
+    shapes = [jax.ShapeDtypeStruct((local, own_cells), F32) for _ in masks]
     outs = pl.pallas_call(
-        functools.partial(gain_kernel, mems, pieces, tops, longitudes),
+        functools.partial(gain_kernel, mems, pieces, longitudes),
         out_shape=shapes,
         in_specs=[SMEM] + [VMEM] * (3 + len(flat)),
         out_specs=[VMEM] * len(shapes),
@@ -220,34 +232,20 @@
         cost_estimate=pl.CostEstimate(flops=5000000000, bytes_accessed=4000000, transcendentals=0),
         compiler_params=pltpu.CompilerParams(vmem_limit_bytes=24 << 20),
         name="gain",
-    )(observed_blocks[0], eastern_average_flags[0], observed_values[0], observed_error[0], *flat)
-    carried = [(outs[-1], [(0, 0)])]
-    for bit, sent, top in zip(bits, outs, tops):
-        moving = [(a, g) for a, g in carried if any(left & bit for left, _ in g)]
-        moving.append((sent, [(masks[j], 0) for j in top]))
-        stay = [(a, [(left if not left & bit else -1, pm) for left, pm in g]) for a, g in carried]
-        came = [
-            (
-                lax.ppermute(a, "mem", xor_pairs(mems, bit)),
-                [(left ^ bit if left > 0 and left & bit else -1, pm ^ bit) for left, pm in g],
-            )
-            for a, g in moving
-        ]
-        carried = stay + came
-    where = {}
-    for index, (_, g) in enumerate(carried):
-        for at, (left, pm) in enumerate(g):
-            if left == 0:
-                where[pm] = (index, at)
+    )(*tables, *flat)
+    came = {0: outs[0]}
+    for mask in sorted(masks[1:], reverse=True):
+        pairs = [(i, i ^ mask) for i in range(mems)]
+        came[mask] = lax.ppermute(outs[masks.index(mask)], "mem", pairs)
     return pl.pallas_call(
-        functools.partial(place_kernel, masks, where, longitudes),
+        functools.partial(place_kernel, masks, longitudes),
         out_shape=jax.ShapeDtypeStruct((local, rows, longitudes), F32),
-        in_specs=[VMEM] * len(carried),
+        in_specs=[VMEM] * mems,
         out_specs=VMEM,
         cost_estimate=pl.CostEstimate(flops=100000, bytes_accessed=600000, transcendentals=0),
         compiler_params=pltpu.CompilerParams(vmem_limit_bytes=8 << 20),
         name="place",
-    )(*[a for a, _ in carried])
+    )(*[came[m] for m in masks])
 
 
 def solution(mesh):

time: 41.1 us -> 37.5 us (0.912)
  starting transfers between devices: 16.2 us -> 11.8 us
  waiting for transfers between devices: 14.3 us -> 15.7 us
  local copies, waits for them, and re-layouts: 1.71 us -> 1.05 us
    ppermute x2, starting transfers between devices: 7.46 us -> 3.02 us  [body(): far.append(lax.ppermute(near[k], 'lat', far_pairs))]
    ppermute x2, waiting for transfers between devices: 0.44 us -> 2.54 us  [body(): far.append(lax.ppermute(near[k], 'lat', far_pairs))]
    ppermute x3, waiting for transfers between devices: 5.06 us -> 3.14 us  [body(): came[mask] = lax.ppermute(outs[masks.index(mask)], 'mem', pairs)]
    ppermute x2, waiting for transfers between devices: 4.45 us -> 5.17 us  [body(): near.append(lax.ppermute(own, 'lat', near_pairs))]
    unnamed x14, local copies, waits for them, and re-layouts: 0.7 us -> 0.04 us
    ppermute x6, waiting for transfers between devices: 4.36 us -> 4.8 us  [body(): held = held + [lax.ppermute(a, 'mem', xor_pairs(mems, bit)) for a in held]]
  transfers between devices with their start and end apart: 13 -> 13, of which waited for: 7 -> 8; matrix products, arithmetic and copies ran while one was open for 0% -> 0% of each run, Pallas kernels for 3% -> 3%
where the time goes in v3:
time: 37.5 us; the launch traced here: 37.3 us
  waiting for transfers between devices  15.7 us (42%)
  starting transfers between devices  11.8 us (31%)
  Pallas kernels  8.6 us (23%)
  local copies, waits for them, and re-layouts  1.05 us (3%)
    pallas_call x1, Pallas kernels, body(): pl.pallas_call(functools.partial(gain_kernel, mems, pieces, longitudes),...  6.7 us
    ppermute x2, waiting for transfers between devices, body(): near.append(lax.ppermute(own, 'lat', near_pairs))  5.17 us
    ppermute x6, waiting for transfers between devices, body(): held = held + [lax.ppermute(a, 'mem', xor_pairs(mems, bit)) for a in held]  4.8 us
    ppermute x6, starting transfers between devices, body(): held = held + [lax.ppermute(a, 'mem', xor_pairs(mems, bit)) for a in held]  3.47 us
    ppermute x2, starting transfers between devices, body(): near.append(lax.ppermute(own, 'lat', near_pairs))  3.14 us
    ppermute x3, waiting for transfers between devices, body(): came[mask] = lax.ppermute(outs[masks.index(mask)], 'mem', pairs)  3.14 us
    ppermute x2, starting transfers between devices, body(): far.append(lax.ppermute(near[k], 'lat', far_pairs))  3.02 us
    ppermute x2, waiting for transfers between devices, body(): far.append(lax.ppermute(near[k], 'lat', far_pairs))  2.54 us
  transfers between devices with their start and end apart: 13, of which 8 were waited for; matrix products, arithmetic and copies ran while one was open for 0% of the time, Pallas kernels for 3%

profile of v3, /device:TPU:0, one launch (start us, length us, event | category | flops | bytes accessed | tf_op | source)
XLA Modules:
  0.0 37.3 jit_solution(13578559932262217449)
XLA Ops:
  0.0 1.0 %fusion = (f32[32,2,512]{2,1,0:T(2,128)S(1)}, f32[32,2,512]{2,1,0:T(2,128)S(1)}) fusion(f32[64,2,512]{2,1,0:T(2,128)} %own.3), kind=kLoop, calls=%fused_computation.1 | loop fusion | bytes 524288 | tf_op jit(solution)/shard_map/slice | solution.py:198
  1.0 0.0 copy-start
  1.1 0.1 pad_maximum_fusion
  1.2 3.1 %collective-permute-start = (f32[34,2,512]{2,1,0:T(2,128)S(1)}, f32[34,2,512]{2,1,0:T(2,128)S(1)}, u32[]{:S(2)}, u32[]{:S(2)}) collective-permute-start(f32[34,2,512]{2,1,0:T(2,128)S(1)} %pad_maximum_fusion), channel_id=1, source_target_pairs={{0,1},{1,0},{2,3},{3,2},{4,5},{5,4},{6,7},{7,6},{8,9},{9,8},{10,11... | collective-permute-start | bytes 417800 | tf_op jit(solution)/shard_map/ppermute | solution.py:201
  4.2 0.1 collective-permute-start.2
  4.3 4.4 %collective-permute-done.near.coef_near = f32[34,2,512]{2,1,0:T(2,128)S(1)} collective-permute-done((f32[34,2,512]{2,1,0:T(2,128)S(1)}, f32[34,2,512]{2,1,0:T(2,128)S(1)}, u32[]{:S(2)}, u32[]{:S(2)}) %collective-permute-start) | collective-permute-done | bytes 139296 | tf_op jit(solution)/shard_map/ppermute | solution.py:201
  8.8 2.1 %collective-permute-start.1 = (f32[34,2,512]{2,1,0:T(2,128)S(1)}, f32[34,2,512]{2,1,0:T(2,128)S(1)}, u32[]{:S(2)}, u32[]{:S(2)}) collective-permute-start(f32[34,2,512]{2,1,0:T(2,128)S(1)} %collective-permute-done.near.coef_near), channel_id=1, source_target_pairs={{0,2},{2,4},{4,6},{3,1},{5,3},{7,5},{6,7},{1,0},{8,10},{10,12},{12... | collective-permute-start | bytes 417800 | tf_op jit(solution)/shard_map/ppermute | solution.py:203
  10.8 0.7 %collective-permute-done.2.near = f32[32,2,512]{2,1,0:T(2,128)S(1)} collective-permute-done((f32[32,2,512]{2,1,0:T(2,128)S(1)}, f32[32,2,512]{2,1,0:T(2,128)S(1)}, u32[]{:S(2)}, u32[]{:S(2)}) %collective-permute-start.2) | collective-permute-done | bytes 131104 | tf_op jit(solution)/shard_map/ppermute | solution.py:201
  11.6 0.9 %collective-permute-start.3 = (f32[32,2,512]{2,1,0:T(2,128)S(1)}, f32[32,2,512]{2,1,0:T(2,128)S(1)}, u32[]{:S(2)}, u32[]{:S(2)}) collective-permute-start(f32[32,2,512]{2,1,0:T(2,128)S(1)} %collective-permute-done.2.near), channel_id=1, source_target_pairs={{0,2},{2,4},{4,6},{3,1},{5,3},{7,5},{6,7},{1,0},{8,10},{10,12},{12... | collective-permute-start | bytes 393224 | tf_op jit(solution)/shard_map/ppermute | solution.py:203
  12.5 2.5 %collective-permute-done.1.far.coef_far = f32[34,2,512]{2,1,0:T(2,128)S(1)} collective-permute-done((f32[34,2,512]{2,1,0:T(2,128)S(1)}, f32[34,2,512]{2,1,0:T(2,128)S(1)}, u32[]{:S(2)}, u32[]{:S(2)}) %collective-permute-start.1) | collective-permute-done | bytes 139296 | tf_op jit(solution)/shard_map/ppermute | solution.py:203
  15.1 0.5 %forecast.2.refs_0_ = f32[32,1024]{1,0:T(8,128)S(1)} custom-call(f32[64,2,512]{2,1,0:T(2,128)S(1)} %copy-done, f32[2,512]{1,0:T(2,128)S(1)} %copy-done.1, f32[2,512]{1,0:T(2,128)S(1)} %copy-done.2, f32[34,2,512]{2,1,0:T(2,128)S(1)} %collective-permute-done.near.coef_near, f32[34,2,512]{2,1,0:T(2,128)S(1)} %collective-permute-done.1.far.coef_far, ...), custom_call_target="tpu_custom_call" | custom-call | flops 2000000 | bytes 2000000 | tf_op jit(solution)/shard_map/forecast/pallas_call | solution.py:207
  15.6 1.9 %collective-permute-start.4 = (f32[32,1024]{1,0:T(8,128)S(1)}, f32[32,1024]{1,0:T(8,128)S(1)}, u32[]{:S(2)}, u32[]{:S(2)}) collective-permute-start(f32[32,1024]{1,0:T(8,128)S(1)} %forecast.2.refs_0_), channel_id=1, source_target_pairs={{0,16},{8,24},{16,0},{24,8},{1,17},{9,25},{17,1},{25,9},{2,18},{10... | collective-permute-start | bytes 393224 | tf_op jit(solution)/shard_map/ppermute | solution.py:218
  17.5 0.5 %forecast.3.refs_1_ = f32[32,1024]{1,0:T(8,128)S(1)} custom-call(f32[64,2,512]{2,1,0:T(2,128)S(1)} %copy-done, f32[2,512]{1,0:T(2,128)S(1)} %copy-done.1, f32[2,512]{1,0:T(2,128)S(1)} %copy-done.2, f32[32,2,512]{2,1,0:T(2,128)S(1)} %collective-permute-done.2.near, f32[32,2,512]{2,1,0:T(2,128)S(1)} %collective-permute-done.3.far, ...), custom_call_target="tpu_custom_call" | custom-call | flops 2000000 | bytes 2000000 | tf_op jit(solution)/shard_map/forecast/pallas_call | solution.py:207
  18.1 1.0 %collective-permute-start.5 = (f32[32,1024]{1,0:T(8,128)S(1)}, f32[32,1024]{1,0:T(8,128)S(1)}, u32[]{:S(2)}, u32[]{:S(2)}) collective-permute-start(f32[32,1024]{1,0:T(8,128)S(1)} %forecast.3.refs_1_), channel_id=1, source_target_pairs={{0,16},{8,24},{16,0},{24,8},{1,17},{9,25},{17,1},{25,9},{2,18},{10... | collective-permute-start | bytes 393224 | tf_op jit(solution)/shard_map/ppermute | solution.py:218
  19.1 0.5 %collective-permute-start.7 = (f32[32,1024]{1,0:T(8,128)S(1)}, f32[32,1024]{1,0:T(8,128)S(1)}, u32[]{:S(2)}, u32[]{:S(2)}) collective-permute-start(f32[32,1024]{1,0:T(8,128)S(1)} %forecast.3.refs_1_), channel_id=1, source_target_pairs={{0,8},{8,0},{16,24},{24,16},{1,9},{9,1},{17,25},{25,17},{2,10},{10... | collective-permute-start | bytes 393224 | tf_op jit(solution)/shard_map/ppermute | solution.py:218
  19.6 1.8 %collective-permute-done.4.refs_2_ = f32[32,1024]{1,0:T(8,128)S(1)} collective-permute-done((f32[32,1024]{1,0:T(8,128)S(1)}, f32[32,1024]{1,0:T(8,128)S(1)}, u32[]{:S(2)}, u32[]{:S(2)}) %collective-permute-start.4) | collective-permute-done | bytes 131104 | tf_op jit(solution)/shard_map/ppermute | solution.py:218
  21.4 1.7 %collective-permute-done.5.refs_3_ = f32[32,1024]{1,0:T(8,128)S(1)} collective-permute-done((f32[32,1024]{1,0:T(8,128)S(1)}, f32[32,1024]{1,0:T(8,128)S(1)}, u32[]{:S(2)}, u32[]{:S(2)}) %collective-permute-start.5) | collective-permute-done | bytes 131104 | tf_op jit(solution)/shard_map/ppermute | solution.py:218
  23.1 1.3 %collective-permute-done.9.refs_7_ = f32[32,1024]{1,0:T(8,128)S(1)} collective-permute-done((f32[32,1024]{1,0:T(8,128)S(1)}, f32[32,1024]{1,0:T(8,128)S(1)}, u32[]{:S(2)}, u32[]{:S(2)}) %collective-permute-start.9) | collective-permute-done | bytes 131104 | tf_op jit(solution)/shard_map/ppermute | solution.py:218
  24.5 6.7 %gain.1 = (f32[64,256]{1,0:T(8,128)S(1)}, f32[64,256]{1,0:T(8,128)S(1)}, f32[64,256]{1,0:T(8,128)S(1)}, f32[64,256]{1,0:T(8,128)S(1)}) custom-call(s32[4,4]{1,0:T(4,128)S(1)} %bitcast.13, s32[4,512]{1,0:T(4,128)S(1)} %bitcast.10, f32[1,512]{1,0:T(1,128)S(1)} %bitcast.16, f32[1,512]{1,0:T(1,128)S(1)} %bitcast.19, f32[32,1024]{1,0:T(8,128)S(1)} %forecast.2.refs_0_, ...), custom_call_target="tpu_custom_call" | custom-call | flops 5000000000 | bytes 4000000 | tf_op jit(solution)/shard_map/gain/pallas_call | solution.py:226
  31.2 1.0 %collective-permute-start.10 = (f32[64,256]{1,0:T(8,128)S(1)}, f32[64,256]{1,0:T(8,128)S(1)}, u32[]{:S(2)}, u32[]{:S(2)}) collective-permute-start(f32[64,256]{1,0:T(8,128)S(1)} %get-tuple-element.10), channel_id=1, source_target_pairs={{0,16},{8,24},{16,0},{24,8},{1,17},{9,25},{17,1},{25,9},{2,18},{10... | collective-permute-start | bytes 196616 | tf_op jit(solution)/shard_map/ppermute | solution.py:239
  32.2 1.2 %collective-permute-start.12 = (f32[64,256]{1,0:T(8,128)S(1)}, f32[64,256]{1,0:T(8,128)S(1)}, u32[]{:S(2)}, u32[]{:S(2)}) collective-permute-start(f32[64,256]{1,0:T(8,128)S(1)} %get-tuple-element.12), channel_id=1, source_target_pairs={{0,24},{8,16},{16,8},{24,0},{1,25},{9,17},{17,9},{25,1},{2,26},{10... | collective-permute-start | bytes 196616 | tf_op jit(solution)/shard_map/ppermute | solution.py:239
  33.4 2.4 %collective-permute-done.10.refs_1_ = f32[64,256]{1,0:T(8,128)S(1)} collective-permute-done((f32[64,256]{1,0:T(8,128)S(1)}, f32[64,256]{1,0:T(8,128)S(1)}, u32[]{:S(2)}, u32[]{:S(2)}) %collective-permute-start.10) | collective-permute-done | bytes 65568 | tf_op jit(solution)/shard_map/ppermute | solution.py:239
  35.8 0.7 %collective-permute-done.12.refs_3_ = f32[64,256]{1,0:T(8,128)S(1)} collective-permute-done((f32[64,256]{1,0:T(8,128)S(1)}, f32[64,256]{1,0:T(8,128)S(1)}, u32[]{:S(2)}, u32[]{:S(2)}) %collective-permute-start.12) | collective-permute-done | bytes 65568 | tf_op jit(solution)/shard_map/ppermute | solution.py:239
  36.5 0.8 %place.1 = f32[64,2,512]{2,1,0:T(2,128)} custom-call(f32[64,256]{1,0:T(8,128)S(1)} %get-tuple-element.9.refs_0_, f32[64,256]{1,0:T(8,128)S(1)} %collective-permute-done.10.refs_1_, f32[64,256]{1,0:T(8,128)S(1)} %collective-permute-done.11.refs_2_, f32[64,256]{1,0:T(8,128)S(1)} %collective-permute-done.12.refs_3_), custom_call_target="tpu_custom_call" | custom-call | flops 100000 | bytes 600000 | tf_op jit(solution)/shard_map/place/pallas_call | solution.py:240
  (22 shorter events, 0.1 us)
Async XLA Ops:
  0.0 1.0 %copy-start.1 = (f32[2,512]{1,0:T(2,128)S(1)}, f32[2,512]{1,0:T(2,128)}, u32[]{:S(2)}) copy-start(f32[2,512]{1,0:T(2,128)} %dif.3) | copy-start | bytes 12292
  0.0 1.0 %copy-start.2 = (f32[2,512]{1,0:T(2,128)S(1)}, f32[2,512]{1,0:T(2,128)}, u32[]{:S(2)}) copy-start(f32[2,512]{1,0:T(2,128)} %wind.3) | copy-start | bytes 12292
  1.0 14.0 %copy-start = (f32[64,2,512]{2,1,0:T(2,128)S(1)}, f32[64,2,512]{2,1,0:T(2,128)}, u32[]{:S(2)}) copy-start(f32[64,2,512]{2,1,0:T(2,128)} %own.3) | copy-start | bytes 786436
  1.1 14.0 %copy-start.4 = (s32[1,4,4]{2,1,0:T(4,128)S(1)}, s32[1,4,4]{2,1,0:T(4,128)}, u32[]{:S(2)}) copy-start(s32[1,4,4]{2,1,0:T(4,128)} %param.10) | copy-start | bytes 196
  1.1 14.0 %copy-start.5 = (f32[1,1,512]{2,1,0:T(1,128)S(1)}, f32[1,1,512]{2,1,0:T(1,128)}, u32[]{:S(2)}) copy-start(f32[1,1,512]{2,1,0:T(1,128)} %param.12) | copy-start | bytes 6148
  1.1 14.0 %copy-start.6 = (f32[1,1,512]{2,1,0:T(1,128)S(1)}, f32[1,1,512]{2,1,0:T(1,128)}, u32[]{:S(2)}) copy-start(f32[1,1,512]{2,1,0:T(1,128)} %param.13) | copy-start | bytes 6148
  1.2 13.9 %copy-start.3 = (s32[1,4,512]{2,1,0:T(4,128)S(1)}, s32[1,4,512]{2,1,0:T(4,128)}, u32[]{:S(2)}) copy-start(s32[1,4,512]{2,1,0:T(4,128)} %param.11) | copy-start | bytes 24580
  1.2 7.6 %collective-permute-start = (f32[34,2,512]{2,1,0:T(2,128)S(1)}, f32[34,2,512]{2,1,0:T(2,128)S(1)}, u32[]{:S(2)}, u32[]{:S(2)}) collective-permute-start(f32[34,2,512]{2,1,0:T(2,128)S(1)} %pad_maximum_fusion), channel_id=1, source_target_pairs={{0,1},{1,0},{2,3},{3,2},{4,5},{5,4},{6,7},{7,6},{8,9},{9,8},{10,11... | collective-permute-start | bytes 417800 | tf_op jit(solution)/shard_map/ppermute | solution.py:201
  4.2 7.3 %collective-permute-start.2 = (f32[32,2,512]{2,1,0:T(2,128)S(1)}, f32[32,2,512]{2,1,0:T(2,128)S(1)}, u32[]{:S(2)}, u32[]{:S(2)}) collective-permute-start(f32[32,2,512]{2,1,0:T(2,128)S(1)} %get-tuple-element.13), channel_id=1, source_target_pairs={{0,1},{1,0},{2,3},{3,2},{4,5},{5,4},{6,7},{7,6},{8,9},{9,8},{10,11... | collective-permute-start | bytes 393224 | tf_op jit(solution)/shard_map/ppermute | solution.py:201
  8.8 6.3 %collective-permute-start.1 = (f32[34,2,512]{2,1,0:T(2,128)S(1)}, f32[34,2,512]{2,1,0:T(2,128)S(1)}, u32[]{:S(2)}, u32[]{:S(2)}) collective-permute-start(f32[34,2,512]{2,1,0:T(2,128)S(1)} %collective-permute-done.near.coef_near), channel_id=1, source_target_pairs={{0,2},{2,4},{4,6},{3,1},{5,3},{7,5},{6,7},{1,0},{8,10},{10,12},{12... | collective-permute-start | bytes 417800 | tf_op jit(solution)/shard_map/ppermute | solution.py:203
  11.6 6.0 %collective-permute-start.3 = (f32[32,2,512]{2,1,0:T(2,128)S(1)}, f32[32,2,512]{2,1,0:T(2,128)S(1)}, u32[]{:S(2)}, u32[]{:S(2)}) collective-permute-start(f32[32,2,512]{2,1,0:T(2,128)S(1)} %collective-permute-done.2.near), channel_id=1, source_target_pairs={{0,2},{2,4},{4,6},{3,1},{5,3},{7,5},{6,7},{1,0},{8,10},{10,12},{12... | collective-permute-start | bytes 393224 | tf_op jit(solution)/shard_map/ppermute | solution.py:203
  15.6 5.8 %collective-permute-start.4 = (f32[32,1024]{1,0:T(8,128)S(1)}, f32[32,1024]{1,0:T(8,128)S(1)}, u32[]{:S(2)}, u32[]{:S(2)}) collective-permute-start(f32[32,1024]{1,0:T(8,128)S(1)} %forecast.2.refs_0_), channel_id=1, source_target_pairs={{0,16},{8,24},{16,0},{24,8},{1,17},{9,25},{17,1},{25,9},{2,18},{10... | collective-permute-start | bytes 393224 | tf_op jit(solution)/shard_map/ppermute | solution.py:218
  18.1 5.0 %collective-permute-start.5 = (f32[32,1024]{1,0:T(8,128)S(1)}, f32[32,1024]{1,0:T(8,128)S(1)}, u32[]{:S(2)}, u32[]{:S(2)}) collective-permute-start(f32[32,1024]{1,0:T(8,128)S(1)} %forecast.3.refs_1_), channel_id=1, source_target_pairs={{0,16},{8,24},{16,0},{24,8},{1,17},{9,25},{17,1},{25,9},{2,18},{10... | collective-permute-start | bytes 393224 | tf_op jit(solution)/shard_map/ppermute | solution.py:218
  19.1 4.0 %collective-permute-start.6 = (f32[32,1024]{1,0:T(8,128)S(1)}, f32[32,1024]{1,0:T(8,128)S(1)}, u32[]{:S(2)}, u32[]{:S(2)}) collective-permute-start(f32[32,1024]{1,0:T(8,128)S(1)} %forecast.2.refs_0_), channel_id=1, source_target_pairs={{0,8},{8,0},{16,24},{24,16},{1,9},{9,1},{17,25},{25,17},{2,10},{10... | collective-permute-start | bytes 393224 | tf_op jit(solution)/shard_map/ppermute | solution.py:218
  19.1 4.0 %collective-permute-start.7 = (f32[32,1024]{1,0:T(8,128)S(1)}, f32[32,1024]{1,0:T(8,128)S(1)}, u32[]{:S(2)}, u32[]{:S(2)}) collective-permute-start(f32[32,1024]{1,0:T(8,128)S(1)} %forecast.3.refs_1_), channel_id=1, source_target_pairs={{0,8},{8,0},{16,24},{24,16},{1,9},{9,1},{17,25},{25,17},{2,10},{10... | collective-permute-start | bytes 393224 | tf_op jit(solution)/shard_map/ppermute | solution.py:218
  21.4 1.7 %collective-permute-start.8 = (f32[32,1024]{1,0:T(8,128)S(1)}, f32[32,1024]{1,0:T(8,128)S(1)}, u32[]{:S(2)}, u32[]{:S(2)}) collective-permute-start(f32[32,1024]{1,0:T(8,128)S(1)} %collective-permute-done.4.refs_2_), channel_id=1, source_target_pairs={{0,8},{8,0},{16,24},{24,16},{1,9},{9,1},{17,25},{25,17},{2,10},{10... | collective-permute-start | bytes 393224 | tf_op jit(solution)/shard_map/ppermute | solution.py:218
  23.1 1.3 %collective-permute-start.9 = (f32[32,1024]{1,0:T(8,128)S(1)}, f32[32,1024]{1,0:T(8,128)S(1)}, u32[]{:S(2)}, u32[]{:S(2)}) collective-permute-start(f32[32,1024]{1,0:T(8,128)S(1)} %collective-permute-done.5.refs_3_), channel_id=1, source_target_pairs={{0,8},{8,0},{16,24},{24,16},{1,9},{9,1},{17,25},{25,17},{2,10},{10... | collective-permute-start | bytes 393224 | tf_op jit(solution)/shard_map/ppermute | solution.py:218
  31.2 4.6 %collective-permute-start.10 = (f32[64,256]{1,0:T(8,128)S(1)}, f32[64,256]{1,0:T(8,128)S(1)}, u32[]{:S(2)}, u32[]{:S(2)}) collective-permute-start(f32[64,256]{1,0:T(8,128)S(1)} %get-tuple-element.10), channel_id=1, source_target_pairs={{0,16},{8,24},{16,0},{24,8},{1,17},{9,25},{17,1},{25,9},{2,18},{10... | collective-permute-start | bytes 196616 | tf_op jit(solution)/shard_map/ppermute | solution.py:239
  32.2 3.6 %collective-permute-start.11 = (f32[64,256]{1,0:T(8,128)S(1)}, f32[64,256]{1,0:T(8,128)S(1)}, u32[]{:S(2)}, u32[]{:S(2)}) collective-permute-start(f32[64,256]{1,0:T(8,128)S(1)} %get-tuple-element.11), channel_id=1, source_target_pairs={{0,8},{8,0},{16,24},{24,16},{1,9},{9,1},{17,25},{25,17},{2,10},{10... | collective-permute-start | bytes 196616 | tf_op jit(solution)/shard_map/ppermute | solution.py:239
  32.2 4.3 %collective-permute-start.12 = (f32[64,256]{1,0:T(8,128)S(1)}, f32[64,256]{1,0:T(8,128)S(1)}, u32[]{:S(2)}, u32[]{:S(2)}) collective-permute-start(f32[64,256]{1,0:T(8,128)S(1)} %get-tuple-element.12), channel_id=1, source_target_pairs={{0,24},{8,16},{16,8},{24,0},{1,25},{9,17},{17,9},{25,1},{2,26},{10... | collective-permute-start | bytes 196616 | tf_op jit(solution)/shard_map/ppermute | solution.py:239

commit v4 on v3

--- a/solution.py
+++ b/solution.py
@@ -7,7 +7,7 @@
 from jax.experimental.pallas import tpu as pltpu
 from jax.sharding import PartitionSpec as P
 
-NEWTON = 4
+
 ADVECTION = 0.1
 F32 = jnp.float32
 BF16 = jnp.bfloat16
@@ -80,75 +80,123 @@
     return high, (x - high.astype(F32)).astype(BF16)
 
 
-def dot3(a, b, dims=(((1,), (0,)), ((), ()))):
-    mul = functools.partial(lax.dot_general, dimension_numbers=dims, preferred_element_type=F32)
-    return mul(a[0], b[0]) + (mul(a[0], b[1]) + mul(a[1], b[0]))
-
-
-def gain_kernel(groups, pieces, longitudes, blocks, flags, values, errors, *refs):
-    parts = refs[: groups * pieces]
-    outs = refs[groups * pieces : -2]
-    seen, cells = refs[-2:]
+def dot3(a, b, width=256):
+    rows = a[0].shape[0]
+    mul = functools.partial(jnp.dot, preferred_element_type=F32)
+    stacked = jnp.concatenate(a, axis=0)
+    out = []
+    for at in range(0, b[0].shape[1], width):
+        both = mul(stacked, b[0][:, at : at + width])
+        out.append(both[:rows] + (both[rows:] + mul(a[0], b[1][:, at : at + width])))
+    return jnp.concatenate(out, axis=1)
+
+
+def dot1(a, b, width=256):
+    mul = functools.partial(jnp.dot, preferred_element_type=F32)
+    return jnp.concatenate([mul(a, b[:, at : at + width]) for at in range(0, b.shape[1], width)], axis=1)
+
+
+def observe(parts, longitudes, own_cells, blocks, flags):
     patch = lax.axis_index("mem")
-    total, observations = seen.shape
-    own_cells = cells.shape[1]
     block_count = blocks.shape[1]
-    width = observations // block_count
+    width = flags.shape[1] // block_count
     row_blocks = longitudes // width
     flag = flags[pl.ds(patch, 1), :]
     lane = lax.broadcasted_iota(jnp.int32, (1, width), 1)
+    columns = []
     for i in range(block_count):
         c = blocks[patch, i]
         row = lax.div(c, row_blocks)
         n = row * row_blocks + lax.rem(c - row * row_blocks + 1, row_blocks)
         averaged = flag[:, i * width : (i + 1) * width] == 1
-        at = 0
+        values = []
         for part in parts:
-            size = part.shape[0]
             direct = part[:, pl.ds(pl.multiple_of(c * width, width), width)]
             beyond = part[:, pl.ds(pl.multiple_of(n * width, width), width)]
-            east = jnp.where(
-                lane == width - 1, pltpu.roll(beyond, width - 1, 1), pltpu.roll(direct, width - 1, 1)
-            )
-            seen[at : at + size, i * width : (i + 1) * width] = jnp.where(
-                averaged, 0.5 * (direct + east), direct
-            )
-            at += size
-    at = 0
-    for part in parts:
-        size = part.shape[0]
-        cells[at : at + size, :] = part[:, pl.ds(pl.multiple_of(patch * own_cells, own_cells), own_cells)]
-        at += size
+            east = pltpu.roll(jnp.where(lane == 0, beyond, direct), width - 1, 1)
+            values.append(jnp.where(averaged, 0.5 * (direct + east), direct))
+        columns.append(jnp.concatenate(values, axis=0))
+    return jnp.concatenate(columns, axis=1), own(parts, own_cells)
+
+
+def own(parts, own_cells):
+    at = pl.multiple_of(lax.axis_index("mem") * own_cells, own_cells)
+    return jnp.concatenate([part[:, pl.ds(at, own_cells)] for part in parts], axis=0)
+
+
+def doubled(x):
+    high, low = split(x)
+    return jnp.concatenate([high, high, low, low], axis=0)
+
+
+def moments(seen, cells, before, count):
+    if before is None:
+        seen_mean = jnp.sum(seen, axis=0, keepdims=True) * (1.0 / count)
+        cell_mean = jnp.sum(cells, axis=0, keepdims=True) * (1.0 / count)
+        left = seen - seen_mean
+        right, right_cells = left, cells - cell_mean
+    else:
+        left, right_cells = seen - before[0], cells - before[1]
+        shift = jnp.sum(left, axis=0, keepdims=True) * (1.0 / count)
+        cell_shift = jnp.sum(right_cells, axis=0, keepdims=True) * (1.0 / count)
+        seen_mean, cell_mean = before[0] + shift, before[1] + cell_shift
+        right, right_cells = left - shift, right_cells - cell_shift
+    turned = jnp.concatenate(split(left), axis=0).T
+    turned = jnp.concatenate([turned, turned], axis=1)
+    return dot1(turned, doubled(right)), dot1(turned, doubled(right_cells)), seen_mean, cell_mean
+
+
+def moment_kernel(has_before, count, longitudes, blocks, flags, *refs):
+    refs = list(refs)
+    outs = refs[-5:]
+    before = refs[:4] if has_before else None
+    parts = refs[4 if has_before else 0 : -5]
+    seen, cells = observe(parts, longitudes, outs[1].shape[1], blocks, flags)
+    means = None if before is None else (before[2][...], before[3][...])
+    square, cross, seen_mean, cell_mean = moments(seen, cells, means, count)
+    if before is not None:
+        square, cross = square + before[0][...], cross + before[1][...]
+    for out, value in zip(outs, (square, cross, seen_mean, cell_mean, seen)):
+        out[...] = value
+
+
+def gain_kernel(earlier, last, order, longitudes, blocks, flags, values, errors, *refs):
+    cov, outs = refs[-1], refs[-1 - (1 + max(j for j, _ in order)) : -1]
+    before, first_seen, parts = refs[:4], refs[4 : 4 + earlier], refs[4 + earlier : 4 + earlier + len(order)]
+    own_cells = outs[0].shape[1]
+    total = sum(part.shape[0] for part in parts)
     scale = 1.0 / (total - 1.0)
-    raw = seen[...]
-    seen_mean = jnp.sum(raw, axis=0, keepdims=True) * (1.0 / total)
-    offset = raw - seen_mean
-    off = split(offset)
-    turned = split(offset.T)
-    covariance = dot3(turned, off) * scale
-    down = lax.broadcasted_iota(jnp.int32, covariance.shape, 0)
-    across = lax.broadcasted_iota(jnp.int32, covariance.shape, 1)
-    covariance = covariance + jnp.where(down == across, errors[...], 0.0)
+    last_seen, last_cells = observe(parts[-last:], longitudes, own_cells, blocks, flags)
+    square, cross, seen_mean, _ = moments(last_seen, last_cells, (before[2][...], before[3][...]), total)
+    cross = split((cross + before[1][...]) * scale)
+    cov[...] = (square + before[0][...]) * scale
+    tile = 128
+    down = lax.broadcasted_iota(jnp.int32, (tile, tile), 0)
+    across = lax.broadcasted_iota(jnp.int32, (tile, tile), 1)
+    for at in range(0, cov.shape[0], tile):
+        here = slice(at, at + tile)
+        cov[here, here] += jnp.where(down == across, errors[:, here], 0.0)
+    covariance = cov[...]
     inverse_scale = 1.0 / jnp.sum(jnp.abs(covariance), axis=0, keepdims=True)
-    start = ((values[...] - seen_mean) - 0.5 * offset) * inverse_scale
+    seen = jnp.concatenate([ref[...] for ref in first_seen] + [last_seen], axis=0)
+    start = ((values[...] - seen_mean) - 0.5 * (seen - seen_mean)) * inverse_scale
     b1 = covariance * inverse_scale
     s1 = split(b1)
     b2 = 2.0 * b1 - dot3(s1, s1)
     s2 = split(b2)
     b4 = 2.0 * b2 - dot3(s2, s2)
     s4 = split(b4)
-    q = start
-    for _ in range(3):
+    q = start + (start - dot1(start.astype(BF16), s4[0]))
+    for _ in range(2):
         q = start + (q - dot3(split(q), s4))
     q = 2.0 * q - dot3(split(q), s2)
     q = 2.0 * q - dot3(split(q), s1)
-    mix = dot3(split(q), off, (((1,), (1,)), ((), ()))) * scale
-    state = cells[...]
-    shift = state - jnp.sum(state, axis=0, keepdims=True) * (1.0 / total)
-    analysed = state + dot3(split(mix), split(shift))
-    size = total // groups
-    for j, out in enumerate(outs):
-        out[...] = analysed[j * size : (j + 1) * size, :]
+    update = dot3(split(q), cross)
+    at = 0
+    for part, (j, row) in zip(parts, order):
+        size = part.shape[0]
+        outs[j][row : row + size, :] = own([part], own_cells) + update[at : at + size, :]
+        at += size
 
 
 def place_kernel(masks, longitudes, *refs):
@@ -178,7 +226,6 @@
     observations = observed_values.shape[-1]
     cell_count = rows * longitudes
     own_cells = cell_count // mems
-    total = local * mems
     near_pairs = xor_pairs(lats, 1)
     far_pairs = [(i, i + 2) for i in range(0, lats - 2, 2)] + [(i, i - 2) for i in range(3, lats, 2)]
     far_pairs += [(lats - 2, lats - 1), (1, 0)]
@@ -202,7 +249,19 @@
     for k in range(pieces):
         far.append(lax.ppermute(near[k], "lat", far_pairs))
     tables = observed_blocks[0], eastern_average_flags[0], observed_values[0], observed_error[0]
-    parts = [[] for _ in range(pieces)]
+    top, low_bits = bits[0], bits[1:]
+
+    def spread(a):
+        held = [a]
+        for bit in low_bits:
+            held = held + [lax.ppermute(b, "mem", xor_pairs(mems, bit)) for b in held]
+        return held
+
+    masks = [0]
+    for bit in low_bits:
+        masks = masks + [m ^ bit for m in masks]
+    masks = masks + [m ^ top for m in masks]
+    near_half, far_half = [], []
     for k in range(pieces):
         band = pl.pallas_call(
             functools.partial(forecast_kernel, lats, firsts[k], counts[k], 2 if k == 0 else 0),
@@ -211,28 +270,51 @@
             out_specs=VMEM,
             cost_estimate=pl.CostEstimate(flops=2000000, bytes_accessed=2000000, transcendentals=0),
             compiler_params=pltpu.CompilerParams(vmem_limit_bytes=8 << 20),
-            name="forecast",
         )(ensemble, diffusivity, north_wind, near[k], far[k], near[0], far[0], *tables)
-        held = [band]
-        for bit in bits:
-            held = held + [lax.ppermute(a, "mem", xor_pairs(mems, bit)) for a in held]
-        parts[k] = held
-    masks = [0]
-    for bit in bits:
-        masks = masks + [m ^ bit for m in masks]
-
-    flat = [parts[k][j] for j in range(mems) for k in range(pieces)]
-    shapes = [jax.ShapeDtypeStruct((local, own_cells), F32) for _ in masks]
+        far_half.append(lax.ppermute(band, "mem", xor_pairs(mems, top)))
+        near_half.append(spread(band))
+
+    def add_moments(stage, before, count):
+        members = sum(a.shape[0] for a in stage)
+        *after, stage_seen = pl.pallas_call(
+            functools.partial(moment_kernel, len(before) > 0, count + members, longitudes),
+            out_shape=[
+                jax.ShapeDtypeStruct((observations, observations), F32),
+                jax.ShapeDtypeStruct((observations, own_cells), F32),
+                jax.ShapeDtypeStruct((1, observations), F32),
+                jax.ShapeDtypeStruct((1, own_cells), F32),
+                jax.ShapeDtypeStruct((members, observations), F32),
+            ],
+            in_specs=[SMEM] + [VMEM] * (1 + len(before) + len(stage)),
+            out_specs=[VMEM] * 5,
+            cost_estimate=pl.CostEstimate(flops=800000000, bytes_accessed=3000000, transcendentals=0),
+            compiler_params=pltpu.CompilerParams(vmem_limit_bytes=16 << 20),
+        )(*tables[:2], *before, *stage)
+        return after, stage_seen
+
+    stage = [near_half[k][j] for k in range(pieces) for j in range(mems // 2)]
+    flat, order = stage, [(j, firsts[k]) for k in range(pieces) for j in range(mems // 2)]
+    before, stage_seen = add_moments(stage, (), 0)
+    seen = [stage_seen]
+    for k in range(pieces):
+        stage = spread(far_half[k])
+        if k < pieces - 1:
+            before, stage_seen = add_moments(stage, before, sum(a.shape[0] for a in flat))
+            seen.append(stage_seen)
+        flat = flat + stage
+        order = order + [(j, firsts[k]) for j in range(mems // 2, mems)]
     outs = pl.pallas_call(
-        functools.partial(gain_kernel, mems, pieces, longitudes),
-        out_shape=shapes,
-        in_specs=[SMEM] + [VMEM] * (3 + len(flat)),
-        out_specs=[VMEM] * len(shapes),
-        scratch_shapes=[pltpu.VMEM((total, observations), F32), pltpu.VMEM((total, own_cells), F32)],
+        functools.partial(
+            gain_kernel, len(seen), len(stage), order, longitudes
+        ),
+        out_shape=[jax.ShapeDtypeStruct((local, own_cells), F32) for _ in masks],
+        in_specs=[SMEM] + [VMEM] * (3 + len(before) + len(seen) + len(flat)),
+        out_specs=[VMEM] * mems,
+        scratch_shapes=[pltpu.VMEM((observations, observations), F32)],
         cost_estimate=pl.CostEstimate(flops=5000000000, bytes_accessed=4000000, transcendentals=0),
         compiler_params=pltpu.CompilerParams(vmem_limit_bytes=24 << 20),
         name="gain",
-    )(*tables, *flat)
+    )(*tables, *before, *seen, *flat)
     came = {0: outs[0]}
     for mask in sorted(masks[1:], reverse=True):
         pairs = [(i, i ^ mask) for i in range(mems)]

time: 37.5 us -> 38 us (1.013)
  Pallas kernels: 8.6 us -> 9.83 us
  waiting for transfers between devices: 15.7 us -> 15.1 us
    ppermute x6, waiting for transfers between devices: 4.8 us -> 3.48 us  [the longest x2 3.47 us: body(): far_half.append(lax.ppermute(band, 'mem', xor_pairs(mems, top)))]
    pallas_call x1 -> x3, Pallas kernels: 6.7 us -> 7.92 us  [the longest x1 5.46 us: body(): pl.pallas_call(functools.partial(gain_kernel, len(seen), len(stage), orde...]
    ppermute x3, waiting for transfers between devices: 3.14 us -> 3.93 us  [body(): came[mask] = lax.ppermute(outs[masks.index(mask)], 'mem', pairs)]
  transfers between devices with their start and end apart: 13 -> 13, of which waited for: 8 -> 7; matrix products, arithmetic and copies ran while one was open for 0% -> 0% of each run, Pallas kernels for 3% -> 9%
where the time goes in v4:
time: 38 us; the launch traced here: 37.9 us
  waiting for transfers between devices  15.1 us (40%)
  starting transfers between devices  11.6 us (31%)
  Pallas kernels  9.83 us (26%)
  local copies, waits for them, and re-layouts  1.05 us (3%)
    pallas_call x1, Pallas kernels, body(): pl.pallas_call(functools.partial(gain_kernel, len(seen), len(stage), orde...  5.46 us
    ppermute x2, waiting for transfers between devices, body(): near.append(lax.ppermute(own, 'lat', near_pairs))  5.17 us
    ppermute x3, waiting for transfers between devices, body(): came[mask] = lax.ppermute(outs[masks.index(mask)], 'mem', pairs)  3.93 us
    ppermute x2, waiting for transfers between devices, body(): far_half.append(lax.ppermute(band, 'mem', xor_pairs(mems, top)))  3.47 us
    ppermute x2, starting transfers between devices, body(): near.append(lax.ppermute(own, 'lat', near_pairs))  3.14 us
    ppermute x2, starting transfers between devices, body(): far.append(lax.ppermute(near[k], 'lat', far_pairs))  3.02 us
    ppermute x2, starting transfers between devices, body(): far_half.append(lax.ppermute(band, 'mem', xor_pairs(mems, top)))  2.96 us
    ppermute x2, waiting for transfers between devices, body(): far.append(lax.ppermute(near[k], 'lat', far_pairs))  2.54 us
  transfers between devices with their start and end apart: 13, of which 7 were waited for; matrix products, arithmetic and copies ran while one was open for 0% of the time, Pallas kernels for 9%

profile of v4, /device:TPU:0, one launch (start us, length us, event | category | flops | bytes accessed | tf_op | source)
XLA Modules:
  0.0 37.9 jit_solution(6991711283522260086)
XLA Ops:
  0.0 1.0 %fusion = (f32[32,2,512]{2,1,0:T(2,128)S(1)}, f32[32,2,512]{2,1,0:T(2,128)S(1)}) fusion(f32[64,2,512]{2,1,0:T(2,128)} %own.3), kind=kLoop, calls=%fused_computation.1 | loop fusion | bytes 524288 | tf_op jit(solution)/shard_map/slice | solution.py:245
  1.2 3.1 %collective-permute-start = (f32[34,2,512]{2,1,0:T(2,128)S(1)}, f32[34,2,512]{2,1,0:T(2,128)S(1)}, u32[]{:S(2)}, u32[]{:S(2)}) collective-permute-start(f32[34,2,512]{2,1,0:T(2,128)S(1)} %pad_maximum_fusion), channel_id=1, source_target_pairs={{0,1},{1,0},{2,3},{3,2},{4,5},{5,4},{6,7},{7,6},{8,9},{9,8},{10,11... | collective-permute-start | bytes 417800 | tf_op jit(solution)/shard_map/ppermute | solution.py:248
  4.2 0.1 collective-permute-start.3
  4.3 4.4 %collective-permute-done.near.coef_near = f32[34,2,512]{2,1,0:T(2,128)S(1)} collective-permute-done((f32[34,2,512]{2,1,0:T(2,128)S(1)}, f32[34,2,512]{2,1,0:T(2,128)S(1)}, u32[]{:S(2)}, u32[]{:S(2)}) %collective-permute-start) | collective-permute-done | bytes 139296 | tf_op jit(solution)/shard_map/ppermute | solution.py:248
  8.8 2.1 %collective-permute-start.1 = (f32[34,2,512]{2,1,0:T(2,128)S(1)}, f32[34,2,512]{2,1,0:T(2,128)S(1)}, u32[]{:S(2)}, u32[]{:S(2)}) collective-permute-start(f32[34,2,512]{2,1,0:T(2,128)S(1)} %collective-permute-done.near.coef_near), channel_id=1, source_target_pairs={{0,2},{2,4},{4,6},{3,1},{5,3},{7,5},{6,7},{1,0},{8,10},{10,12},{12... | collective-permute-start | bytes 417800 | tf_op jit(solution)/shard_map/ppermute | solution.py:250
  10.8 0.7 %collective-permute-done.3.near = f32[32,2,512]{2,1,0:T(2,128)S(1)} collective-permute-done((f32[32,2,512]{2,1,0:T(2,128)S(1)}, f32[32,2,512]{2,1,0:T(2,128)S(1)}, u32[]{:S(2)}, u32[]{:S(2)}) %collective-permute-start.3) | collective-permute-done | bytes 131104 | tf_op jit(solution)/shard_map/ppermute | solution.py:248
  11.6 0.9 %collective-permute-start.4 = (f32[32,2,512]{2,1,0:T(2,128)S(1)}, f32[32,2,512]{2,1,0:T(2,128)S(1)}, u32[]{:S(2)}, u32[]{:S(2)}) collective-permute-start(f32[32,2,512]{2,1,0:T(2,128)S(1)} %collective-permute-done.3.near), channel_id=1, source_target_pairs={{0,2},{2,4},{4,6},{3,1},{5,3},{7,5},{6,7},{1,0},{8,10},{10,12},{12... | collective-permute-start | bytes 393224 | tf_op jit(solution)/shard_map/ppermute | solution.py:250
  12.5 2.5 %collective-permute-done.1.far.coef_far = f32[34,2,512]{2,1,0:T(2,128)S(1)} collective-permute-done((f32[34,2,512]{2,1,0:T(2,128)S(1)}, f32[34,2,512]{2,1,0:T(2,128)S(1)}, u32[]{:S(2)}, u32[]{:S(2)}) %collective-permute-start.1) | collective-permute-done | bytes 139296 | tf_op jit(solution)/shard_map/ppermute | solution.py:250
  15.1 0.5 %shard_map.73.refs_0_.refs_6_ = f32[32,1024]{1,0:T(8,128)S(1)} custom-call(f32[64,2,512]{2,1,0:T(2,128)S(1)} %copy-done, f32[2,512]{1,0:T(2,128)S(1)} %copy-done.1, f32[2,512]{1,0:T(2,128)S(1)} %copy-done.2, f32[34,2,512]{2,1,0:T(2,128)S(1)} %collective-permute-done.near.coef_near, f32[34,2,512]{2,1,0:T(2,128)S(1)} %collective-permute-done.1.far.coef_far, ...), custom_call_target="tpu_custom_call" | custom-call | flops 2000000 | bytes 2000000 | tf_op jit(solution)/shard_map/pallas_call | solution.py:266
  15.6 1.9 %collective-permute-start.6 = (f32[32,1024]{1,0:T(8,128)S(1)}, f32[32,1024]{1,0:T(8,128)S(1)}, u32[]{:S(2)}, u32[]{:S(2)}) collective-permute-start(f32[32,1024]{1,0:T(8,128)S(1)} %shard_map.73.refs_0_.refs_6_), channel_id=1, source_target_pairs={{0,16},{8,24},{16,0},{24,8},{1,17},{9,25},{17,1},{25,9},{2,18},{10... | collective-permute-start | bytes 393224 | tf_op jit(solution)/shard_map/ppermute | solution.py:274
  17.5 0.5 %shard_map.74.refs_2_.refs_8_ = f32[32,1024]{1,0:T(8,128)S(1)} custom-call(f32[64,2,512]{2,1,0:T(2,128)S(1)} %copy-done, f32[2,512]{1,0:T(2,128)S(1)} %copy-done.1, f32[2,512]{1,0:T(2,128)S(1)} %copy-done.2, f32[32,2,512]{2,1,0:T(2,128)S(1)} %collective-permute-done.3.near, f32[32,2,512]{2,1,0:T(2,128)S(1)} %collective-permute-done.4.far, ...), custom_call_target="tpu_custom_call" | custom-call | flops 2000000 | bytes 2000000 | tf_op jit(solution)/shard_map/pallas_call | solution.py:266
  18.1 1.0 %collective-permute-start.8 = (f32[32,1024]{1,0:T(8,128)S(1)}, f32[32,1024]{1,0:T(8,128)S(1)}, u32[]{:S(2)}, u32[]{:S(2)}) collective-permute-start(f32[32,1024]{1,0:T(8,128)S(1)} %shard_map.74.refs_2_.refs_8_), channel_id=1, source_target_pairs={{0,16},{8,24},{16,0},{24,8},{1,17},{9,25},{17,1},{25,9},{2,18},{10... | collective-permute-start | bytes 393224 | tf_op jit(solution)/shard_map/ppermute | solution.py:274
  19.1 0.5 %collective-permute-start.2 = (f32[32,1024]{1,0:T(8,128)S(1)}, f32[32,1024]{1,0:T(8,128)S(1)}, u32[]{:S(2)}, u32[]{:S(2)}) collective-permute-start(f32[32,1024]{1,0:T(8,128)S(1)} %shard_map.73.refs_0_.refs_6_), channel_id=1, source_target_pairs={{0,8},{8,0},{16,24},{24,16},{1,9},{9,1},{17,25},{25,17},{2,10},{10... | collective-permute-start | bytes 393224 | tf_op jit(solution)/shard_map/ppermute | solution.py:257
  19.6 1.8 %collective-permute-done.6.refs_4_.refs_10_ = f32[32,1024]{1,0:T(8,128)S(1)} collective-permute-done((f32[32,1024]{1,0:T(8,128)S(1)}, f32[32,1024]{1,0:T(8,128)S(1)}, u32[]{:S(2)}, u32[]{:S(2)}) %collective-permute-start.6) | collective-permute-done | bytes 131104 | tf_op jit(solution)/shard_map/ppermute | solution.py:274
  21.4 1.7 %collective-permute-done.8.refs_12_ = f32[32,1024]{1,0:T(8,128)S(1)} collective-permute-done((f32[32,1024]{1,0:T(8,128)S(1)}, f32[32,1024]{1,0:T(8,128)S(1)}, u32[]{:S(2)}, u32[]{:S(2)}) %collective-permute-start.8) | collective-permute-done | bytes 131104 | tf_op jit(solution)/shard_map/ppermute | solution.py:274
  23.1 1.4 %shard_map.75 = (f32[512,512]{1,0:T(8,128)S(1)}, f32[512,256]{1,0:T(8,128)S(1)}, f32[1,512]{1,0:T(1,128)S(1)}, f32[1,256]{1,0:T(1,128)S(1)}, f32[128,512]{1,0:T(8,128)S(1)}) custom-call(s32[4,4]{1,0:T(4,128)S(1)} %bitcast.15, s32[4,512]{1,0:T(4,128)S(1)} %bitcast.10, f32[32,1024]{1,0:T(8,128)S(1)} %shard_map.73.refs_0_.refs_6_, ...), custom_call_target="tpu_custom_call" | custom-call | flops 800000000 | bytes 3000000 | tf_op jit(solution)/shard_map/pallas_call | solution.py:279
  24.5 1.1 %shard_map.76 = (f32[512,512]{1,0:T(8,128)S(1)}, f32[512,256]{1,0:T(8,128)S(1)}, f32[1,512]{1,0:T(1,128)S(1)}, f32[1,256]{1,0:T(1,128)S(1)}, f32[64,512]{1,0:T(8,128)S(1)}) custom-call(s32[4,4]{1,0:T(4,128)S(1)} %bitcast.16, s32[4,512]{1,0:T(4,128)S(1)} %bitcast.11, f32[512,512]{1,0:T(8,128)S(1)} %get-tuple-element.19.refs_0_, ...), custom_call_target="tpu_custom_call" | custom-call | flops 800000000 | bytes 3000000 | tf_op jit(solution)/shard_map/pallas_call | solution.py:279
  25.6 5.5 %gain.1 = (f32[64,256]{1,0:T(8,128)S(1)}, f32[64,256]{1,0:T(8,128)S(1)}, f32[64,256]{1,0:T(8,128)S(1)}, f32[64,256]{1,0:T(8,128)S(1)}) custom-call(s32[4,4]{1,0:T(4,128)S(1)} %bitcast.17, s32[4,512]{1,0:T(4,128)S(1)} %bitcast.12, f32[1,512]{1,0:T(1,128)S(1)} %bitcast.20, f32[1,512]{1,0:T(1,128)S(1)} %bitcast.23, f32[512,512]{1,0:T(8,128)S(1)} %get-tuple-element.23.refs_0_, ...), custom_call_target="tpu_custom_call" | custom-call | flops 5000000000 | bytes 4000000 | tf_op jit(solution)/shard_map/gain/pallas_call | solution.py:306
  31.1 0.6 %collective-permute-start.10 = (f32[64,256]{1,0:T(8,128)S(1)}, f32[64,256]{1,0:T(8,128)S(1)}, u32[]{:S(2)}, u32[]{:S(2)}) collective-permute-start(f32[64,256]{1,0:T(8,128)S(1)} %get-tuple-element.30), channel_id=1, source_target_pairs={{0,8},{8,0},{16,24},{24,16},{1,9},{9,1},{17,25},{25,17},{2,10},{10... | collective-permute-start | bytes 196616 | tf_op jit(solution)/shard_map/ppermute | solution.py:321
  31.7 1.0 %collective-permute-start.11 = (f32[64,256]{1,0:T(8,128)S(1)}, f32[64,256]{1,0:T(8,128)S(1)}, u32[]{:S(2)}, u32[]{:S(2)}) collective-permute-start(f32[64,256]{1,0:T(8,128)S(1)} %get-tuple-element.31), channel_id=1, source_target_pairs={{0,16},{8,24},{16,0},{24,8},{1,17},{9,25},{17,1},{25,9},{2,18},{10... | collective-permute-start | bytes 196616 | tf_op jit(solution)/shard_map/ppermute | solution.py:321
  32.6 0.5 %collective-permute-start.12 = (f32[64,256]{1,0:T(8,128)S(1)}, f32[64,256]{1,0:T(8,128)S(1)}, u32[]{:S(2)}, u32[]{:S(2)}) collective-permute-start(f32[64,256]{1,0:T(8,128)S(1)} %get-tuple-element.32), channel_id=1, source_target_pairs={{0,24},{8,16},{16,8},{24,0},{1,25},{9,17},{17,9},{25,1},{2,26},{10... | collective-permute-start | bytes 196616 | tf_op jit(solution)/shard_map/ppermute | solution.py:321
  33.1 3.1 %collective-permute-done.11.refs_2_ = f32[64,256]{1,0:T(8,128)S(1)} collective-permute-done((f32[64,256]{1,0:T(8,128)S(1)}, f32[64,256]{1,0:T(8,128)S(1)}, u32[]{:S(2)}, u32[]{:S(2)}) %collective-permute-start.11) | collective-permute-done | bytes 65568 | tf_op jit(solution)/shard_map/ppermute | solution.py:321
  36.2 0.8 %collective-permute-done.12.refs_3_ = f32[64,256]{1,0:T(8,128)S(1)} collective-permute-done((f32[64,256]{1,0:T(8,128)S(1)}, f32[64,256]{1,0:T(8,128)S(1)}, u32[]{:S(2)}, u32[]{:S(2)}) %collective-permute-start.12) | collective-permute-done | bytes 65568 | tf_op jit(solution)/shard_map/ppermute | solution.py:321
  37.0 0.8 %place.1 = f32[64,2,512]{2,1,0:T(2,128)} custom-call(f32[64,256]{1,0:T(8,128)S(1)} %get-tuple-element.29.refs_0_, f32[64,256]{1,0:T(8,128)S(1)} %collective-permute-done.10.refs_1_, f32[64,256]{1,0:T(8,128)S(1)} %collective-permute-done.11.refs_2_, f32[64,256]{1,0:T(8,128)S(1)} %collective-permute-done.12.refs_3_), custom_call_target="tpu_custom_call" | custom-call | flops 100000 | bytes 600000 | tf_op jit(solution)/shard_map/place/pallas_call | solution.py:322
  (24 shorter events, 0.1 us)
Async XLA Ops:
  0.0 1.0 %copy-start.1 = (f32[2,512]{1,0:T(2,128)S(1)}, f32[2,512]{1,0:T(2,128)}, u32[]{:S(2)}) copy-start(f32[2,512]{1,0:T(2,128)} %dif.3) | copy-start | bytes 12292
  0.0 1.0 %copy-start.2 = (f32[2,512]{1,0:T(2,128)S(1)}, f32[2,512]{1,0:T(2,128)}, u32[]{:S(2)}) copy-start(f32[2,512]{1,0:T(2,128)} %wind.3) | copy-start | bytes 12292
  1.0 14.0 %copy-start = (f32[64,2,512]{2,1,0:T(2,128)S(1)}, f32[64,2,512]{2,1,0:T(2,128)}, u32[]{:S(2)}) copy-start(f32[64,2,512]{2,1,0:T(2,128)} %own.3) | copy-start | bytes 786436
  1.1 14.0 %copy-start.4 = (s32[1,4,4]{2,1,0:T(4,128)S(1)}, s32[1,4,4]{2,1,0:T(4,128)}, u32[]{:S(2)}) copy-start(s32[1,4,4]{2,1,0:T(4,128)} %param.10) | copy-start | bytes 196
  1.1 14.0 %copy-start.5 = (f32[1,1,512]{2,1,0:T(1,128)S(1)}, f32[1,1,512]{2,1,0:T(1,128)}, u32[]{:S(2)}) copy-start(f32[1,1,512]{2,1,0:T(1,128)} %param.12) | copy-start | bytes 6148
  1.1 14.0 %copy-start.6 = (f32[1,1,512]{2,1,0:T(1,128)S(1)}, f32[1,1,512]{2,1,0:T(1,128)}, u32[]{:S(2)}) copy-start(f32[1,1,512]{2,1,0:T(1,128)} %param.13) | copy-start | bytes 6148
  1.2 13.9 %copy-start.3 = (s32[1,4,512]{2,1,0:T(4,128)S(1)}, s32[1,4,512]{2,1,0:T(4,128)}, u32[]{:S(2)}) copy-start(s32[1,4,512]{2,1,0:T(4,128)} %param.11) | copy-start | bytes 24580
  1.2 7.6 %collective-permute-start = (f32[34,2,512]{2,1,0:T(2,128)S(1)}, f32[34,2,512]{2,1,0:T(2,128)S(1)}, u32[]{:S(2)}, u32[]{:S(2)}) collective-permute-start(f32[34,2,512]{2,1,0:T(2,128)S(1)} %pad_maximum_fusion), channel_id=1, source_target_pairs={{0,1},{1,0},{2,3},{3,2},{4,5},{5,4},{6,7},{7,6},{8,9},{9,8},{10,11... | collective-permute-start | bytes 417800 | tf_op jit(solution)/shard_map/ppermute | solution.py:248
  4.2 7.3 %collective-permute-start.3 = (f32[32,2,512]{2,1,0:T(2,128)S(1)}, f32[32,2,512]{2,1,0:T(2,128)S(1)}, u32[]{:S(2)}, u32[]{:S(2)}) collective-permute-start(f32[32,2,512]{2,1,0:T(2,128)S(1)} %get-tuple-element.33), channel_id=1, source_target_pairs={{0,1},{1,0},{2,3},{3,2},{4,5},{5,4},{6,7},{7,6},{8,9},{9,8},{10,11... | collective-permute-start | bytes 393224 | tf_op jit(solution)/shard_map/ppermute | solution.py:248
  8.8 6.3 %collective-permute-start.1 = (f32[34,2,512]{2,1,0:T(2,128)S(1)}, f32[34,2,512]{2,1,0:T(2,128)S(1)}, u32[]{:S(2)}, u32[]{:S(2)}) collective-permute-start(f32[34,2,512]{2,1,0:T(2,128)S(1)} %collective-permute-done.near.coef_near), channel_id=1, source_target_pairs={{0,2},{2,4},{4,6},{3,1},{5,3},{7,5},{6,7},{1,0},{8,10},{10,12},{12... | collective-permute-start | bytes 417800 | tf_op jit(solution)/shard_map/ppermute | solution.py:250
  11.6 6.0 %collective-permute-start.4 = (f32[32,2,512]{2,1,0:T(2,128)S(1)}, f32[32,2,512]{2,1,0:T(2,128)S(1)}, u32[]{:S(2)}, u32[]{:S(2)}) collective-permute-start(f32[32,2,512]{2,1,0:T(2,128)S(1)} %collective-permute-done.3.near), channel_id=1, source_target_pairs={{0,2},{2,4},{4,6},{3,1},{5,3},{7,5},{6,7},{1,0},{8,10},{10,12},{12... | collective-permute-start | bytes 393224 | tf_op jit(solution)/shard_map/ppermute | solution.py:250
  15.6 5.8 %collective-permute-start.6 = (f32[32,1024]{1,0:T(8,128)S(1)}, f32[32,1024]{1,0:T(8,128)S(1)}, u32[]{:S(2)}, u32[]{:S(2)}) collective-permute-start(f32[32,1024]{1,0:T(8,128)S(1)} %shard_map.73.refs_0_.refs_6_), channel_id=1, source_target_pairs={{0,16},{8,24},{16,0},{24,8},{1,17},{9,25},{17,1},{25,9},{2,18},{10... | collective-permute-start | bytes 393224 | tf_op jit(solution)/shard_map/ppermute | solution.py:274
  18.1 5.0 %collective-permute-start.8 = (f32[32,1024]{1,0:T(8,128)S(1)}, f32[32,1024]{1,0:T(8,128)S(1)}, u32[]{:S(2)}, u32[]{:S(2)}) collective-permute-start(f32[32,1024]{1,0:T(8,128)S(1)} %shard_map.74.refs_2_.refs_8_), channel_id=1, source_target_pairs={{0,16},{8,24},{16,0},{24,8},{1,17},{9,25},{17,1},{25,9},{2,18},{10... | collective-permute-start | bytes 393224 | tf_op jit(solution)/shard_map/ppermute | solution.py:274
  19.1 4.0 %collective-permute-start.5 = (f32[32,1024]{1,0:T(8,128)S(1)}, f32[32,1024]{1,0:T(8,128)S(1)}, u32[]{:S(2)}, u32[]{:S(2)}) collective-permute-start(f32[32,1024]{1,0:T(8,128)S(1)} %shard_map.74.refs_2_.refs_8_), channel_id=1, source_target_pairs={{0,8},{8,0},{16,24},{24,16},{1,9},{9,1},{17,25},{25,17},{2,10},{10... | collective-permute-start | bytes 393224 | tf_op jit(solution)/shard_map/ppermute | solution.py:257
  19.1 4.0 %collective-permute-start.2 = (f32[32,1024]{1,0:T(8,128)S(1)}, f32[32,1024]{1,0:T(8,128)S(1)}, u32[]{:S(2)}, u32[]{:S(2)}) collective-permute-start(f32[32,1024]{1,0:T(8,128)S(1)} %shard_map.73.refs_0_.refs_6_), channel_id=1, source_target_pairs={{0,8},{8,0},{16,24},{24,16},{1,9},{9,1},{17,25},{25,17},{2,10},{10... | collective-permute-start | bytes 393224 | tf_op jit(solution)/shard_map/ppermute | solution.py:257
  21.4 3.1 %collective-permute-start.7 = (f32[32,1024]{1,0:T(8,128)S(1)}, f32[32,1024]{1,0:T(8,128)S(1)}, u32[]{:S(2)}, u32[]{:S(2)}) collective-permute-start(f32[32,1024]{1,0:T(8,128)S(1)} %collective-permute-done.6.refs_4_.refs_10_), channel_id=1, source_target_pairs={{0,8},{8,0},{16,24},{24,16},{1,9},{9,1},{17,25},{25,17},{2,10},{10... | collective-permute-start | bytes 393224 | tf_op jit(solution)/shard_map/ppermute | solution.py:257
  23.1 2.5 %collective-permute-start.9 = (f32[32,1024]{1,0:T(8,128)S(1)}, f32[32,1024]{1,0:T(8,128)S(1)}, u32[]{:S(2)}, u32[]{:S(2)}) collective-permute-start(f32[32,1024]{1,0:T(8,128)S(1)} %collective-permute-done.8.refs_12_), channel_id=1, source_target_pairs={{0,8},{8,0},{16,24},{24,16},{1,9},{9,1},{17,25},{25,17},{2,10},{10... | collective-permute-start | bytes 393224 | tf_op jit(solution)/shard_map/ppermute | solution.py:257
  31.1 2.0 %collective-permute-start.10 = (f32[64,256]{1,0:T(8,128)S(1)}, f32[64,256]{1,0:T(8,128)S(1)}, u32[]{:S(2)}, u32[]{:S(2)}) collective-permute-start(f32[64,256]{1,0:T(8,128)S(1)} %get-tuple-element.30), channel_id=1, source_target_pairs={{0,8},{8,0},{16,24},{24,16},{1,9},{9,1},{17,25},{25,17},{2,10},{10... | collective-permute-start | bytes 196616 | tf_op jit(solution)/shard_map/ppermute | solution.py:321
  31.7 4.6 %collective-permute-start.11 = (f32[64,256]{1,0:T(8,128)S(1)}, f32[64,256]{1,0:T(8,128)S(1)}, u32[]{:S(2)}, u32[]{:S(2)}) collective-permute-start(f32[64,256]{1,0:T(8,128)S(1)} %get-tuple-element.31), channel_id=1, source_target_pairs={{0,16},{8,24},{16,0},{24,8},{1,17},{9,25},{17,1},{25,9},{2,18},{10... | collective-permute-start | bytes 196616 | tf_op jit(solution)/shard_map/ppermute | solution.py:321
  32.6 4.4 %collective-permute-start.12 = (f32[64,256]{1,0:T(8,128)S(1)}, f32[64,256]{1,0:T(8,128)S(1)}, u32[]{:S(2)}, u32[]{:S(2)}) collective-permute-start(f32[64,256]{1,0:T(8,128)S(1)} %get-tuple-element.32), channel_id=1, source_target_pairs={{0,24},{8,16},{16,8},{24,0},{1,25},{9,17},{17,9},{25,1},{2,26},{10... | collective-permute-start | bytes 196616 | tf_op jit(solution)/shard_map/ppermute | solution.py:321

commit v5 on v4

--- a/solution.py
+++ b/solution.py
@@ -160,31 +160,53 @@
         out[...] = value
 
 
+def square(x):
+    half = x[0].shape[0] // 2
+    first, second = slice(0, half), slice(half, 2 * half)
+
+    def block(rows, columns):
+        mul = functools.partial(jnp.dot, preferred_element_type=F32)
+        (high, low), (high_right, low_right) = [p[rows] for p in x], [p[:, columns] for p in x]
+        quarter = half // 2
+        out = []
+        for at in (0, quarter):
+            h, l = high[at : at + quarter], low[at : at + quarter]
+            both = mul(jnp.concatenate([h, l], axis=0), high_right)
+            out.append(both[:quarter] + (both[quarter:] + mul(h, low_right)))
+        return jnp.concatenate(out, axis=0)
+
+    corner = block(first, second)
+    above = jnp.concatenate([block(first, first), corner], axis=1)
+    below = jnp.concatenate([corner.T, block(second, second)], axis=1)
+    return jnp.concatenate([above, below], axis=0)
+
+
 def gain_kernel(earlier, last, order, longitudes, blocks, flags, values, errors, *refs):
     cov, outs = refs[-1], refs[-1 - (1 + max(j for j, _ in order)) : -1]
     before, first_seen, parts = refs[:4], refs[4 : 4 + earlier], refs[4 + earlier : 4 + earlier + len(order)]
     own_cells = outs[0].shape[1]
     total = sum(part.shape[0] for part in parts)
-    scale = 1.0 / (total - 1.0)
     last_seen, last_cells = observe(parts[-last:], longitudes, own_cells, blocks, flags)
-    square, cross, seen_mean, _ = moments(last_seen, last_cells, (before[2][...], before[3][...]), total)
-    cross = split((cross + before[1][...]) * scale)
-    cov[...] = (square + before[0][...]) * scale
+    square_sum, cross, seen_mean, _ = moments(last_seen, last_cells, (before[2][...], before[3][...]), total)
+    cov[...] = square_sum + before[0][...]
     tile = 128
     down = lax.broadcasted_iota(jnp.int32, (tile, tile), 0)
     across = lax.broadcasted_iota(jnp.int32, (tile, tile), 1)
     for at in range(0, cov.shape[0], tile):
         here = slice(at, at + tile)
-        cov[here, here] += jnp.where(down == across, errors[:, here], 0.0)
+        cov[here, here] += jnp.where(down == across, errors[:, here] * (total - 1.0), 0.0)
     covariance = cov[...]
-    inverse_scale = 1.0 / jnp.sum(jnp.abs(covariance), axis=0, keepdims=True)
+    size = jnp.abs(covariance)
+    root = lax.rsqrt(jnp.sum(size, axis=0, keepdims=True))
+    root_down = lax.rsqrt(jnp.sum(size, axis=1, keepdims=True))
+    cross = split((cross + before[1][...]) * root_down)
     seen = jnp.concatenate([ref[...] for ref in first_seen] + [last_seen], axis=0)
-    start = ((values[...] - seen_mean) - 0.5 * (seen - seen_mean)) * inverse_scale
-    b1 = covariance * inverse_scale
+    start = ((values[...] - seen_mean) - 0.5 * (seen - seen_mean)) * root
+    b1 = (covariance * root_down) * root
     s1 = split(b1)
-    b2 = 2.0 * b1 - dot3(s1, s1)
+    b2 = 2.0 * b1 - square(s1)
     s2 = split(b2)
-    b4 = 2.0 * b2 - dot3(s2, s2)
+    b4 = 2.0 * b2 - square(s2)
     s4 = split(b4)
     q = start + (start - dot1(start.astype(BF16), s4[0]))
     for _ in range(2):

time: 38 us -> 37.8 us (level)
  no operation moved by 1% of the time
where the time goes in v5:
time: 37.8 us; the launch traced here: 37.6 us
  waiting for transfers between devices  15.1 us (40%)
  starting transfers between devices  11.7 us (31%)
  Pallas kernels  9.62 us (25%)
  local copies, waits for them, and re-layouts  1.05 us (3%)
    pallas_call x1, Pallas kernels, body(): pl.pallas_call(functools.partial(gain_kernel, len(seen), len(stage), orde...  5.24 us
    ppermute x2, waiting for transfers between devices, body(): near.append(lax.ppermute(own, 'lat', near_pairs))  5.17 us
    ppermute x3, waiting for transfers between devices, body(): came[mask] = lax.ppermute(outs[masks.index(mask)], 'mem', pairs)  3.92 us
    ppermute x2, waiting for transfers between devices, body(): far_half.append(lax.ppermute(band, 'mem', xor_pairs(mems, top)))  3.47 us
    ppermute x2, starting transfers between devices, body(): near.append(lax.ppermute(own, 'lat', near_pairs))  3.14 us
    ppermute x2, starting transfers between devices, body(): far.append(lax.ppermute(near[k], 'lat', far_pairs))  3.02 us
    ppermute x2, starting transfers between devices, body(): far_half.append(lax.ppermute(band, 'mem', xor_pairs(mems, top)))  2.96 us
    ppermute x2, waiting for transfers between devices, body(): far.append(lax.ppermute(near[k], 'lat', far_pairs))  2.54 us
  transfers between devices with their start and end apart: 13, of which 7 were waited for; matrix products, arithmetic and copies ran while one was open for 0% of the time, Pallas kernels for 9%

profile of v5, /device:TPU:0, one launch (start us, length us, event | category | flops | bytes accessed | tf_op | source)
XLA Modules:
  0.0 37.6 jit_solution(3761957202604659494)
XLA Ops:
  0.0 1.0 %fusion = (f32[32,2,512]{2,1,0:T(2,128)S(1)}, f32[32,2,512]{2,1,0:T(2,128)S(1)}) fusion(f32[64,2,512]{2,1,0:T(2,128)} %own.3), kind=kLoop, calls=%fused_computation.1 | loop fusion | bytes 524288 | tf_op jit(solution)/shard_map/slice | solution.py:267
  1.2 3.1 %collective-permute-start = (f32[34,2,512]{2,1,0:T(2,128)S(1)}, f32[34,2,512]{2,1,0:T(2,128)S(1)}, u32[]{:S(2)}, u32[]{:S(2)}) collective-permute-start(f32[34,2,512]{2,1,0:T(2,128)S(1)} %pad_maximum_fusion), channel_id=1, source_target_pairs={{0,1},{1,0},{2,3},{3,2},{4,5},{5,4},{6,7},{7,6},{8,9},{9,8},{10,11... | collective-permute-start | bytes 417800 | tf_op jit(solution)/shard_map/ppermute | solution.py:270
  4.2 0.1 collective-permute-start.3
  4.3 4.4 %collective-permute-done.near.coef_near = f32[34,2,512]{2,1,0:T(2,128)S(1)} collective-permute-done((f32[34,2,512]{2,1,0:T(2,128)S(1)}, f32[34,2,512]{2,1,0:T(2,128)S(1)}, u32[]{:S(2)}, u32[]{:S(2)}) %collective-permute-start) | collective-permute-done | bytes 139296 | tf_op jit(solution)/shard_map/ppermute | solution.py:270
  8.8 2.1 %collective-permute-start.1 = (f32[34,2,512]{2,1,0:T(2,128)S(1)}, f32[34,2,512]{2,1,0:T(2,128)S(1)}, u32[]{:S(2)}, u32[]{:S(2)}) collective-permute-start(f32[34,2,512]{2,1,0:T(2,128)S(1)} %collective-permute-done.near.coef_near), channel_id=1, source_target_pairs={{0,2},{2,4},{4,6},{3,1},{5,3},{7,5},{6,7},{1,0},{8,10},{10,12},{12... | collective-permute-start | bytes 417800 | tf_op jit(solution)/shard_map/ppermute | solution.py:272
  10.8 0.7 %collective-permute-done.3.near = f32[32,2,512]{2,1,0:T(2,128)S(1)} collective-permute-done((f32[32,2,512]{2,1,0:T(2,128)S(1)}, f32[32,2,512]{2,1,0:T(2,128)S(1)}, u32[]{:S(2)}, u32[]{:S(2)}) %collective-permute-start.3) | collective-permute-done | bytes 131104 | tf_op jit(solution)/shard_map/ppermute | solution.py:270
  11.6 0.9 %collective-permute-start.4 = (f32[32,2,512]{2,1,0:T(2,128)S(1)}, f32[32,2,512]{2,1,0:T(2,128)S(1)}, u32[]{:S(2)}, u32[]{:S(2)}) collective-permute-start(f32[32,2,512]{2,1,0:T(2,128)S(1)} %collective-permute-done.3.near), channel_id=1, source_target_pairs={{0,2},{2,4},{4,6},{3,1},{5,3},{7,5},{6,7},{1,0},{8,10},{10,12},{12... | collective-permute-start | bytes 393224 | tf_op jit(solution)/shard_map/ppermute | solution.py:272
  12.5 2.5 %collective-permute-done.1.far.coef_far = f32[34,2,512]{2,1,0:T(2,128)S(1)} collective-permute-done((f32[34,2,512]{2,1,0:T(2,128)S(1)}, f32[34,2,512]{2,1,0:T(2,128)S(1)}, u32[]{:S(2)}, u32[]{:S(2)}) %collective-permute-start.1) | collective-permute-done | bytes 139296 | tf_op jit(solution)/shard_map/ppermute | solution.py:272
  15.1 0.5 %shard_map.73.refs_0_.refs_6_ = f32[32,1024]{1,0:T(8,128)S(1)} custom-call(f32[64,2,512]{2,1,0:T(2,128)S(1)} %copy-done, f32[2,512]{1,0:T(2,128)S(1)} %copy-done.1, f32[2,512]{1,0:T(2,128)S(1)} %copy-done.2, f32[34,2,512]{2,1,0:T(2,128)S(1)} %collective-permute-done.near.coef_near, f32[34,2,512]{2,1,0:T(2,128)S(1)} %collective-permute-done.1.far.coef_far, ...), custom_call_target="tpu_custom_call" | custom-call | flops 2000000 | bytes 2000000 | tf_op jit(solution)/shard_map/pallas_call | solution.py:288
  15.6 1.9 %collective-permute-start.6 = (f32[32,1024]{1,0:T(8,128)S(1)}, f32[32,1024]{1,0:T(8,128)S(1)}, u32[]{:S(2)}, u32[]{:S(2)}) collective-permute-start(f32[32,1024]{1,0:T(8,128)S(1)} %shard_map.73.refs_0_.refs_6_), channel_id=1, source_target_pairs={{0,16},{8,24},{16,0},{24,8},{1,17},{9,25},{17,1},{25,9},{2,18},{10... | collective-permute-start | bytes 393224 | tf_op jit(solution)/shard_map/ppermute | solution.py:296
  17.5 0.5 %shard_map.74.refs_2_.refs_8_ = f32[32,1024]{1,0:T(8,128)S(1)} custom-call(f32[64,2,512]{2,1,0:T(2,128)S(1)} %copy-done, f32[2,512]{1,0:T(2,128)S(1)} %copy-done.1, f32[2,512]{1,0:T(2,128)S(1)} %copy-done.2, f32[32,2,512]{2,1,0:T(2,128)S(1)} %collective-permute-done.3.near, f32[32,2,512]{2,1,0:T(2,128)S(1)} %collective-permute-done.4.far, ...), custom_call_target="tpu_custom_call" | custom-call | flops 2000000 | bytes 2000000 | tf_op jit(solution)/shard_map/pallas_call | solution.py:288
  18.1 1.0 %collective-permute-start.8 = (f32[32,1024]{1,0:T(8,128)S(1)}, f32[32,1024]{1,0:T(8,128)S(1)}, u32[]{:S(2)}, u32[]{:S(2)}) collective-permute-start(f32[32,1024]{1,0:T(8,128)S(1)} %shard_map.74.refs_2_.refs_8_), channel_id=1, source_target_pairs={{0,16},{8,24},{16,0},{24,8},{1,17},{9,25},{17,1},{25,9},{2,18},{10... | collective-permute-start | bytes 393224 | tf_op jit(solution)/shard_map/ppermute | solution.py:296
  19.1 0.5 %collective-permute-start.2 = (f32[32,1024]{1,0:T(8,128)S(1)}, f32[32,1024]{1,0:T(8,128)S(1)}, u32[]{:S(2)}, u32[]{:S(2)}) collective-permute-start(f32[32,1024]{1,0:T(8,128)S(1)} %shard_map.73.refs_0_.refs_6_), channel_id=1, source_target_pairs={{0,8},{8,0},{16,24},{24,16},{1,9},{9,1},{17,25},{25,17},{2,10},{10... | collective-permute-start | bytes 393224 | tf_op jit(solution)/shard_map/ppermute | solution.py:279
  19.6 1.8 %collective-permute-done.6.refs_4_.refs_10_ = f32[32,1024]{1,0:T(8,128)S(1)} collective-permute-done((f32[32,1024]{1,0:T(8,128)S(1)}, f32[32,1024]{1,0:T(8,128)S(1)}, u32[]{:S(2)}, u32[]{:S(2)}) %collective-permute-start.6) | collective-permute-done | bytes 131104 | tf_op jit(solution)/shard_map/ppermute | solution.py:296
  21.4 1.7 %collective-permute-done.8.refs_12_ = f32[32,1024]{1,0:T(8,128)S(1)} collective-permute-done((f32[32,1024]{1,0:T(8,128)S(1)}, f32[32,1024]{1,0:T(8,128)S(1)}, u32[]{:S(2)}, u32[]{:S(2)}) %collective-permute-start.8) | collective-permute-done | bytes 131104 | tf_op jit(solution)/shard_map/ppermute | solution.py:296
  23.1 1.4 %shard_map.75 = (f32[512,512]{1,0:T(8,128)S(1)}, f32[512,256]{1,0:T(8,128)S(1)}, f32[1,512]{1,0:T(1,128)S(1)}, f32[1,256]{1,0:T(1,128)S(1)}, f32[128,512]{1,0:T(8,128)S(1)}) custom-call(s32[4,4]{1,0:T(4,128)S(1)} %bitcast.15, s32[4,512]{1,0:T(4,128)S(1)} %bitcast.10, f32[32,1024]{1,0:T(8,128)S(1)} %shard_map.73.refs_0_.refs_6_, ...), custom_call_target="tpu_custom_call" | custom-call | flops 800000000 | bytes 3000000 | tf_op jit(solution)/shard_map/pallas_call | solution.py:301
  24.5 1.1 %shard_map.76 = (f32[512,512]{1,0:T(8,128)S(1)}, f32[512,256]{1,0:T(8,128)S(1)}, f32[1,512]{1,0:T(1,128)S(1)}, f32[1,256]{1,0:T(1,128)S(1)}, f32[64,512]{1,0:T(8,128)S(1)}) custom-call(s32[4,4]{1,0:T(4,128)S(1)} %bitcast.16, s32[4,512]{1,0:T(4,128)S(1)} %bitcast.11, f32[512,512]{1,0:T(8,128)S(1)} %get-tuple-element.19.refs_0_, ...), custom_call_target="tpu_custom_call" | custom-call | flops 800000000 | bytes 3000000 | tf_op jit(solution)/shard_map/pallas_call | solution.py:301
  25.6 5.2 %gain.1 = (f32[64,256]{1,0:T(8,128)S(1)}, f32[64,256]{1,0:T(8,128)S(1)}, f32[64,256]{1,0:T(8,128)S(1)}, f32[64,256]{1,0:T(8,128)S(1)}) custom-call(s32[4,4]{1,0:T(4,128)S(1)} %bitcast.17, s32[4,512]{1,0:T(4,128)S(1)} %bitcast.12, f32[1,512]{1,0:T(1,128)S(1)} %bitcast.20, f32[1,512]{1,0:T(1,128)S(1)} %bitcast.23, f32[512,512]{1,0:T(8,128)S(1)} %get-tuple-element.23.refs_0_, ...), custom_call_target="tpu_custom_call" | custom-call | flops 5000000000 | bytes 4000000 | tf_op jit(solution)/shard_map/gain/pallas_call | solution.py:328
  30.9 0.6 %collective-permute-start.10 = (f32[64,256]{1,0:T(8,128)S(1)}, f32[64,256]{1,0:T(8,128)S(1)}, u32[]{:S(2)}, u32[]{:S(2)}) collective-permute-start(f32[64,256]{1,0:T(8,128)S(1)} %get-tuple-element.30), channel_id=1, source_target_pairs={{0,8},{8,0},{16,24},{24,16},{1,9},{9,1},{17,25},{25,17},{2,10},{10... | collective-permute-start | bytes 196616 | tf_op jit(solution)/shard_map/ppermute | solution.py:343
  31.5 1.0 %collective-permute-start.11 = (f32[64,256]{1,0:T(8,128)S(1)}, f32[64,256]{1,0:T(8,128)S(1)}, u32[]{:S(2)}, u32[]{:S(2)}) collective-permute-start(f32[64,256]{1,0:T(8,128)S(1)} %get-tuple-element.31), channel_id=1, source_target_pairs={{0,16},{8,24},{16,0},{24,8},{1,17},{9,25},{17,1},{25,9},{2,18},{10... | collective-permute-start | bytes 196616 | tf_op jit(solution)/shard_map/ppermute | solution.py:343
  32.4 0.5 %collective-permute-start.12 = (f32[64,256]{1,0:T(8,128)S(1)}, f32[64,256]{1,0:T(8,128)S(1)}, u32[]{:S(2)}, u32[]{:S(2)}) collective-permute-start(f32[64,256]{1,0:T(8,128)S(1)} %get-tuple-element.32), channel_id=1, source_target_pairs={{0,24},{8,16},{16,8},{24,0},{1,25},{9,17},{17,9},{25,1},{2,26},{10... | collective-permute-start | bytes 196616 | tf_op jit(solution)/shard_map/ppermute | solution.py:343
  32.9 3.1 %collective-permute-done.11.refs_2_ = f32[64,256]{1,0:T(8,128)S(1)} collective-permute-done((f32[64,256]{1,0:T(8,128)S(1)}, f32[64,256]{1,0:T(8,128)S(1)}, u32[]{:S(2)}, u32[]{:S(2)}) %collective-permute-start.11) | collective-permute-done | bytes 65568 | tf_op jit(solution)/shard_map/ppermute | solution.py:343
  36.0 0.8 %collective-permute-done.12.refs_3_ = f32[64,256]{1,0:T(8,128)S(1)} collective-permute-done((f32[64,256]{1,0:T(8,128)S(1)}, f32[64,256]{1,0:T(8,128)S(1)}, u32[]{:S(2)}, u32[]{:S(2)}) %collective-permute-start.12) | collective-permute-done | bytes 65568 | tf_op jit(solution)/shard_map/ppermute | solution.py:343
  36.8 0.8 %place.1 = f32[64,2,512]{2,1,0:T(2,128)} custom-call(f32[64,256]{1,0:T(8,128)S(1)} %get-tuple-element.29.refs_0_, f32[64,256]{1,0:T(8,128)S(1)} %collective-permute-done.10.refs_1_, f32[64,256]{1,0:T(8,128)S(1)} %collective-permute-done.11.refs_2_, f32[64,256]{1,0:T(8,128)S(1)} %collective-permute-done.12.refs_3_), custom_call_target="tpu_custom_call" | custom-call | flops 100000 | bytes 600000 | tf_op jit(solution)/shard_map/place/pallas_call | solution.py:344
  (24 shorter events, 0.1 us)
Async XLA Ops:
  0.0 1.0 %copy-start.1 = (f32[2,512]{1,0:T(2,128)S(1)}, f32[2,512]{1,0:T(2,128)}, u32[]{:S(2)}) copy-start(f32[2,512]{1,0:T(2,128)} %dif.3) | copy-start | bytes 12292
  0.0 1.0 %copy-start.2 = (f32[2,512]{1,0:T(2,128)S(1)}, f32[2,512]{1,0:T(2,128)}, u32[]{:S(2)}) copy-start(f32[2,512]{1,0:T(2,128)} %wind.3) | copy-start | bytes 12292
  1.0 14.0 %copy-start = (f32[64,2,512]{2,1,0:T(2,128)S(1)}, f32[64,2,512]{2,1,0:T(2,128)}, u32[]{:S(2)}) copy-start(f32[64,2,512]{2,1,0:T(2,128)} %own.3) | copy-start | bytes 786436
  1.1 14.0 %copy-start.4 = (s32[1,4,4]{2,1,0:T(4,128)S(1)}, s32[1,4,4]{2,1,0:T(4,128)}, u32[]{:S(2)}) copy-start(s32[1,4,4]{2,1,0:T(4,128)} %param.10) | copy-start | bytes 196
  1.1 14.0 %copy-start.5 = (f32[1,1,512]{2,1,0:T(1,128)S(1)}, f32[1,1,512]{2,1,0:T(1,128)}, u32[]{:S(2)}) copy-start(f32[1,1,512]{2,1,0:T(1,128)} %param.12) | copy-start | bytes 6148
  1.1 14.0 %copy-start.6 = (f32[1,1,512]{2,1,0:T(1,128)S(1)}, f32[1,1,512]{2,1,0:T(1,128)}, u32[]{:S(2)}) copy-start(f32[1,1,512]{2,1,0:T(1,128)} %param.13) | copy-start | bytes 6148
  1.2 13.9 %copy-start.3 = (s32[1,4,512]{2,1,0:T(4,128)S(1)}, s32[1,4,512]{2,1,0:T(4,128)}, u32[]{:S(2)}) copy-start(s32[1,4,512]{2,1,0:T(4,128)} %param.11) | copy-start | bytes 24580
  1.2 7.6 %collective-permute-start = (f32[34,2,512]{2,1,0:T(2,128)S(1)}, f32[34,2,512]{2,1,0:T(2,128)S(1)}, u32[]{:S(2)}, u32[]{:S(2)}) collective-permute-start(f32[34,2,512]{2,1,0:T(2,128)S(1)} %pad_maximum_fusion), channel_id=1, source_target_pairs={{0,1},{1,0},{2,3},{3,2},{4,5},{5,4},{6,7},{7,6},{8,9},{9,8},{10,11... | collective-permute-start | bytes 417800 | tf_op jit(solution)/shard_map/ppermute | solution.py:270
  4.2 7.3 %collective-permute-start.3 = (f32[32,2,512]{2,1,0:T(2,128)S(1)}, f32[32,2,512]{2,1,0:T(2,128)S(1)}, u32[]{:S(2)}, u32[]{:S(2)}) collective-permute-start(f32[32,2,512]{2,1,0:T(2,128)S(1)} %get-tuple-element.33), channel_id=1, source_target_pairs={{0,1},{1,0},{2,3},{3,2},{4,5},{5,4},{6,7},{7,6},{8,9},{9,8},{10,11... | collective-permute-start | bytes 393224 | tf_op jit(solution)/shard_map/ppermute | solution.py:270
  8.8 6.3 %collective-permute-start.1 = (f32[34,2,512]{2,1,0:T(2,128)S(1)}, f32[34,2,512]{2,1,0:T(2,128)S(1)}, u32[]{:S(2)}, u32[]{:S(2)}) collective-permute-start(f32[34,2,512]{2,1,0:T(2,128)S(1)} %collective-permute-done.near.coef_near), channel_id=1, source_target_pairs={{0,2},{2,4},{4,6},{3,1},{5,3},{7,5},{6,7},{1,0},{8,10},{10,12},{12... | collective-permute-start | bytes 417800 | tf_op jit(solution)/shard_map/ppermute | solution.py:272
  11.6 6.0 %collective-permute-start.4 = (f32[32,2,512]{2,1,0:T(2,128)S(1)}, f32[32,2,512]{2,1,0:T(2,128)S(1)}, u32[]{:S(2)}, u32[]{:S(2)}) collective-permute-start(f32[32,2,512]{2,1,0:T(2,128)S(1)} %collective-permute-done.3.near), channel_id=1, source_target_pairs={{0,2},{2,4},{4,6},{3,1},{5,3},{7,5},{6,7},{1,0},{8,10},{10,12},{12... | collective-permute-start | bytes 393224 | tf_op jit(solution)/shard_map/ppermute | solution.py:272
  15.6 5.8 %collective-permute-start.6 = (f32[32,1024]{1,0:T(8,128)S(1)}, f32[32,1024]{1,0:T(8,128)S(1)}, u32[]{:S(2)}, u32[]{:S(2)}) collective-permute-start(f32[32,1024]{1,0:T(8,128)S(1)} %shard_map.73.refs_0_.refs_6_), channel_id=1, source_target_pairs={{0,16},{8,24},{16,0},{24,8},{1,17},{9,25},{17,1},{25,9},{2,18},{10... | collective-permute-start | bytes 393224 | tf_op jit(solution)/shard_map/ppermute | solution.py:296
  18.1 5.0 %collective-permute-start.8 = (f32[32,1024]{1,0:T(8,128)S(1)}, f32[32,1024]{1,0:T(8,128)S(1)}, u32[]{:S(2)}, u32[]{:S(2)}) collective-permute-start(f32[32,1024]{1,0:T(8,128)S(1)} %shard_map.74.refs_2_.refs_8_), channel_id=1, source_target_pairs={{0,16},{8,24},{16,0},{24,8},{1,17},{9,25},{17,1},{25,9},{2,18},{10... | collective-permute-start | bytes 393224 | tf_op jit(solution)/shard_map/ppermute | solution.py:296
  19.1 4.0 %collective-permute-start.5 = (f32[32,1024]{1,0:T(8,128)S(1)}, f32[32,1024]{1,0:T(8,128)S(1)}, u32[]{:S(2)}, u32[]{:S(2)}) collective-permute-start(f32[32,1024]{1,0:T(8,128)S(1)} %shard_map.74.refs_2_.refs_8_), channel_id=1, source_target_pairs={{0,8},{8,0},{16,24},{24,16},{1,9},{9,1},{17,25},{25,17},{2,10},{10... | collective-permute-start | bytes 393224 | tf_op jit(solution)/shard_map/ppermute | solution.py:279
  19.1 4.0 %collective-permute-start.2 = (f32[32,1024]{1,0:T(8,128)S(1)}, f32[32,1024]{1,0:T(8,128)S(1)}, u32[]{:S(2)}, u32[]{:S(2)}) collective-permute-start(f32[32,1024]{1,0:T(8,128)S(1)} %shard_map.73.refs_0_.refs_6_), channel_id=1, source_target_pairs={{0,8},{8,0},{16,24},{24,16},{1,9},{9,1},{17,25},{25,17},{2,10},{10... | collective-permute-start | bytes 393224 | tf_op jit(solution)/shard_map/ppermute | solution.py:279
  21.4 3.1 %collective-permute-start.7 = (f32[32,1024]{1,0:T(8,128)S(1)}, f32[32,1024]{1,0:T(8,128)S(1)}, u32[]{:S(2)}, u32[]{:S(2)}) collective-permute-start(f32[32,1024]{1,0:T(8,128)S(1)} %collective-permute-done.6.refs_4_.refs_10_), channel_id=1, source_target_pairs={{0,8},{8,0},{16,24},{24,16},{1,9},{9,1},{17,25},{25,17},{2,10},{10... | collective-permute-start | bytes 393224 | tf_op jit(solution)/shard_map/ppermute | solution.py:279
  23.1 2.5 %collective-permute-start.9 = (f32[32,1024]{1,0:T(8,128)S(1)}, f32[32,1024]{1,0:T(8,128)S(1)}, u32[]{:S(2)}, u32[]{:S(2)}) collective-permute-start(f32[32,1024]{1,0:T(8,128)S(1)} %collective-permute-done.8.refs_12_), channel_id=1, source_target_pairs={{0,8},{8,0},{16,24},{24,16},{1,9},{9,1},{17,25},{25,17},{2,10},{10... | collective-permute-start | bytes 393224 | tf_op jit(solution)/shard_map/ppermute | solution.py:279
  30.9 2.0 %collective-permute-start.10 = (f32[64,256]{1,0:T(8,128)S(1)}, f32[64,256]{1,0:T(8,128)S(1)}, u32[]{:S(2)}, u32[]{:S(2)}) collective-permute-start(f32[64,256]{1,0:T(8,128)S(1)} %get-tuple-element.30), channel_id=1, source_target_pairs={{0,8},{8,0},{16,24},{24,16},{1,9},{9,1},{17,25},{25,17},{2,10},{10... | collective-permute-start | bytes 196616 | tf_op jit(solution)/shard_map/ppermute | solution.py:343
  31.5 4.6 %collective-permute-start.11 = (f32[64,256]{1,0:T(8,128)S(1)}, f32[64,256]{1,0:T(8,128)S(1)}, u32[]{:S(2)}, u32[]{:S(2)}) collective-permute-start(f32[64,256]{1,0:T(8,128)S(1)} %get-tuple-element.31), channel_id=1, source_target_pairs={{0,16},{8,24},{16,0},{24,8},{1,17},{9,25},{17,1},{25,9},{2,18},{10... | collective-permute-start | bytes 196616 | tf_op jit(solution)/shard_map/ppermute | solution.py:343
  32.4 4.4 %collective-permute-start.12 = (f32[64,256]{1,0:T(8,128)S(1)}, f32[64,256]{1,0:T(8,128)S(1)}, u32[]{:S(2)}, u32[]{:S(2)}) collective-permute-start(f32[64,256]{1,0:T(8,128)S(1)} %get-tuple-element.32), channel_id=1, source_target_pairs={{0,24},{8,16},{16,8},{24,0},{1,25},{9,17},{17,9},{25,1},{2,26},{10... | collective-permute-start | bytes 196616 | tf_op jit(solution)/shard_map/ppermute | solution.py:343

commit v6 on v5

--- a/solution.py
+++ b/solution.py
@@ -181,10 +181,12 @@
     return jnp.concatenate([above, below], axis=0)
 
 
-def gain_kernel(earlier, last, order, longitudes, blocks, flags, values, errors, *refs):
-    cov, outs = refs[-1], refs[-1 - (1 + max(j for j, _ in order)) : -1]
+def gain_kernel(earlier, last, near_parts, order, longitudes, blocks, flags, values, errors, *refs):
+    cov, left = refs[-1], refs[-10:-1]
+    outs = refs[4 + earlier + len(order) : -10]
     before, first_seen, parts = refs[:4], refs[4 : 4 + earlier], refs[4 + earlier : 4 + earlier + len(order)]
     own_cells = outs[0].shape[1]
+    near_rows = left[0].shape[0]
     total = sum(part.shape[0] for part in parts)
     last_seen, last_cells = observe(parts[-last:], longitudes, own_cells, blocks, flags)
     square_sum, cross, seen_mean, _ = moments(last_seen, last_cells, (before[2][...], before[3][...]), total)
@@ -208,17 +210,29 @@
     s2 = split(b2)
     b4 = 2.0 * b2 - square(s2)
     s4 = split(b4)
+    for out, value in zip(left, (start[:near_rows],) + s4 + s2 + s1 + cross):
+        out[...] = value
+    finish(start[near_rows:], s4, (s2, s1), cross, parts[near_parts:], order[near_parts:], outs)
+
+
+def finish(start, s4, factors, cross, parts, order, outs):
     q = start + (start - dot1(start.astype(BF16), s4[0]))
     for _ in range(2):
         q = start + (q - dot3(split(q), s4))
-    q = 2.0 * q - dot3(split(q), s2)
-    q = 2.0 * q - dot3(split(q), s1)
+    for factor in factors:
+        q = 2.0 * q - dot3(split(q), factor)
     update = dot3(split(q), cross)
     at = 0
     for part, (j, row) in zip(parts, order):
         size = part.shape[0]
-        outs[j][row : row + size, :] = own([part], own_cells) + update[at : at + size, :]
+        outs[j][row : row + size, :] = own([part], outs[j].shape[1]) + update[at : at + size, :]
         at += size
+
+
+def finish_kernel(order, start, *refs):
+    s4, s2, s1, cross = [(refs[i][...], refs[i + 1][...]) for i in (0, 2, 4, 6)]
+    parts, outs = refs[8 : 8 + len(order)], refs[8 + len(order) :]
+    finish(start[...], s4, (s2, s1), cross, parts, order, outs)
 
 
 def place_kernel(masks, longitudes, *refs):
@@ -325,18 +339,39 @@
             seen.append(stage_seen)
         flat = flat + stage
         order = order + [(j, firsts[k]) for j in range(mems // 2, mems)]
-    outs = pl.pallas_call(
+    near_parts = pieces * (mems // 2)
+    near_order, far_order = order[:near_parts], [(j - mems // 2, row) for j, row in order[near_parts:]]
+    to_member = jax.ShapeDtypeStruct((local, own_cells), F32)
+    far_mems = mems - mems // 2
+    part_of_product = [jax.ShapeDtypeStruct((observations, observations), BF16)] * 2
+    part_of_cross = [jax.ShapeDtypeStruct((observations, own_cells), BF16)] * 2
+    near_rows = local * (mems // 2)
+    done = pl.pallas_call(
         functools.partial(
-            gain_kernel, len(seen), len(stage), order, longitudes
+            gain_kernel, len(seen), len(stage), near_parts, near_order + far_order, longitudes
         ),
-        out_shape=[jax.ShapeDtypeStruct((local, own_cells), F32) for _ in masks],
+        out_shape=[to_member] * far_mems
+        + [jax.ShapeDtypeStruct((near_rows, observations), F32)]
+        + part_of_product * 3
+        + part_of_cross,
         in_specs=[SMEM] + [VMEM] * (3 + len(before) + len(seen) + len(flat)),
-        out_specs=[VMEM] * mems,
+        out_specs=[VMEM] * (far_mems + 9),
         scratch_shapes=[pltpu.VMEM((observations, observations), F32)],
         cost_estimate=pl.CostEstimate(flops=5000000000, bytes_accessed=4000000, transcendentals=0),
         compiler_params=pltpu.CompilerParams(vmem_limit_bytes=24 << 20),
         name="gain",
     )(*tables, *before, *seen, *flat)
+    far_outs = done[:far_mems]
+    near_outs = pl.pallas_call(
+        functools.partial(finish_kernel, near_order),
+        out_shape=[to_member] * (mems // 2),
+        in_specs=[VMEM] * (9 + near_parts),
+        out_specs=[VMEM] * (mems // 2),
+        cost_estimate=pl.CostEstimate(flops=600000000, bytes_accessed=2000000, transcendentals=0),
+        compiler_params=pltpu.CompilerParams(vmem_limit_bytes=16 << 20),
+        name="finish",
+    )(*done[far_mems:], *flat[:near_parts])
+    outs = list(near_outs) + list(far_outs)
     came = {0: outs[0]}
     for mask in sorted(masks[1:], reverse=True):
         pairs = [(i, i ^ mask) for i in range(mems)]

time: 37.8 us -> 38.7 us (1.024)
  Pallas kernels: 9.62 us -> 10.6 us
    pallas_call x1 -> x2, Pallas kernels: 5.24 us -> 6.21 us  [the longest x1 4.45 us: body(): pl.pallas_call(functools.partial(gain_kernel, len(seen), len(stage), near...]
where the time goes in v6:
time: 38.7 us; the launch traced here: 38.6 us
  waiting for transfers between devices  15.1 us (39%)
  starting transfers between devices  11.6 us (30%)
  Pallas kernels  10.6 us (27%)
  local copies, waits for them, and re-layouts  1.05 us (3%)
    ppermute x2, waiting for transfers between devices, body(): near.append(lax.ppermute(own, 'lat', near_pairs))  5.17 us
    pallas_call x1, Pallas kernels, body(): pl.pallas_call(functools.partial(gain_kernel, len(seen), len(stage), near...  4.45 us
    ppermute x3, waiting for transfers between devices, body(): came[mask] = lax.ppermute(outs[masks.index(mask)], 'mem', pairs)  3.94 us
    ppermute x2, waiting for transfers between devices, body(): far_half.append(lax.ppermute(band, 'mem', xor_pairs(mems, top)))  3.47 us
    ppermute x2, starting transfers between devices, body(): near.append(lax.ppermute(own, 'lat', near_pairs))  3.14 us
    ppermute x2, starting transfers between devices, body(): far.append(lax.ppermute(near[k], 'lat', far_pairs))  3.02 us
    ppermute x2, starting transfers between devices, body(): far_half.append(lax.ppermute(band, 'mem', xor_pairs(mems, top)))  2.96 us
    ppermute x2, waiting for transfers between devices, body(): far.append(lax.ppermute(near[k], 'lat', far_pairs))  2.54 us
  transfers between devices with their start and end apart: 13, of which 7 were waited for; matrix products, arithmetic and copies ran while one was open for 0% of the time, Pallas kernels for 9%

profile of v6, /device:TPU:0, one launch (start us, length us, event | category | flops | bytes accessed | tf_op | source)
XLA Modules:
  0.0 38.6 jit_solution(8814902352525587741)
XLA Ops:
  0.0 1.0 %fusion = (f32[32,2,512]{2,1,0:T(2,128)S(1)}, f32[32,2,512]{2,1,0:T(2,128)S(1)}) fusion(f32[64,2,512]{2,1,0:T(2,128)} %own.3), kind=kLoop, calls=%fused_computation.1 | loop fusion | bytes 524288 | tf_op jit(solution)/shard_map/slice | solution.py:281
  1.2 3.1 %collective-permute-start = (f32[34,2,512]{2,1,0:T(2,128)S(1)}, f32[34,2,512]{2,1,0:T(2,128)S(1)}, u32[]{:S(2)}, u32[]{:S(2)}) collective-permute-start(f32[34,2,512]{2,1,0:T(2,128)S(1)} %pad_maximum_fusion), channel_id=1, source_target_pairs={{0,1},{1,0},{2,3},{3,2},{4,5},{5,4},{6,7},{7,6},{8,9},{9,8},{10,11... | collective-permute-start | bytes 417800 | tf_op jit(solution)/shard_map/ppermute | solution.py:284
  4.3 4.4 %collective-permute-done.near.coef_near = f32[34,2,512]{2,1,0:T(2,128)S(1)} collective-permute-done((f32[34,2,512]{2,1,0:T(2,128)S(1)}, f32[34,2,512]{2,1,0:T(2,128)S(1)}, u32[]{:S(2)}, u32[]{:S(2)}) %collective-permute-start) | collective-permute-done | bytes 139296 | tf_op jit(solution)/shard_map/ppermute | solution.py:284
  8.8 2.1 %collective-permute-start.1 = (f32[34,2,512]{2,1,0:T(2,128)S(1)}, f32[34,2,512]{2,1,0:T(2,128)S(1)}, u32[]{:S(2)}, u32[]{:S(2)}) collective-permute-start(f32[34,2,512]{2,1,0:T(2,128)S(1)} %collective-permute-done.near.coef_near), channel_id=1, source_target_pairs={{0,2},{2,4},{4,6},{3,1},{5,3},{7,5},{6,7},{1,0},{8,10},{10,12},{12... | collective-permute-start | bytes 417800 | tf_op jit(solution)/shard_map/ppermute | solution.py:286
  10.8 0.7 %collective-permute-done.3.near = f32[32,2,512]{2,1,0:T(2,128)S(1)} collective-permute-done((f32[32,2,512]{2,1,0:T(2,128)S(1)}, f32[32,2,512]{2,1,0:T(2,128)S(1)}, u32[]{:S(2)}, u32[]{:S(2)}) %collective-permute-start.3) | collective-permute-done | bytes 131104 | tf_op jit(solution)/shard_map/ppermute | solution.py:284
  11.6 0.9 %collective-permute-start.4 = (f32[32,2,512]{2,1,0:T(2,128)S(1)}, f32[32,2,512]{2,1,0:T(2,128)S(1)}, u32[]{:S(2)}, u32[]{:S(2)}) collective-permute-start(f32[32,2,512]{2,1,0:T(2,128)S(1)} %collective-permute-done.3.near), channel_id=1, source_target_pairs={{0,2},{2,4},{4,6},{3,1},{5,3},{7,5},{6,7},{1,0},{8,10},{10,12},{12... | collective-permute-start | bytes 393224 | tf_op jit(solution)/shard_map/ppermute | solution.py:286
  12.5 2.5 %collective-permute-done.1.far.coef_far = f32[34,2,512]{2,1,0:T(2,128)S(1)} collective-permute-done((f32[34,2,512]{2,1,0:T(2,128)S(1)}, f32[34,2,512]{2,1,0:T(2,128)S(1)}, u32[]{:S(2)}, u32[]{:S(2)}) %collective-permute-start.1) | collective-permute-done | bytes 139296 | tf_op jit(solution)/shard_map/ppermute | solution.py:286
  15.1 0.5 %shard_map.73.refs_0_.refs_6_.refs_8_ = f32[32,1024]{1,0:T(8,128)S(1)} custom-call(f32[64,2,512]{2,1,0:T(2,128)S(1)} %copy-done, f32[2,512]{1,0:T(2,128)S(1)} %copy-done.1, f32[2,512]{1,0:T(2,128)S(1)} %copy-done.2, f32[34,2,512]{2,1,0:T(2,128)S(1)} %collective-permute-done.near.coef_near, f32[34,2,512]{2,1,0:T(2,128)S(1)} %collective-permute-done.1.far.coef_far, ...), custom_call_target="tpu_custom_call" | custom-call | flops 2000000 | bytes 2000000 | tf_op jit(solution)/shard_map/pallas_call | solution.py:302
  15.6 1.9 %collective-permute-start.6 = (f32[32,1024]{1,0:T(8,128)S(1)}, f32[32,1024]{1,0:T(8,128)S(1)}, u32[]{:S(2)}, u32[]{:S(2)}) collective-permute-start(f32[32,1024]{1,0:T(8,128)S(1)} %shard_map.73.refs_0_.refs_6_.refs_8_), channel_id=1, source_target_pairs={{0,16},{8,24},{16,0},{24,8},{1,17},{9,25},{17,1},{25,9},{2,18},{10... | collective-permute-start | bytes 393224 | tf_op jit(solution)/shard_map/ppermute | solution.py:310
  17.5 0.5 %shard_map.74.refs_2_.refs_8_.refs_10_ = f32[32,1024]{1,0:T(8,128)S(1)} custom-call(f32[64,2,512]{2,1,0:T(2,128)S(1)} %copy-done, f32[2,512]{1,0:T(2,128)S(1)} %copy-done.1, f32[2,512]{1,0:T(2,128)S(1)} %copy-done.2, f32[32,2,512]{2,1,0:T(2,128)S(1)} %collective-permute-done.3.near, f32[32,2,512]{2,1,0:T(2,128)S(1)} %collective-permute-done.4.far, ...), custom_call_target="tpu_custom_call" | custom-call | flops 2000000 | bytes 2000000 | tf_op jit(solution)/shard_map/pallas_call | solution.py:302
  18.1 1.0 %collective-permute-start.8 = (f32[32,1024]{1,0:T(8,128)S(1)}, f32[32,1024]{1,0:T(8,128)S(1)}, u32[]{:S(2)}, u32[]{:S(2)}) collective-permute-start(f32[32,1024]{1,0:T(8,128)S(1)} %shard_map.74.refs_2_.refs_8_.refs_10_), channel_id=1, source_target_pairs={{0,16},{8,24},{16,0},{24,8},{1,17},{9,25},{17,1},{25,9},{2,18},{10... | collective-permute-start | bytes 393224 | tf_op jit(solution)/shard_map/ppermute | solution.py:310
  19.1 0.5 %collective-permute-start.5 = (f32[32,1024]{1,0:T(8,128)S(1)}, f32[32,1024]{1,0:T(8,128)S(1)}, u32[]{:S(2)}, u32[]{:S(2)}) collective-permute-start(f32[32,1024]{1,0:T(8,128)S(1)} %shard_map.74.refs_2_.refs_8_.refs_10_), channel_id=1, source_target_pairs={{0,8},{8,0},{16,24},{24,16},{1,9},{9,1},{17,25},{25,17},{2,10},{10... | collective-permute-start | bytes 393224 | tf_op jit(solution)/shard_map/ppermute | solution.py:293
  19.6 1.8 %collective-permute-done.6.refs_4_.refs_10_ = f32[32,1024]{1,0:T(8,128)S(1)} collective-permute-done((f32[32,1024]{1,0:T(8,128)S(1)}, f32[32,1024]{1,0:T(8,128)S(1)}, u32[]{:S(2)}, u32[]{:S(2)}) %collective-permute-start.6) | collective-permute-done | bytes 131104 | tf_op jit(solution)/shard_map/ppermute | solution.py:310
  21.4 1.7 %collective-permute-done.8.refs_12_ = f32[32,1024]{1,0:T(8,128)S(1)} collective-permute-done((f32[32,1024]{1,0:T(8,128)S(1)}, f32[32,1024]{1,0:T(8,128)S(1)}, u32[]{:S(2)}, u32[]{:S(2)}) %collective-permute-start.8) | collective-permute-done | bytes 131104 | tf_op jit(solution)/shard_map/ppermute | solution.py:310
  23.1 1.4 %shard_map.75 = (f32[512,512]{1,0:T(8,128)S(1)}, f32[512,256]{1,0:T(8,128)S(1)}, f32[1,512]{1,0:T(1,128)S(1)}, f32[1,256]{1,0:T(1,128)S(1)}, f32[128,512]{1,0:T(8,128)S(1)}) custom-call(s32[4,4]{1,0:T(4,128)S(1)} %bitcast.15, s32[4,512]{1,0:T(4,128)S(1)} %bitcast.10, f32[32,1024]{1,0:T(8,128)S(1)} %shard_map.73.refs_0_.refs_6_.refs_8_, ...), custom_call_target="tpu_custom_call" | custom-call | flops 800000000 | bytes 3000000 | tf_op jit(solution)/shard_map/pallas_call | solution.py:315
  24.5 1.1 %shard_map.76 = (f32[512,512]{1,0:T(8,128)S(1)}, f32[512,256]{1,0:T(8,128)S(1)}, f32[1,512]{1,0:T(1,128)S(1)}, f32[1,256]{1,0:T(1,128)S(1)}, f32[64,512]{1,0:T(8,128)S(1)}) custom-call(s32[4,4]{1,0:T(4,128)S(1)} %bitcast.16, s32[4,512]{1,0:T(4,128)S(1)} %bitcast.11, f32[512,512]{1,0:T(8,128)S(1)} %get-tuple-element.28.refs_0_, ...), custom_call_target="tpu_custom_call" | custom-call | flops 800000000 | bytes 3000000 | tf_op jit(solution)/shard_map/pallas_call | solution.py:315
  25.6 4.4 %gain.1 = (f32[64,256]{1,0:T(8,128)S(1)}, f32[64,256]{1,0:T(8,128)S(1)}, f32[128,512]{1,0:T(8,128)S(1)}, bf16[512,512]{1,0:T(8,128)(2,1)S(1)}, bf16[512,512]{1,0...) custom-call(s32[4,4]{1,0:T(4,128)S(1)} %bitcast.17, ...), custom_call_target="tpu_custom_call" | custom-call | flops 5000000000 | bytes 4000000 | tf_op jit(solution)/shard_map/gain/pallas_call | solution.py:349
  30.1 1.8 %finish.1 = (f32[64,256]{1,0:T(8,128)S(1)}, f32[64,256]{1,0:T(8,128)S(1)}) custom-call(f32[128,512]{1,0:T(8,128)S(1)} %get-tuple-element.38.start, bf16[512,512]{1,0:T(8,128)(2,1)S(1)} %get-tuple-element.39.refs_0_, bf16[512,512]{1,0:T(8,128)(2,1)S(1)} %get-tuple-element.40.refs_1_, bf16[512,512]{1,0:T(8,128)(2,1)S(1)} %get-tuple-element.41.refs_2_, ...), custom_call_target="tpu_custom_call" | custom-call | flops 600000000 | bytes 2000000 | tf_op jit(solution)/shard_map/finish/pallas_call | solution.py:365
  31.8 0.6 %collective-permute-start.10 = (f32[64,256]{1,0:T(8,128)S(1)}, f32[64,256]{1,0:T(8,128)S(1)}, u32[]{:S(2)}, u32[]{:S(2)}) collective-permute-start(f32[64,256]{1,0:T(8,128)S(1)} %get-tuple-element.48), channel_id=1, source_target_pairs={{0,8},{8,0},{16,24},{24,16},{1,9},{9,1},{17,25},{25,17},{2,10},{10... | collective-permute-start | bytes 196616 | tf_op jit(solution)/shard_map/ppermute | solution.py:378
  32.4 1.0 %collective-permute-start.11 = (f32[64,256]{1,0:T(8,128)S(1)}, f32[64,256]{1,0:T(8,128)S(1)}, u32[]{:S(2)}, u32[]{:S(2)}) collective-permute-start(f32[64,256]{1,0:T(8,128)S(1)} %get-tuple-element.49), channel_id=1, source_target_pairs={{0,16},{8,24},{16,0},{24,8},{1,17},{9,25},{17,1},{25,9},{2,18},{10... | collective-permute-start | bytes 196616 | tf_op jit(solution)/shard_map/ppermute | solution.py:378
  33.4 0.4 %collective-permute-start.12 = (f32[64,256]{1,0:T(8,128)S(1)}, f32[64,256]{1,0:T(8,128)S(1)}, u32[]{:S(2)}, u32[]{:S(2)}) collective-permute-start(f32[64,256]{1,0:T(8,128)S(1)} %get-tuple-element.50), channel_id=1, source_target_pairs={{0,24},{8,16},{16,8},{24,0},{1,25},{9,17},{17,9},{25,1},{2,26},{10... | collective-permute-start | bytes 196616 | tf_op jit(solution)/shard_map/ppermute | solution.py:378
  33.8 3.1 %collective-permute-done.11.refs_2_ = f32[64,256]{1,0:T(8,128)S(1)} collective-permute-done((f32[64,256]{1,0:T(8,128)S(1)}, f32[64,256]{1,0:T(8,128)S(1)}, u32[]{:S(2)}, u32[]{:S(2)}) %collective-permute-start.11) | collective-permute-done | bytes 65568 | tf_op jit(solution)/shard_map/ppermute | solution.py:378
  37.0 0.8 %collective-permute-done.12.refs_3_ = f32[64,256]{1,0:T(8,128)S(1)} collective-permute-done((f32[64,256]{1,0:T(8,128)S(1)}, f32[64,256]{1,0:T(8,128)S(1)}, u32[]{:S(2)}, u32[]{:S(2)}) %collective-permute-start.12) | collective-permute-done | bytes 65568 | tf_op jit(solution)/shard_map/ppermute | solution.py:378
  37.8 0.8 %place.1 = f32[64,2,512]{2,1,0:T(2,128)} custom-call(f32[64,256]{1,0:T(8,128)S(1)} %get-tuple-element.47.refs_0_, f32[64,256]{1,0:T(8,128)S(1)} %collective-permute-done.10.refs_1_, f32[64,256]{1,0:T(8,128)S(1)} %collective-permute-done.11.refs_2_, f32[64,256]{1,0:T(8,128)S(1)} %collective-permute-done.12.refs_3_), custom_call_target="tpu_custom_call" | custom-call | flops 100000 | bytes 600000 | tf_op jit(solution)/shard_map/place/pallas_call | solution.py:379
  (25 shorter events, 0.2 us)
Async XLA Ops:
  0.0 1.0 %copy-start.1 = (f32[2,512]{1,0:T(2,128)S(1)}, f32[2,512]{1,0:T(2,128)}, u32[]{:S(2)}) copy-start(f32[2,512]{1,0:T(2,128)} %dif.3) | copy-start | bytes 12292
  0.0 1.0 %copy-start.2 = (f32[2,512]{1,0:T(2,128)S(1)}, f32[2,512]{1,0:T(2,128)}, u32[]{:S(2)}) copy-start(f32[2,512]{1,0:T(2,128)} %wind.3) | copy-start | bytes 12292
  1.0 14.0 %copy-start = (f32[64,2,512]{2,1,0:T(2,128)S(1)}, f32[64,2,512]{2,1,0:T(2,128)}, u32[]{:S(2)}) copy-start(f32[64,2,512]{2,1,0:T(2,128)} %own.3) | copy-start | bytes 786436
  1.1 14.0 %copy-start.4 = (s32[1,4,4]{2,1,0:T(4,128)S(1)}, s32[1,4,4]{2,1,0:T(4,128)}, u32[]{:S(2)}) copy-start(s32[1,4,4]{2,1,0:T(4,128)} %param.10) | copy-start | bytes 196
  1.1 14.0 %copy-start.5 = (f32[1,1,512]{2,1,0:T(1,128)S(1)}, f32[1,1,512]{2,1,0:T(1,128)}, u32[]{:S(2)}) copy-start(f32[1,1,512]{2,1,0:T(1,128)} %param.12) | copy-start | bytes 6148
  1.1 14.0 %copy-start.6 = (f32[1,1,512]{2,1,0:T(1,128)S(1)}, f32[1,1,512]{2,1,0:T(1,128)}, u32[]{:S(2)}) copy-start(f32[1,1,512]{2,1,0:T(1,128)} %param.13) | copy-start | bytes 6148
  1.2 13.9 %copy-start.3 = (s32[1,4,512]{2,1,0:T(4,128)S(1)}, s32[1,4,512]{2,1,0:T(4,128)}, u32[]{:S(2)}) copy-start(s32[1,4,512]{2,1,0:T(4,128)} %param.11) | copy-start | bytes 24580
  1.2 7.6 %collective-permute-start = (f32[34,2,512]{2,1,0:T(2,128)S(1)}, f32[34,2,512]{2,1,0:T(2,128)S(1)}, u32[]{:S(2)}, u32[]{:S(2)}) collective-permute-start(f32[34,2,512]{2,1,0:T(2,128)S(1)} %pad_maximum_fusion), channel_id=1, source_target_pairs={{0,1},{1,0},{2,3},{3,2},{4,5},{5,4},{6,7},{7,6},{8,9},{9,8},{10,11... | collective-permute-start | bytes 417800 | tf_op jit(solution)/shard_map/ppermute | solution.py:284
  4.2 7.3 %collective-permute-start.3 = (f32[32,2,512]{2,1,0:T(2,128)S(1)}, f32[32,2,512]{2,1,0:T(2,128)S(1)}, u32[]{:S(2)}, u32[]{:S(2)}) collective-permute-start(f32[32,2,512]{2,1,0:T(2,128)S(1)} %get-tuple-element.51), channel_id=1, source_target_pairs={{0,1},{1,0},{2,3},{3,2},{4,5},{5,4},{6,7},{7,6},{8,9},{9,8},{10,11... | collective-permute-start | bytes 393224 | tf_op jit(solution)/shard_map/ppermute | solution.py:284
  8.8 6.3 %collective-permute-start.1 = (f32[34,2,512]{2,1,0:T(2,128)S(1)}, f32[34,2,512]{2,1,0:T(2,128)S(1)}, u32[]{:S(2)}, u32[]{:S(2)}) collective-permute-start(f32[34,2,512]{2,1,0:T(2,128)S(1)} %collective-permute-done.near.coef_near), channel_id=1, source_target_pairs={{0,2},{2,4},{4,6},{3,1},{5,3},{7,5},{6,7},{1,0},{8,10},{10,12},{12... | collective-permute-start | bytes 417800 | tf_op jit(solution)/shard_map/ppermute | solution.py:286
  11.6 6.0 %collective-permute-start.4 = (f32[32,2,512]{2,1,0:T(2,128)S(1)}, f32[32,2,512]{2,1,0:T(2,128)S(1)}, u32[]{:S(2)}, u32[]{:S(2)}) collective-permute-start(f32[32,2,512]{2,1,0:T(2,128)S(1)} %collective-permute-done.3.near), channel_id=1, source_target_pairs={{0,2},{2,4},{4,6},{3,1},{5,3},{7,5},{6,7},{1,0},{8,10},{10,12},{12... | collective-permute-start | bytes 393224 | tf_op jit(solution)/shard_map/ppermute | solution.py:286
  15.6 5.8 %collective-permute-start.6 = (f32[32,1024]{1,0:T(8,128)S(1)}, f32[32,1024]{1,0:T(8,128)S(1)}, u32[]{:S(2)}, u32[]{:S(2)}) collective-permute-start(f32[32,1024]{1,0:T(8,128)S(1)} %shard_map.73.refs_0_.refs_6_.refs_8_), channel_id=1, source_target_pairs={{0,16},{8,24},{16,0},{24,8},{1,17},{9,25},{17,1},{25,9},{2,18},{10... | collective-permute-start | bytes 393224 | tf_op jit(solution)/shard_map/ppermute | solution.py:310
  18.1 5.0 %collective-permute-start.8 = (f32[32,1024]{1,0:T(8,128)S(1)}, f32[32,1024]{1,0:T(8,128)S(1)}, u32[]{:S(2)}, u32[]{:S(2)}) collective-permute-start(f32[32,1024]{1,0:T(8,128)S(1)} %shard_map.74.refs_2_.refs_8_.refs_10_), channel_id=1, source_target_pairs={{0,16},{8,24},{16,0},{24,8},{1,17},{9,25},{17,1},{25,9},{2,18},{10... | collective-permute-start | bytes 393224 | tf_op jit(solution)/shard_map/ppermute | solution.py:310
  19.1 4.0 %collective-permute-start.2 = (f32[32,1024]{1,0:T(8,128)S(1)}, f32[32,1024]{1,0:T(8,128)S(1)}, u32[]{:S(2)}, u32[]{:S(2)}) collective-permute-start(f32[32,1024]{1,0:T(8,128)S(1)} %shard_map.73.refs_0_.refs_6_.refs_8_), channel_id=1, source_target_pairs={{0,8},{8,0},{16,24},{24,16},{1,9},{9,1},{17,25},{25,17},{2,10},{10... | collective-permute-start | bytes 393224 | tf_op jit(solution)/shard_map/ppermute | solution.py:293
  19.1 4.0 %collective-permute-start.5 = (f32[32,1024]{1,0:T(8,128)S(1)}, f32[32,1024]{1,0:T(8,128)S(1)}, u32[]{:S(2)}, u32[]{:S(2)}) collective-permute-start(f32[32,1024]{1,0:T(8,128)S(1)} %shard_map.74.refs_2_.refs_8_.refs_10_), channel_id=1, source_target_pairs={{0,8},{8,0},{16,24},{24,16},{1,9},{9,1},{17,25},{25,17},{2,10},{10... | collective-permute-start | bytes 393224 | tf_op jit(solution)/shard_map/ppermute | solution.py:293
  21.4 3.1 %collective-permute-start.7 = (f32[32,1024]{1,0:T(8,128)S(1)}, f32[32,1024]{1,0:T(8,128)S(1)}, u32[]{:S(2)}, u32[]{:S(2)}) collective-permute-start(f32[32,1024]{1,0:T(8,128)S(1)} %collective-permute-done.6.refs_4_.refs_10_), channel_id=1, source_target_pairs={{0,8},{8,0},{16,24},{24,16},{1,9},{9,1},{17,25},{25,17},{2,10},{10... | collective-permute-start | bytes 393224 | tf_op jit(solution)/shard_map/ppermute | solution.py:293
  23.1 2.5 %collective-permute-start.9 = (f32[32,1024]{1,0:T(8,128)S(1)}, f32[32,1024]{1,0:T(8,128)S(1)}, u32[]{:S(2)}, u32[]{:S(2)}) collective-permute-start(f32[32,1024]{1,0:T(8,128)S(1)} %collective-permute-done.8.refs_12_), channel_id=1, source_target_pairs={{0,8},{8,0},{16,24},{24,16},{1,9},{9,1},{17,25},{25,17},{2,10},{10... | collective-permute-start | bytes 393224 | tf_op jit(solution)/shard_map/ppermute | solution.py:293
  31.8 2.0 %collective-permute-start.10 = (f32[64,256]{1,0:T(8,128)S(1)}, f32[64,256]{1,0:T(8,128)S(1)}, u32[]{:S(2)}, u32[]{:S(2)}) collective-permute-start(f32[64,256]{1,0:T(8,128)S(1)} %get-tuple-element.48), channel_id=1, source_target_pairs={{0,8},{8,0},{16,24},{24,16},{1,9},{9,1},{17,25},{25,17},{2,10},{10... | collective-permute-start | bytes 196616 | tf_op jit(solution)/shard_map/ppermute | solution.py:378
  32.4 4.6 %collective-permute-start.11 = (f32[64,256]{1,0:T(8,128)S(1)}, f32[64,256]{1,0:T(8,128)S(1)}, u32[]{:S(2)}, u32[]{:S(2)}) collective-permute-start(f32[64,256]{1,0:T(8,128)S(1)} %get-tuple-element.49), channel_id=1, source_target_pairs={{0,16},{8,24},{16,0},{24,8},{1,17},{9,25},{17,1},{25,9},{2,18},{10... | collective-permute-start | bytes 196616 | tf_op jit(solution)/shard_map/ppermute | solution.py:378
  33.4 4.4 %collective-permute-start.12 = (f32[64,256]{1,0:T(8,128)S(1)}, f32[64,256]{1,0:T(8,128)S(1)}, u32[]{:S(2)}, u32[]{:S(2)}) collective-permute-start(f32[64,256]{1,0:T(8,128)S(1)} %get-tuple-element.50), channel_id=1, source_target_pairs={{0,24},{8,16},{16,8},{24,0},{1,25},{9,17},{17,9},{25,1},{2,26},{10... | collective-permute-start | bytes 196616 | tf_op jit(solution)/shard_map/ppermute | solution.py:378

commit v7 on v6

--- a/solution.py
+++ b/solution.py
@@ -182,11 +182,10 @@
 
 
 def gain_kernel(earlier, last, near_parts, order, longitudes, blocks, flags, values, errors, *refs):
-    cov, left = refs[-1], refs[-10:-1]
-    outs = refs[4 + earlier + len(order) : -10]
+    cov, left = refs[-1], refs[-11:-1]
+    outs = refs[4 + earlier + len(order) : -11]
     before, first_seen, parts = refs[:4], refs[4 : 4 + earlier], refs[4 + earlier : 4 + earlier + len(order)]
     own_cells = outs[0].shape[1]
-    near_rows = left[0].shape[0]
     total = sum(part.shape[0] for part in parts)
     last_seen, last_cells = observe(parts[-last:], longitudes, own_cells, blocks, flags)
     square_sum, cross, seen_mean, _ = moments(last_seen, last_cells, (before[2][...], before[3][...]), total)
@@ -202,17 +201,21 @@
     root = lax.rsqrt(jnp.sum(size, axis=0, keepdims=True))
     root_down = lax.rsqrt(jnp.sum(size, axis=1, keepdims=True))
     cross = split((cross + before[1][...]) * root_down)
-    seen = jnp.concatenate([ref[...] for ref in first_seen] + [last_seen], axis=0)
-    start = ((values[...] - seen_mean) - 0.5 * (seen - seen_mean)) * root
+    seen = jnp.concatenate([ref[...] for ref in first_seen[1:]] + [last_seen], axis=0)
+    start = weights(seen, seen_mean, values, root)
     b1 = (covariance * root_down) * root
     s1 = split(b1)
     b2 = 2.0 * b1 - square(s1)
     s2 = split(b2)
     b4 = 2.0 * b2 - square(s2)
     s4 = split(b4)
-    for out, value in zip(left, (start[:near_rows],) + s4 + s2 + s1 + cross):
+    for out, value in zip(left, (seen_mean, root) + s4 + s2 + s1 + cross):
         out[...] = value
-    finish(start[near_rows:], s4, (s2, s1), cross, parts[near_parts:], order[near_parts:], outs)
+    finish(start, s4, (s2, s1), cross, parts[near_parts:], order[near_parts:], outs)
+
+
+def weights(seen, seen_mean, values, root):
+    return ((values[...] - seen_mean) - 0.5 * (seen - seen_mean)) * root
 
 
 def finish(start, s4, factors, cross, parts, order, outs):
@@ -229,10 +232,11 @@
         at += size
 
 
-def finish_kernel(order, start, *refs):
+def finish_kernel(order, seen, values, seen_mean, root, *refs):
     s4, s2, s1, cross = [(refs[i][...], refs[i + 1][...]) for i in (0, 2, 4, 6)]
     parts, outs = refs[8 : 8 + len(order)], refs[8 + len(order) :]
-    finish(start[...], s4, (s2, s1), cross, parts, order, outs)
+    start = weights(seen[...], seen_mean[...], values, root[...])
+    finish(start, s4, (s2, s1), cross, parts, order, outs)
 
 
 def place_kernel(masks, longitudes, *refs):
@@ -345,17 +349,16 @@
     far_mems = mems - mems // 2
     part_of_product = [jax.ShapeDtypeStruct((observations, observations), BF16)] * 2
     part_of_cross = [jax.ShapeDtypeStruct((observations, own_cells), BF16)] * 2
-    near_rows = local * (mems // 2)
     done = pl.pallas_call(
         functools.partial(
             gain_kernel, len(seen), len(stage), near_parts, near_order + far_order, longitudes
         ),
         out_shape=[to_member] * far_mems
-        + [jax.ShapeDtypeStruct((near_rows, observations), F32)]
+        + [jax.ShapeDtypeStruct((1, observations), F32)] * 2
         + part_of_product * 3
         + part_of_cross,
         in_specs=[SMEM] + [VMEM] * (3 + len(before) + len(seen) + len(flat)),
-        out_specs=[VMEM] * (far_mems + 9),
+        out_specs=[VMEM] * (far_mems + 10),
         scratch_shapes=[pltpu.VMEM((observations, observations), F32)],
         cost_estimate=pl.CostEstimate(flops=5000000000, bytes_accessed=4000000, transcendentals=0),
         compiler_params=pltpu.CompilerParams(vmem_limit_bytes=24 << 20),
@@ -365,12 +368,12 @@
     near_outs = pl.pallas_call(
         functools.partial(finish_kernel, near_order),
         out_shape=[to_member] * (mems // 2),
-        in_specs=[VMEM] * (9 + near_parts),
+        in_specs=[VMEM] * (12 + near_parts),
         out_specs=[VMEM] * (mems // 2),
         cost_estimate=pl.CostEstimate(flops=600000000, bytes_accessed=2000000, transcendentals=0),
         compiler_params=pltpu.CompilerParams(vmem_limit_bytes=16 << 20),
         name="finish",
-    )(*done[far_mems:], *flat[:near_parts])
+    )(seen[0], observed_values[0], *done[far_mems:], *flat[:near_parts])
     outs = list(near_outs) + list(far_outs)
     came = {0: outs[0]}
     for mask in sorted(masks[1:], reverse=True):

time: 38.7 us -> 38.7 us (level)
  no operation moved by 1% of the time
where the time goes in v7:
time: 38.7 us; the launch traced here: 38.6 us
  waiting for transfers between devices  15.1 us (39%)
  starting transfers between devices  11.7 us (30%)
  Pallas kernels  10.6 us (27%)
  local copies, waits for them, and re-layouts  1.05 us (3%)
    ppermute x2, waiting for transfers between devices, body(): near.append(lax.ppermute(own, 'lat', near_pairs))  5.17 us
    pallas_call x1, Pallas kernels, body(): pl.pallas_call(functools.partial(gain_kernel, len(seen), len(stage), near...  4.42 us
    ppermute x3, waiting for transfers between devices, body(): came[mask] = lax.ppermute(outs[masks.index(mask)], 'mem', pairs)  3.92 us
    ppermute x2, waiting for transfers between devices, body(): far_half.append(lax.ppermute(band, 'mem', xor_pairs(mems, top)))  3.47 us
    ppermute x2, starting transfers between devices, body(): near.append(lax.ppermute(own, 'lat', near_pairs))  3.14 us
    ppermute x2, starting transfers between devices, body(): far.append(lax.ppermute(near[k], 'lat', far_pairs))  3.02 us
    ppermute x2, starting transfers between devices, body(): far_half.append(lax.ppermute(band, 'mem', xor_pairs(mems, top)))  2.96 us
    ppermute x2, waiting for transfers between devices, body(): far.append(lax.ppermute(near[k], 'lat', far_pairs))  2.54 us
  transfers between devices with their start and end apart: 13, of which 7 were waited for; matrix products, arithmetic and copies ran while one was open for 0% of the time, Pallas kernels for 9%

profile of v7, /device:TPU:0, one launch (start us, length us, event | category | flops | bytes accessed | tf_op | source)
XLA Modules:
  0.0 38.6 jit_solution(9808044225354622751)
XLA Ops:
  0.0 1.0 %fusion = (f32[32,2,512]{2,1,0:T(2,128)S(1)}, f32[32,2,512]{2,1,0:T(2,128)S(1)}) fusion(f32[64,2,512]{2,1,0:T(2,128)} %own.3), kind=kLoop, calls=%fused_computation.1 | loop fusion | bytes 524288 | tf_op jit(solution)/shard_map/slice | solution.py:285
  1.2 3.1 %collective-permute-start = (f32[34,2,512]{2,1,0:T(2,128)S(1)}, f32[34,2,512]{2,1,0:T(2,128)S(1)}, u32[]{:S(2)}, u32[]{:S(2)}) collective-permute-start(f32[34,2,512]{2,1,0:T(2,128)S(1)} %pad_maximum_fusion), channel_id=1, source_target_pairs={{0,1},{1,0},{2,3},{3,2},{4,5},{5,4},{6,7},{7,6},{8,9},{9,8},{10,11... | collective-permute-start | bytes 417800 | tf_op jit(solution)/shard_map/ppermute | solution.py:288
  4.3 4.4 %collective-permute-done.near.coef_near = f32[34,2,512]{2,1,0:T(2,128)S(1)} collective-permute-done((f32[34,2,512]{2,1,0:T(2,128)S(1)}, f32[34,2,512]{2,1,0:T(2,128)S(1)}, u32[]{:S(2)}, u32[]{:S(2)}) %collective-permute-start) | collective-permute-done | bytes 139296 | tf_op jit(solution)/shard_map/ppermute | solution.py:288
  8.8 2.1 %collective-permute-start.1 = (f32[34,2,512]{2,1,0:T(2,128)S(1)}, f32[34,2,512]{2,1,0:T(2,128)S(1)}, u32[]{:S(2)}, u32[]{:S(2)}) collective-permute-start(f32[34,2,512]{2,1,0:T(2,128)S(1)} %collective-permute-done.near.coef_near), channel_id=1, source_target_pairs={{0,2},{2,4},{4,6},{3,1},{5,3},{7,5},{6,7},{1,0},{8,10},{10,12},{12... | collective-permute-start | bytes 417800 | tf_op jit(solution)/shard_map/ppermute | solution.py:290
  10.8 0.7 %collective-permute-done.3.near = f32[32,2,512]{2,1,0:T(2,128)S(1)} collective-permute-done((f32[32,2,512]{2,1,0:T(2,128)S(1)}, f32[32,2,512]{2,1,0:T(2,128)S(1)}, u32[]{:S(2)}, u32[]{:S(2)}) %collective-permute-start.3) | collective-permute-done | bytes 131104 | tf_op jit(solution)/shard_map/ppermute | solution.py:288
  11.6 0.9 %collective-permute-start.4 = (f32[32,2,512]{2,1,0:T(2,128)S(1)}, f32[32,2,512]{2,1,0:T(2,128)S(1)}, u32[]{:S(2)}, u32[]{:S(2)}) collective-permute-start(f32[32,2,512]{2,1,0:T(2,128)S(1)} %collective-permute-done.3.near), channel_id=1, source_target_pairs={{0,2},{2,4},{4,6},{3,1},{5,3},{7,5},{6,7},{1,0},{8,10},{10,12},{12... | collective-permute-start | bytes 393224 | tf_op jit(solution)/shard_map/ppermute | solution.py:290
  12.5 2.5 %collective-permute-done.1.far.coef_far = f32[34,2,512]{2,1,0:T(2,128)S(1)} collective-permute-done((f32[34,2,512]{2,1,0:T(2,128)S(1)}, f32[34,2,512]{2,1,0:T(2,128)S(1)}, u32[]{:S(2)}, u32[]{:S(2)}) %collective-permute-start.1) | collective-permute-done | bytes 139296 | tf_op jit(solution)/shard_map/ppermute | solution.py:290
  15.1 0.5 %shard_map.73.refs_0_.refs_6_.refs_8_ = f32[32,1024]{1,0:T(8,128)S(1)} custom-call(f32[64,2,512]{2,1,0:T(2,128)S(1)} %copy-done, f32[2,512]{1,0:T(2,128)S(1)} %copy-done.1, f32[2,512]{1,0:T(2,128)S(1)} %copy-done.2, f32[34,2,512]{2,1,0:T(2,128)S(1)} %collective-permute-done.near.coef_near, f32[34,2,512]{2,1,0:T(2,128)S(1)} %collective-permute-done.1.far.coef_far, ...), custom_call_target="tpu_custom_call" | custom-call | flops 2000000 | bytes 2000000 | tf_op jit(solution)/shard_map/pallas_call | solution.py:306
  15.6 1.9 %collective-permute-start.6 = (f32[32,1024]{1,0:T(8,128)S(1)}, f32[32,1024]{1,0:T(8,128)S(1)}, u32[]{:S(2)}, u32[]{:S(2)}) collective-permute-start(f32[32,1024]{1,0:T(8,128)S(1)} %shard_map.73.refs_0_.refs_6_.refs_8_), channel_id=1, source_target_pairs={{0,16},{8,24},{16,0},{24,8},{1,17},{9,25},{17,1},{25,9},{2,18},{10... | collective-permute-start | bytes 393224 | tf_op jit(solution)/shard_map/ppermute | solution.py:314
  17.5 0.5 %shard_map.74.refs_2_.refs_8_.refs_10_ = f32[32,1024]{1,0:T(8,128)S(1)} custom-call(f32[64,2,512]{2,1,0:T(2,128)S(1)} %copy-done, f32[2,512]{1,0:T(2,128)S(1)} %copy-done.1, f32[2,512]{1,0:T(2,128)S(1)} %copy-done.2, f32[32,2,512]{2,1,0:T(2,128)S(1)} %collective-permute-done.3.near, f32[32,2,512]{2,1,0:T(2,128)S(1)} %collective-permute-done.4.far, ...), custom_call_target="tpu_custom_call" | custom-call | flops 2000000 | bytes 2000000 | tf_op jit(solution)/shard_map/pallas_call | solution.py:306
  18.1 1.0 %collective-permute-start.8 = (f32[32,1024]{1,0:T(8,128)S(1)}, f32[32,1024]{1,0:T(8,128)S(1)}, u32[]{:S(2)}, u32[]{:S(2)}) collective-permute-start(f32[32,1024]{1,0:T(8,128)S(1)} %shard_map.74.refs_2_.refs_8_.refs_10_), channel_id=1, source_target_pairs={{0,16},{8,24},{16,0},{24,8},{1,17},{9,25},{17,1},{25,9},{2,18},{10... | collective-permute-start | bytes 393224 | tf_op jit(solution)/shard_map/ppermute | solution.py:314
  19.1 0.5 %collective-permute-start.5 = (f32[32,1024]{1,0:T(8,128)S(1)}, f32[32,1024]{1,0:T(8,128)S(1)}, u32[]{:S(2)}, u32[]{:S(2)}) collective-permute-start(f32[32,1024]{1,0:T(8,128)S(1)} %shard_map.74.refs_2_.refs_8_.refs_10_), channel_id=1, source_target_pairs={{0,8},{8,0},{16,24},{24,16},{1,9},{9,1},{17,25},{25,17},{2,10},{10... | collective-permute-start | bytes 393224 | tf_op jit(solution)/shard_map/ppermute | solution.py:297
  19.6 1.8 %collective-permute-done.6.refs_4_.refs_10_ = f32[32,1024]{1,0:T(8,128)S(1)} collective-permute-done((f32[32,1024]{1,0:T(8,128)S(1)}, f32[32,1024]{1,0:T(8,128)S(1)}, u32[]{:S(2)}, u32[]{:S(2)}) %collective-permute-start.6) | collective-permute-done | bytes 131104 | tf_op jit(solution)/shard_map/ppermute | solution.py:314
  21.4 1.7 %collective-permute-done.8.refs_12_ = f32[32,1024]{1,0:T(8,128)S(1)} collective-permute-done((f32[32,1024]{1,0:T(8,128)S(1)}, f32[32,1024]{1,0:T(8,128)S(1)}, u32[]{:S(2)}, u32[]{:S(2)}) %collective-permute-start.8) | collective-permute-done | bytes 131104 | tf_op jit(solution)/shard_map/ppermute | solution.py:314
  23.1 1.4 %shard_map.75 = (f32[512,512]{1,0:T(8,128)S(1)}, f32[512,256]{1,0:T(8,128)S(1)}, f32[1,512]{1,0:T(1,128)S(1)}, f32[1,256]{1,0:T(1,128)S(1)}, f32[128,512]{1,0:T(8,128)S(1)}) custom-call(s32[4,4]{1,0:T(4,128)S(1)} %bitcast.19, s32[4,512]{1,0:T(4,128)S(1)} %bitcast.10, f32[32,1024]{1,0:T(8,128)S(1)} %shard_map.73.refs_0_.refs_6_.refs_8_, ...), custom_call_target="tpu_custom_call" | custom-call | flops 800000000 | bytes 3000000 | tf_op jit(solution)/shard_map/pallas_call | solution.py:319
  24.5 1.1 %shard_map.76 = (f32[512,512]{1,0:T(8,128)S(1)}, f32[512,256]{1,0:T(8,128)S(1)}, f32[1,512]{1,0:T(1,128)S(1)}, f32[1,256]{1,0:T(1,128)S(1)}, f32[64,512]{1,0:T(8,128)S(1)}) custom-call(s32[4,4]{1,0:T(4,128)S(1)} %bitcast.20, s32[4,512]{1,0:T(4,128)S(1)} %bitcast.11, f32[512,512]{1,0:T(8,128)S(1)} %get-tuple-element.30.refs_0_, ...), custom_call_target="tpu_custom_call" | custom-call | flops 800000000 | bytes 3000000 | tf_op jit(solution)/shard_map/pallas_call | solution.py:319
  25.6 4.4 %gain.1 = (f32[64,256]{1,0:T(8,128)S(1)}, f32[64,256]{1,0:T(8,128)S(1)}, f32[1,512]{1,0:T(1,128)S(1)}, f32[1,512]{1,0:T(1,128)S(1)}, bf16[512,512]{1,0:T(8,128)(...) custom-call(s32[4,4]{1,0:T(4,128)S(1)} %bitcast.21, ...), custom_call_target="tpu_custom_call" | custom-call | flops 5000000000 | bytes 4000000 | tf_op jit(solution)/shard_map/gain/pallas_call | solution.py:352
  30.1 1.8 %finish.1 = (f32[64,256]{1,0:T(8,128)S(1)}, f32[64,256]{1,0:T(8,128)S(1)}) custom-call(f32[128,512]{1,0:T(8,128)S(1)} %get-tuple-element.29.refs_4_.seen, f32[1,512]{1,0:T(1,128)S(1)} %bitcast.16, f32[1,512]{1,0:T(1,128)S(1)} %get-tuple-element.39.seen_mean, f32[1,512]{1,0:T(1,128)S(1)} %get-tuple-element.40.root, ...), custom_call_target="tpu_custom_call" | custom-call | flops 600000000 | bytes 2000000 | tf_op jit(solution)/shard_map/finish/pallas_call | solution.py:368
  31.8 0.6 %collective-permute-start.10 = (f32[64,256]{1,0:T(8,128)S(1)}, f32[64,256]{1,0:T(8,128)S(1)}, u32[]{:S(2)}, u32[]{:S(2)}) collective-permute-start(f32[64,256]{1,0:T(8,128)S(1)} %get-tuple-element.50), channel_id=1, source_target_pairs={{0,8},{8,0},{16,24},{24,16},{1,9},{9,1},{17,25},{25,17},{2,10},{10... | collective-permute-start | bytes 196616 | tf_op jit(solution)/shard_map/ppermute | solution.py:381
  32.4 1.0 %collective-permute-start.11 = (f32[64,256]{1,0:T(8,128)S(1)}, f32[64,256]{1,0:T(8,128)S(1)}, u32[]{:S(2)}, u32[]{:S(2)}) collective-permute-start(f32[64,256]{1,0:T(8,128)S(1)} %get-tuple-element.51), channel_id=1, source_target_pairs={{0,16},{8,24},{16,0},{24,8},{1,17},{9,25},{17,1},{25,9},{2,18},{10... | collective-permute-start | bytes 196616 | tf_op jit(solution)/shard_map/ppermute | solution.py:381
  33.4 0.5 %collective-permute-start.12 = (f32[64,256]{1,0:T(8,128)S(1)}, f32[64,256]{1,0:T(8,128)S(1)}, u32[]{:S(2)}, u32[]{:S(2)}) collective-permute-start(f32[64,256]{1,0:T(8,128)S(1)} %get-tuple-element.52), channel_id=1, source_target_pairs={{0,24},{8,16},{16,8},{24,0},{1,25},{9,17},{17,9},{25,1},{2,26},{10... | collective-permute-start | bytes 196616 | tf_op jit(solution)/shard_map/ppermute | solution.py:381
  33.9 3.2 %collective-permute-done.11.refs_2_ = f32[64,256]{1,0:T(8,128)S(1)} collective-permute-done((f32[64,256]{1,0:T(8,128)S(1)}, f32[64,256]{1,0:T(8,128)S(1)}, u32[]{:S(2)}, u32[]{:S(2)}) %collective-permute-start.11) | collective-permute-done | bytes 65568 | tf_op jit(solution)/shard_map/ppermute | solution.py:381
  37.0 0.8 %collective-permute-done.12.refs_3_ = f32[64,256]{1,0:T(8,128)S(1)} collective-permute-done((f32[64,256]{1,0:T(8,128)S(1)}, f32[64,256]{1,0:T(8,128)S(1)}, u32[]{:S(2)}, u32[]{:S(2)}) %collective-permute-start.12) | collective-permute-done | bytes 65568 | tf_op jit(solution)/shard_map/ppermute | solution.py:381
  37.8 0.8 %place.1 = f32[64,2,512]{2,1,0:T(2,128)} custom-call(f32[64,256]{1,0:T(8,128)S(1)} %get-tuple-element.49.refs_0_, f32[64,256]{1,0:T(8,128)S(1)} %collective-permute-done.10.refs_1_, f32[64,256]{1,0:T(8,128)S(1)} %collective-permute-done.11.refs_2_, f32[64,256]{1,0:T(8,128)S(1)} %collective-permute-done.12.refs_3_), custom_call_target="tpu_custom_call" | custom-call | flops 100000 | bytes 600000 | tf_op jit(solution)/shard_map/place/pallas_call | solution.py:382
  (25 shorter events, 0.2 us)
Async XLA Ops:
  0.0 1.0 %copy-start.1 = (f32[2,512]{1,0:T(2,128)S(1)}, f32[2,512]{1,0:T(2,128)}, u32[]{:S(2)}) copy-start(f32[2,512]{1,0:T(2,128)} %dif.3) | copy-start | bytes 12292
  0.0 1.0 %copy-start.2 = (f32[2,512]{1,0:T(2,128)S(1)}, f32[2,512]{1,0:T(2,128)}, u32[]{:S(2)}) copy-start(f32[2,512]{1,0:T(2,128)} %wind.3) | copy-start | bytes 12292
  1.0 14.0 %copy-start = (f32[64,2,512]{2,1,0:T(2,128)S(1)}, f32[64,2,512]{2,1,0:T(2,128)}, u32[]{:S(2)}) copy-start(f32[64,2,512]{2,1,0:T(2,128)} %own.3) | copy-start | bytes 786436
  1.1 14.0 %copy-start.4 = (f32[1,1,512]{2,1,0:T(1,128)S(1)}, f32[1,1,512]{2,1,0:T(1,128)}, u32[]{:S(2)}) copy-start(f32[1,1,512]{2,1,0:T(1,128)} %param.12) | copy-start | bytes 6148
  1.1 14.0 %copy-start.5 = (s32[1,4,4]{2,1,0:T(4,128)S(1)}, s32[1,4,4]{2,1,0:T(4,128)}, u32[]{:S(2)}) copy-start(s32[1,4,4]{2,1,0:T(4,128)} %param.10) | copy-start | bytes 196
  1.1 14.0 %copy-start.6 = (f32[1,1,512]{2,1,0:T(1,128)S(1)}, f32[1,1,512]{2,1,0:T(1,128)}, u32[]{:S(2)}) copy-start(f32[1,1,512]{2,1,0:T(1,128)} %param.13) | copy-start | bytes 6148
  1.2 13.9 %copy-start.3 = (s32[1,4,512]{2,1,0:T(4,128)S(1)}, s32[1,4,512]{2,1,0:T(4,128)}, u32[]{:S(2)}) copy-start(s32[1,4,512]{2,1,0:T(4,128)} %param.11) | copy-start | bytes 24580
  1.2 7.6 %collective-permute-start = (f32[34,2,512]{2,1,0:T(2,128)S(1)}, f32[34,2,512]{2,1,0:T(2,128)S(1)}, u32[]{:S(2)}, u32[]{:S(2)}) collective-permute-start(f32[34,2,512]{2,1,0:T(2,128)S(1)} %pad_maximum_fusion), channel_id=1, source_target_pairs={{0,1},{1,0},{2,3},{3,2},{4,5},{5,4},{6,7},{7,6},{8,9},{9,8},{10,11... | collective-permute-start | bytes 417800 | tf_op jit(solution)/shard_map/ppermute | solution.py:288
  4.2 7.3 %collective-permute-start.3 = (f32[32,2,512]{2,1,0:T(2,128)S(1)}, f32[32,2,512]{2,1,0:T(2,128)S(1)}, u32[]{:S(2)}, u32[]{:S(2)}) collective-permute-start(f32[32,2,512]{2,1,0:T(2,128)S(1)} %get-tuple-element.53), channel_id=1, source_target_pairs={{0,1},{1,0},{2,3},{3,2},{4,5},{5,4},{6,7},{7,6},{8,9},{9,8},{10,11... | collective-permute-start | bytes 393224 | tf_op jit(solution)/shard_map/ppermute | solution.py:288
  8.8 6.3 %collective-permute-start.1 = (f32[34,2,512]{2,1,0:T(2,128)S(1)}, f32[34,2,512]{2,1,0:T(2,128)S(1)}, u32[]{:S(2)}, u32[]{:S(2)}) collective-permute-start(f32[34,2,512]{2,1,0:T(2,128)S(1)} %collective-permute-done.near.coef_near), channel_id=1, source_target_pairs={{0,2},{2,4},{4,6},{3,1},{5,3},{7,5},{6,7},{1,0},{8,10},{10,12},{12... | collective-permute-start | bytes 417800 | tf_op jit(solution)/shard_map/ppermute | solution.py:290
  11.6 6.0 %collective-permute-start.4 = (f32[32,2,512]{2,1,0:T(2,128)S(1)}, f32[32,2,512]{2,1,0:T(2,128)S(1)}, u32[]{:S(2)}, u32[]{:S(2)}) collective-permute-start(f32[32,2,512]{2,1,0:T(2,128)S(1)} %collective-permute-done.3.near), channel_id=1, source_target_pairs={{0,2},{2,4},{4,6},{3,1},{5,3},{7,5},{6,7},{1,0},{8,10},{10,12},{12... | collective-permute-start | bytes 393224 | tf_op jit(solution)/shard_map/ppermute | solution.py:290
  15.6 5.8 %collective-permute-start.6 = (f32[32,1024]{1,0:T(8,128)S(1)}, f32[32,1024]{1,0:T(8,128)S(1)}, u32[]{:S(2)}, u32[]{:S(2)}) collective-permute-start(f32[32,1024]{1,0:T(8,128)S(1)} %shard_map.73.refs_0_.refs_6_.refs_8_), channel_id=1, source_target_pairs={{0,16},{8,24},{16,0},{24,8},{1,17},{9,25},{17,1},{25,9},{2,18},{10... | collective-permute-start | bytes 393224 | tf_op jit(solution)/shard_map/ppermute | solution.py:314
  18.1 5.0 %collective-permute-start.8 = (f32[32,1024]{1,0:T(8,128)S(1)}, f32[32,1024]{1,0:T(8,128)S(1)}, u32[]{:S(2)}, u32[]{:S(2)}) collective-permute-start(f32[32,1024]{1,0:T(8,128)S(1)} %shard_map.74.refs_2_.refs_8_.refs_10_), channel_id=1, source_target_pairs={{0,16},{8,24},{16,0},{24,8},{1,17},{9,25},{17,1},{25,9},{2,18},{10... | collective-permute-start | bytes 393224 | tf_op jit(solution)/shard_map/ppermute | solution.py:314
  19.1 4.0 %collective-permute-start.2 = (f32[32,1024]{1,0:T(8,128)S(1)}, f32[32,1024]{1,0:T(8,128)S(1)}, u32[]{:S(2)}, u32[]{:S(2)}) collective-permute-start(f32[32,1024]{1,0:T(8,128)S(1)} %shard_map.73.refs_0_.refs_6_.refs_8_), channel_id=1, source_target_pairs={{0,8},{8,0},{16,24},{24,16},{1,9},{9,1},{17,25},{25,17},{2,10},{10... | collective-permute-start | bytes 393224 | tf_op jit(solution)/shard_map/ppermute | solution.py:297
  19.1 4.0 %collective-permute-start.5 = (f32[32,1024]{1,0:T(8,128)S(1)}, f32[32,1024]{1,0:T(8,128)S(1)}, u32[]{:S(2)}, u32[]{:S(2)}) collective-permute-start(f32[32,1024]{1,0:T(8,128)S(1)} %shard_map.74.refs_2_.refs_8_.refs_10_), channel_id=1, source_target_pairs={{0,8},{8,0},{16,24},{24,16},{1,9},{9,1},{17,25},{25,17},{2,10},{10... | collective-permute-start | bytes 393224 | tf_op jit(solution)/shard_map/ppermute | solution.py:297
  21.4 3.1 %collective-permute-start.7 = (f32[32,1024]{1,0:T(8,128)S(1)}, f32[32,1024]{1,0:T(8,128)S(1)}, u32[]{:S(2)}, u32[]{:S(2)}) collective-permute-start(f32[32,1024]{1,0:T(8,128)S(1)} %collective-permute-done.6.refs_4_.refs_10_), channel_id=1, source_target_pairs={{0,8},{8,0},{16,24},{24,16},{1,9},{9,1},{17,25},{25,17},{2,10},{10... | collective-permute-start | bytes 393224 | tf_op jit(solution)/shard_map/ppermute | solution.py:297
  23.1 2.5 %collective-permute-start.9 = (f32[32,1024]{1,0:T(8,128)S(1)}, f32[32,1024]{1,0:T(8,128)S(1)}, u32[]{:S(2)}, u32[]{:S(2)}) collective-permute-start(f32[32,1024]{1,0:T(8,128)S(1)} %collective-permute-done.8.refs_12_), channel_id=1, source_target_pairs={{0,8},{8,0},{16,24},{24,16},{1,9},{9,1},{17,25},{25,17},{2,10},{10... | collective-permute-start | bytes 393224 | tf_op jit(solution)/shard_map/ppermute | solution.py:297
  31.8 2.0 %collective-permute-start.10 = (f32[64,256]{1,0:T(8,128)S(1)}, f32[64,256]{1,0:T(8,128)S(1)}, u32[]{:S(2)}, u32[]{:S(2)}) collective-permute-start(f32[64,256]{1,0:T(8,128)S(1)} %get-tuple-element.50), channel_id=1, source_target_pairs={{0,8},{8,0},{16,24},{24,16},{1,9},{9,1},{17,25},{25,17},{2,10},{10... | collective-permute-start | bytes 196616 | tf_op jit(solution)/shard_map/ppermute | solution.py:381
  32.4 4.6 %collective-permute-start.11 = (f32[64,256]{1,0:T(8,128)S(1)}, f32[64,256]{1,0:T(8,128)S(1)}, u32[]{:S(2)}, u32[]{:S(2)}) collective-permute-start(f32[64,256]{1,0:T(8,128)S(1)} %get-tuple-element.51), channel_id=1, source_target_pairs={{0,16},{8,24},{16,0},{24,8},{1,17},{9,25},{17,1},{25,9},{2,18},{10... | collective-permute-start | bytes 196616 | tf_op jit(solution)/shard_map/ppermute | solution.py:381
  33.4 4.4 %collective-permute-start.12 = (f32[64,256]{1,0:T(8,128)S(1)}, f32[64,256]{1,0:T(8,128)S(1)}, u32[]{:S(2)}, u32[]{:S(2)}) collective-permute-start(f32[64,256]{1,0:T(8,128)S(1)} %get-tuple-element.52), channel_id=1, source_target_pairs={{0,24},{8,16},{16,8},{24,0},{1,25},{9,17},{17,9},{25,1},{2,26},{10... | collective-permute-start | bytes 196616 | tf_op jit(solution)/shard_map/ppermute | solution.py:381

commit v8 on v6

--- a/solution.py
+++ b/solution.py
@@ -8,6 +8,7 @@
 from jax.sharding import PartitionSpec as P
 
 
+LOTS = 2
 ADVECTION = 0.1
 F32 = jnp.float32
 BF16 = jnp.bfloat16
@@ -236,16 +237,27 @@
 
 
 def place_kernel(masks, longitudes, *refs):
-    sources, out = refs[:-1], refs[-1]
+    sources, (out, laid, sems) = refs[:-3], refs[-3:]
     here = lax.axis_index("mem")
+    lots = sems.shape[0]
+    size = out.shape[0] // lots
     width = sources[0].shape[1]
-    found = [source[...] for source in sources]
-    for patch in range(len(masks)):
-        value = found[0]
-        for m, candidate in zip(masks[1:], found[1:]):
-            value = jnp.where((here ^ m) == patch, candidate, value)
-        row, column = divmod(patch * width, longitudes)
-        out[:, row, column : column + width] = value
+    copies = []
+    for lot in range(lots):
+        members = slice(lot * size, (lot + 1) * size)
+        found = [source[members, :] for source in sources]
+        for patch in range(len(masks)):
+            value = found[0]
+            for m, candidate in zip(masks[1:], found[1:]):
+                value = jnp.where((here ^ m) == patch, candidate, value)
+            row, column = divmod(patch * width, longitudes)
+            laid[members, row, column : column + width] = value
+        copies.append(
+            pltpu.make_async_copy(laid.at[pl.ds(lot * size, size)], out.at[pl.ds(lot * size, size)], sems.at[lot])
+        )
+        copies[-1].start()
+    for copy in copies:
+        copy.wait()
 
 
 def body(
@@ -380,7 +392,8 @@
         functools.partial(place_kernel, masks, longitudes),
         out_shape=jax.ShapeDtypeStruct((local, rows, longitudes), F32),
         in_specs=[VMEM] * mems,
-        out_specs=VMEM,
+        out_specs=pl.BlockSpec(memory_space=pl.ANY),
+        scratch_shapes=[pltpu.VMEM((local, rows, longitudes), F32), pltpu.SemaphoreType.DMA((LOTS,))],
         cost_estimate=pl.CostEstimate(flops=100000, bytes_accessed=600000, transcendentals=0),
         compiler_params=pltpu.CompilerParams(vmem_limit_bytes=8 << 20),
         name="place",

time: 38.7 us -> 38.7 us (level)
  no operation moved by 1% of the time
where the time goes in v8:
time: 38.7 us; the launch traced here: 38.6 us
  waiting for transfers between devices  15.1 us (39%)
  starting transfers between devices  11.6 us (30%)
  Pallas kernels  10.5 us (27%)
  local copies, waits for them, and re-layouts  1.05 us (3%)
    ppermute x2, waiting for transfers between devices, body(): near.append(lax.ppermute(own, 'lat', near_pairs))  5.17 us
    pallas_call x1, Pallas kernels, body(): pl.pallas_call(functools.partial(gain_kernel, len(seen), len(stage), near...  4.45 us
    ppermute x3, waiting for transfers between devices, body(): came[mask] = lax.ppermute(outs[masks.index(mask)], 'mem', pairs)  3.94 us
    ppermute x2, waiting for transfers between devices, body(): far_half.append(lax.ppermute(band, 'mem', xor_pairs(mems, top)))  3.47 us
    ppermute x2, starting transfers between devices, body(): near.append(lax.ppermute(own, 'lat', near_pairs))  3.14 us
    ppermute x2, starting transfers between devices, body(): far.append(lax.ppermute(near[k], 'lat', far_pairs))  3.02 us
    ppermute x2, starting transfers between devices, body(): far_half.append(lax.ppermute(band, 'mem', xor_pairs(mems, top)))  2.96 us
    ppermute x2, waiting for transfers between devices, body(): far.append(lax.ppermute(near[k], 'lat', far_pairs))  2.54 us
  transfers between devices with their start and end apart: 13, of which 7 were waited for; matrix products, arithmetic and copies ran while one was open for 0% of the time, Pallas kernels for 9%

profile of v8, /device:TPU:0, one launch (start us, length us, event | category | flops | bytes accessed | tf_op | source)
XLA Modules:
  0.0 38.6 jit_solution(5270682352741608762)
XLA Ops:
  0.0 1.0 %fusion = (f32[32,2,512]{2,1,0:T(2,128)S(1)}, f32[32,2,512]{2,1,0:T(2,128)S(1)}) fusion(f32[64,2,512]{2,1,0:T(2,128)} %own.3), kind=kLoop, calls=%fused_computation.1 | loop fusion | bytes 524288 | tf_op jit(solution)/shard_map/slice | solution.py:293
  1.2 3.1 %collective-permute-start = (f32[34,2,512]{2,1,0:T(2,128)S(1)}, f32[34,2,512]{2,1,0:T(2,128)S(1)}, u32[]{:S(2)}, u32[]{:S(2)}) collective-permute-start(f32[34,2,512]{2,1,0:T(2,128)S(1)} %pad_maximum_fusion), channel_id=1, source_target_pairs={{0,1},{1,0},{2,3},{3,2},{4,5},{5,4},{6,7},{7,6},{8,9},{9,8},{10,11... | collective-permute-start | bytes 417800 | tf_op jit(solution)/shard_map/ppermute | solution.py:296
  4.3 4.4 %collective-permute-done.near.coef_near = f32[34,2,512]{2,1,0:T(2,128)S(1)} collective-permute-done((f32[34,2,512]{2,1,0:T(2,128)S(1)}, f32[34,2,512]{2,1,0:T(2,128)S(1)}, u32[]{:S(2)}, u32[]{:S(2)}) %collective-permute-start) | collective-permute-done | bytes 139296 | tf_op jit(solution)/shard_map/ppermute | solution.py:296
  8.8 2.1 %collective-permute-start.1 = (f32[34,2,512]{2,1,0:T(2,128)S(1)}, f32[34,2,512]{2,1,0:T(2,128)S(1)}, u32[]{:S(2)}, u32[]{:S(2)}) collective-permute-start(f32[34,2,512]{2,1,0:T(2,128)S(1)} %collective-permute-done.near.coef_near), channel_id=1, source_target_pairs={{0,2},{2,4},{4,6},{3,1},{5,3},{7,5},{6,7},{1,0},{8,10},{10,12},{12... | collective-permute-start | bytes 417800 | tf_op jit(solution)/shard_map/ppermute | solution.py:298
  10.8 0.7 %collective-permute-done.3.near = f32[32,2,512]{2,1,0:T(2,128)S(1)} collective-permute-done((f32[32,2,512]{2,1,0:T(2,128)S(1)}, f32[32,2,512]{2,1,0:T(2,128)S(1)}, u32[]{:S(2)}, u32[]{:S(2)}) %collective-permute-start.3) | collective-permute-done | bytes 131104 | tf_op jit(solution)/shard_map/ppermute | solution.py:296
  11.6 0.9 %collective-permute-start.4 = (f32[32,2,512]{2,1,0:T(2,128)S(1)}, f32[32,2,512]{2,1,0:T(2,128)S(1)}, u32[]{:S(2)}, u32[]{:S(2)}) collective-permute-start(f32[32,2,512]{2,1,0:T(2,128)S(1)} %collective-permute-done.3.near), channel_id=1, source_target_pairs={{0,2},{2,4},{4,6},{3,1},{5,3},{7,5},{6,7},{1,0},{8,10},{10,12},{12... | collective-permute-start | bytes 393224 | tf_op jit(solution)/shard_map/ppermute | solution.py:298
  12.5 2.5 %collective-permute-done.1.far.coef_far = f32[34,2,512]{2,1,0:T(2,128)S(1)} collective-permute-done((f32[34,2,512]{2,1,0:T(2,128)S(1)}, f32[34,2,512]{2,1,0:T(2,128)S(1)}, u32[]{:S(2)}, u32[]{:S(2)}) %collective-permute-start.1) | collective-permute-done | bytes 139296 | tf_op jit(solution)/shard_map/ppermute | solution.py:298
  15.1 0.5 %shard_map.73.refs_0_.refs_6_.refs_8_ = f32[32,1024]{1,0:T(8,128)S(1)} custom-call(f32[64,2,512]{2,1,0:T(2,128)S(1)} %copy-done, f32[2,512]{1,0:T(2,128)S(1)} %copy-done.1, f32[2,512]{1,0:T(2,128)S(1)} %copy-done.2, f32[34,2,512]{2,1,0:T(2,128)S(1)} %collective-permute-done.near.coef_near, f32[34,2,512]{2,1,0:T(2,128)S(1)} %collective-permute-done.1.far.coef_far, ...), custom_call_target="tpu_custom_call" | custom-call | flops 2000000 | bytes 2000000 | tf_op jit(solution)/shard_map/pallas_call | solution.py:314
  15.6 1.9 %collective-permute-start.6 = (f32[32,1024]{1,0:T(8,128)S(1)}, f32[32,1024]{1,0:T(8,128)S(1)}, u32[]{:S(2)}, u32[]{:S(2)}) collective-permute-start(f32[32,1024]{1,0:T(8,128)S(1)} %shard_map.73.refs_0_.refs_6_.refs_8_), channel_id=1, source_target_pairs={{0,16},{8,24},{16,0},{24,8},{1,17},{9,25},{17,1},{25,9},{2,18},{10... | collective-permute-start | bytes 393224 | tf_op jit(solution)/shard_map/ppermute | solution.py:322
  17.5 0.5 %shard_map.74.refs_2_.refs_8_.refs_10_ = f32[32,1024]{1,0:T(8,128)S(1)} custom-call(f32[64,2,512]{2,1,0:T(2,128)S(1)} %copy-done, f32[2,512]{1,0:T(2,128)S(1)} %copy-done.1, f32[2,512]{1,0:T(2,128)S(1)} %copy-done.2, f32[32,2,512]{2,1,0:T(2,128)S(1)} %collective-permute-done.3.near, f32[32,2,512]{2,1,0:T(2,128)S(1)} %collective-permute-done.4.far, ...), custom_call_target="tpu_custom_call" | custom-call | flops 2000000 | bytes 2000000 | tf_op jit(solution)/shard_map/pallas_call | solution.py:314
  18.1 1.0 %collective-permute-start.8 = (f32[32,1024]{1,0:T(8,128)S(1)}, f32[32,1024]{1,0:T(8,128)S(1)}, u32[]{:S(2)}, u32[]{:S(2)}) collective-permute-start(f32[32,1024]{1,0:T(8,128)S(1)} %shard_map.74.refs_2_.refs_8_.refs_10_), channel_id=1, source_target_pairs={{0,16},{8,24},{16,0},{24,8},{1,17},{9,25},{17,1},{25,9},{2,18},{10... | collective-permute-start | bytes 393224 | tf_op jit(solution)/shard_map/ppermute | solution.py:322
  19.1 0.5 %collective-permute-start.5 = (f32[32,1024]{1,0:T(8,128)S(1)}, f32[32,1024]{1,0:T(8,128)S(1)}, u32[]{:S(2)}, u32[]{:S(2)}) collective-permute-start(f32[32,1024]{1,0:T(8,128)S(1)} %shard_map.74.refs_2_.refs_8_.refs_10_), channel_id=1, source_target_pairs={{0,8},{8,0},{16,24},{24,16},{1,9},{9,1},{17,25},{25,17},{2,10},{10... | collective-permute-start | bytes 393224 | tf_op jit(solution)/shard_map/ppermute | solution.py:305
  19.6 1.8 %collective-permute-done.6.refs_4_.refs_10_ = f32[32,1024]{1,0:T(8,128)S(1)} collective-permute-done((f32[32,1024]{1,0:T(8,128)S(1)}, f32[32,1024]{1,0:T(8,128)S(1)}, u32[]{:S(2)}, u32[]{:S(2)}) %collective-permute-start.6) | collective-permute-done | bytes 131104 | tf_op jit(solution)/shard_map/ppermute | solution.py:322
  21.4 1.7 %collective-permute-done.8.refs_12_ = f32[32,1024]{1,0:T(8,128)S(1)} collective-permute-done((f32[32,1024]{1,0:T(8,128)S(1)}, f32[32,1024]{1,0:T(8,128)S(1)}, u32[]{:S(2)}, u32[]{:S(2)}) %collective-permute-start.8) | collective-permute-done | bytes 131104 | tf_op jit(solution)/shard_map/ppermute | solution.py:322
  23.1 1.4 %shard_map.75 = (f32[512,512]{1,0:T(8,128)S(1)}, f32[512,256]{1,0:T(8,128)S(1)}, f32[1,512]{1,0:T(1,128)S(1)}, f32[1,256]{1,0:T(1,128)S(1)}, f32[128,512]{1,0:T(8,128)S(1)}) custom-call(s32[4,4]{1,0:T(4,128)S(1)} %bitcast.15, s32[4,512]{1,0:T(4,128)S(1)} %bitcast.10, f32[32,1024]{1,0:T(8,128)S(1)} %shard_map.73.refs_0_.refs_6_.refs_8_, ...), custom_call_target="tpu_custom_call" | custom-call | flops 800000000 | bytes 3000000 | tf_op jit(solution)/shard_map/pallas_call | solution.py:327
  24.5 1.1 %shard_map.76 = (f32[512,512]{1,0:T(8,128)S(1)}, f32[512,256]{1,0:T(8,128)S(1)}, f32[1,512]{1,0:T(1,128)S(1)}, f32[1,256]{1,0:T(1,128)S(1)}, f32[64,512]{1,0:T(8,128)S(1)}) custom-call(s32[4,4]{1,0:T(4,128)S(1)} %bitcast.16, s32[4,512]{1,0:T(4,128)S(1)} %bitcast.11, f32[512,512]{1,0:T(8,128)S(1)} %get-tuple-element.28.refs_0_, ...), custom_call_target="tpu_custom_call" | custom-call | flops 800000000 | bytes 3000000 | tf_op jit(solution)/shard_map/pallas_call | solution.py:327
  25.6 4.4 %gain.1 = (f32[64,256]{1,0:T(8,128)S(1)}, f32[64,256]{1,0:T(8,128)S(1)}, f32[128,512]{1,0:T(8,128)S(1)}, bf16[512,512]{1,0:T(8,128)(2,1)S(1)}, bf16[512,512]{1,0...) custom-call(s32[4,4]{1,0:T(4,128)S(1)} %bitcast.17, ...), custom_call_target="tpu_custom_call" | custom-call | flops 5000000000 | bytes 4000000 | tf_op jit(solution)/shard_map/gain/pallas_call | solution.py:361
  30.1 1.8 %finish.1 = (f32[64,256]{1,0:T(8,128)S(1)}, f32[64,256]{1,0:T(8,128)S(1)}) custom-call(f32[128,512]{1,0:T(8,128)S(1)} %get-tuple-element.38.start, bf16[512,512]{1,0:T(8,128)(2,1)S(1)} %get-tuple-element.39.refs_0_, bf16[512,512]{1,0:T(8,128)(2,1)S(1)} %get-tuple-element.40.refs_1_, bf16[512,512]{1,0:T(8,128)(2,1)S(1)} %get-tuple-element.41.refs_2_, ...), custom_call_target="tpu_custom_call" | custom-call | flops 600000000 | bytes 2000000 | tf_op jit(solution)/shard_map/finish/pallas_call | solution.py:377
  31.8 0.6 %collective-permute-start.10 = (f32[64,256]{1,0:T(8,128)S(1)}, f32[64,256]{1,0:T(8,128)S(1)}, u32[]{:S(2)}, u32[]{:S(2)}) collective-permute-start(f32[64,256]{1,0:T(8,128)S(1)} %get-tuple-element.48), channel_id=1, source_target_pairs={{0,8},{8,0},{16,24},{24,16},{1,9},{9,1},{17,25},{25,17},{2,10},{10... | collective-permute-start | bytes 196616 | tf_op jit(solution)/shard_map/ppermute | solution.py:390
  32.4 1.0 %collective-permute-start.11 = (f32[64,256]{1,0:T(8,128)S(1)}, f32[64,256]{1,0:T(8,128)S(1)}, u32[]{:S(2)}, u32[]{:S(2)}) collective-permute-start(f32[64,256]{1,0:T(8,128)S(1)} %get-tuple-element.49), channel_id=1, source_target_pairs={{0,16},{8,24},{16,0},{24,8},{1,17},{9,25},{17,1},{25,9},{2,18},{10... | collective-permute-start | bytes 196616 | tf_op jit(solution)/shard_map/ppermute | solution.py:390
  33.4 0.4 %collective-permute-start.12 = (f32[64,256]{1,0:T(8,128)S(1)}, f32[64,256]{1,0:T(8,128)S(1)}, u32[]{:S(2)}, u32[]{:S(2)}) collective-permute-start(f32[64,256]{1,0:T(8,128)S(1)} %get-tuple-element.50), channel_id=1, source_target_pairs={{0,24},{8,16},{16,8},{24,0},{1,25},{9,17},{17,9},{25,1},{2,26},{10... | collective-permute-start | bytes 196616 | tf_op jit(solution)/shard_map/ppermute | solution.py:390
  33.8 3.1 %collective-permute-done.11.refs_2_ = f32[64,256]{1,0:T(8,128)S(1)} collective-permute-done((f32[64,256]{1,0:T(8,128)S(1)}, f32[64,256]{1,0:T(8,128)S(1)}, u32[]{:S(2)}, u32[]{:S(2)}) %collective-permute-start.11) | collective-permute-done | bytes 65568 | tf_op jit(solution)/shard_map/ppermute | solution.py:390
  37.0 0.8 %collective-permute-done.12.refs_3_ = f32[64,256]{1,0:T(8,128)S(1)} collective-permute-done((f32[64,256]{1,0:T(8,128)S(1)}, f32[64,256]{1,0:T(8,128)S(1)}, u32[]{:S(2)}, u32[]{:S(2)}) %collective-permute-start.12) | collective-permute-done | bytes 65568 | tf_op jit(solution)/shard_map/ppermute | solution.py:390
  37.8 0.8 %place.1 = f32[64,2,512]{2,1,0:T(2,128)} custom-call(f32[64,256]{1,0:T(8,128)S(1)} %get-tuple-element.47.refs_0_, f32[64,256]{1,0:T(8,128)S(1)} %collective-permute-done.10.refs_1_, f32[64,256]{1,0:T(8,128)S(1)} %collective-permute-done.11.refs_2_, f32[64,256]{1,0:T(8,128)S(1)} %collective-permute-done.12.refs_3_), custom_call_target="tpu_custom_call" | custom-call | flops 100000 | bytes 600000 | tf_op jit(solution)/shard_map/place/pallas_call | solution.py:391
  (25 shorter events, 0.2 us)
Async XLA Ops:
  0.0 1.0 %copy-start.1 = (f32[2,512]{1,0:T(2,128)S(1)}, f32[2,512]{1,0:T(2,128)}, u32[]{:S(2)}) copy-start(f32[2,512]{1,0:T(2,128)} %dif.3) | copy-start | bytes 12292
  0.0 1.0 %copy-start.2 = (f32[2,512]{1,0:T(2,128)S(1)}, f32[2,512]{1,0:T(2,128)}, u32[]{:S(2)}) copy-start(f32[2,512]{1,0:T(2,128)} %wind.3) | copy-start | bytes 12292
  1.0 14.0 %copy-start = (f32[64,2,512]{2,1,0:T(2,128)S(1)}, f32[64,2,512]{2,1,0:T(2,128)}, u32[]{:S(2)}) copy-start(f32[64,2,512]{2,1,0:T(2,128)} %own.3) | copy-start | bytes 786436
  1.1 14.0 %copy-start.4 = (s32[1,4,4]{2,1,0:T(4,128)S(1)}, s32[1,4,4]{2,1,0:T(4,128)}, u32[]{:S(2)}) copy-start(s32[1,4,4]{2,1,0:T(4,128)} %param.10) | copy-start | bytes 196
  1.1 14.0 %copy-start.5 = (f32[1,1,512]{2,1,0:T(1,128)S(1)}, f32[1,1,512]{2,1,0:T(1,128)}, u32[]{:S(2)}) copy-start(f32[1,1,512]{2,1,0:T(1,128)} %param.12) | copy-start | bytes 6148
  1.1 14.0 %copy-start.6 = (f32[1,1,512]{2,1,0:T(1,128)S(1)}, f32[1,1,512]{2,1,0:T(1,128)}, u32[]{:S(2)}) copy-start(f32[1,1,512]{2,1,0:T(1,128)} %param.13) | copy-start | bytes 6148
  1.2 13.9 %copy-start.3 = (s32[1,4,512]{2,1,0:T(4,128)S(1)}, s32[1,4,512]{2,1,0:T(4,128)}, u32[]{:S(2)}) copy-start(s32[1,4,512]{2,1,0:T(4,128)} %param.11) | copy-start | bytes 24580
  1.2 7.6 %collective-permute-start = (f32[34,2,512]{2,1,0:T(2,128)S(1)}, f32[34,2,512]{2,1,0:T(2,128)S(1)}, u32[]{:S(2)}, u32[]{:S(2)}) collective-permute-start(f32[34,2,512]{2,1,0:T(2,128)S(1)} %pad_maximum_fusion), channel_id=1, source_target_pairs={{0,1},{1,0},{2,3},{3,2},{4,5},{5,4},{6,7},{7,6},{8,9},{9,8},{10,11... | collective-permute-start | bytes 417800 | tf_op jit(solution)/shard_map/ppermute | solution.py:296
  4.2 7.3 %collective-permute-start.3 = (f32[32,2,512]{2,1,0:T(2,128)S(1)}, f32[32,2,512]{2,1,0:T(2,128)S(1)}, u32[]{:S(2)}, u32[]{:S(2)}) collective-permute-start(f32[32,2,512]{2,1,0:T(2,128)S(1)} %get-tuple-element.51), channel_id=1, source_target_pairs={{0,1},{1,0},{2,3},{3,2},{4,5},{5,4},{6,7},{7,6},{8,9},{9,8},{10,11... | collective-permute-start | bytes 393224 | tf_op jit(solution)/shard_map/ppermute | solution.py:296
  8.8 6.3 %collective-permute-start.1 = (f32[34,2,512]{2,1,0:T(2,128)S(1)}, f32[34,2,512]{2,1,0:T(2,128)S(1)}, u32[]{:S(2)}, u32[]{:S(2)}) collective-permute-start(f32[34,2,512]{2,1,0:T(2,128)S(1)} %collective-permute-done.near.coef_near), channel_id=1, source_target_pairs={{0,2},{2,4},{4,6},{3,1},{5,3},{7,5},{6,7},{1,0},{8,10},{10,12},{12... | collective-permute-start | bytes 417800 | tf_op jit(solution)/shard_map/ppermute | solution.py:298
  11.6 6.0 %collective-permute-start.4 = (f32[32,2,512]{2,1,0:T(2,128)S(1)}, f32[32,2,512]{2,1,0:T(2,128)S(1)}, u32[]{:S(2)}, u32[]{:S(2)}) collective-permute-start(f32[32,2,512]{2,1,0:T(2,128)S(1)} %collective-permute-done.3.near), channel_id=1, source_target_pairs={{0,2},{2,4},{4,6},{3,1},{5,3},{7,5},{6,7},{1,0},{8,10},{10,12},{12... | collective-permute-start | bytes 393224 | tf_op jit(solution)/shard_map/ppermute | solution.py:298
  15.6 5.8 %collective-permute-start.6 = (f32[32,1024]{1,0:T(8,128)S(1)}, f32[32,1024]{1,0:T(8,128)S(1)}, u32[]{:S(2)}, u32[]{:S(2)}) collective-permute-start(f32[32,1024]{1,0:T(8,128)S(1)} %shard_map.73.refs_0_.refs_6_.refs_8_), channel_id=1, source_target_pairs={{0,16},{8,24},{16,0},{24,8},{1,17},{9,25},{17,1},{25,9},{2,18},{10... | collective-permute-start | bytes 393224 | tf_op jit(solution)/shard_map/ppermute | solution.py:322
  18.1 5.0 %collective-permute-start.8 = (f32[32,1024]{1,0:T(8,128)S(1)}, f32[32,1024]{1,0:T(8,128)S(1)}, u32[]{:S(2)}, u32[]{:S(2)}) collective-permute-start(f32[32,1024]{1,0:T(8,128)S(1)} %shard_map.74.refs_2_.refs_8_.refs_10_), channel_id=1, source_target_pairs={{0,16},{8,24},{16,0},{24,8},{1,17},{9,25},{17,1},{25,9},{2,18},{10... | collective-permute-start | bytes 393224 | tf_op jit(solution)/shard_map/ppermute | solution.py:322
  19.1 4.0 %collective-permute-start.2 = (f32[32,1024]{1,0:T(8,128)S(1)}, f32[32,1024]{1,0:T(8,128)S(1)}, u32[]{:S(2)}, u32[]{:S(2)}) collective-permute-start(f32[32,1024]{1,0:T(8,128)S(1)} %shard_map.73.refs_0_.refs_6_.refs_8_), channel_id=1, source_target_pairs={{0,8},{8,0},{16,24},{24,16},{1,9},{9,1},{17,25},{25,17},{2,10},{10... | collective-permute-start | bytes 393224 | tf_op jit(solution)/shard_map/ppermute | solution.py:305
  19.1 4.0 %collective-permute-start.5 = (f32[32,1024]{1,0:T(8,128)S(1)}, f32[32,1024]{1,0:T(8,128)S(1)}, u32[]{:S(2)}, u32[]{:S(2)}) collective-permute-start(f32[32,1024]{1,0:T(8,128)S(1)} %shard_map.74.refs_2_.refs_8_.refs_10_), channel_id=1, source_target_pairs={{0,8},{8,0},{16,24},{24,16},{1,9},{9,1},{17,25},{25,17},{2,10},{10... | collective-permute-start | bytes 393224 | tf_op jit(solution)/shard_map/ppermute | solution.py:305
  21.4 3.1 %collective-permute-start.7 = (f32[32,1024]{1,0:T(8,128)S(1)}, f32[32,1024]{1,0:T(8,128)S(1)}, u32[]{:S(2)}, u32[]{:S(2)}) collective-permute-start(f32[32,1024]{1,0:T(8,128)S(1)} %collective-permute-done.6.refs_4_.refs_10_), channel_id=1, source_target_pairs={{0,8},{8,0},{16,24},{24,16},{1,9},{9,1},{17,25},{25,17},{2,10},{10... | collective-permute-start | bytes 393224 | tf_op jit(solution)/shard_map/ppermute | solution.py:305
  23.1 2.5 %collective-permute-start.9 = (f32[32,1024]{1,0:T(8,128)S(1)}, f32[32,1024]{1,0:T(8,128)S(1)}, u32[]{:S(2)}, u32[]{:S(2)}) collective-permute-start(f32[32,1024]{1,0:T(8,128)S(1)} %collective-permute-done.8.refs_12_), channel_id=1, source_target_pairs={{0,8},{8,0},{16,24},{24,16},{1,9},{9,1},{17,25},{25,17},{2,10},{10... | collective-permute-start | bytes 393224 | tf_op jit(solution)/shard_map/ppermute | solution.py:305
  31.8 2.0 %collective-permute-start.10 = (f32[64,256]{1,0:T(8,128)S(1)}, f32[64,256]{1,0:T(8,128)S(1)}, u32[]{:S(2)}, u32[]{:S(2)}) collective-permute-start(f32[64,256]{1,0:T(8,128)S(1)} %get-tuple-element.48), channel_id=1, source_target_pairs={{0,8},{8,0},{16,24},{24,16},{1,9},{9,1},{17,25},{25,17},{2,10},{10... | collective-permute-start | bytes 196616 | tf_op jit(solution)/shard_map/ppermute | solution.py:390
  32.4 4.6 %collective-permute-start.11 = (f32[64,256]{1,0:T(8,128)S(1)}, f32[64,256]{1,0:T(8,128)S(1)}, u32[]{:S(2)}, u32[]{:S(2)}) collective-permute-start(f32[64,256]{1,0:T(8,128)S(1)} %get-tuple-element.49), channel_id=1, source_target_pairs={{0,16},{8,24},{16,0},{24,8},{1,17},{9,25},{17,1},{25,9},{2,18},{10... | collective-permute-start | bytes 196616 | tf_op jit(solution)/shard_map/ppermute | solution.py:390
  33.4 4.4 %collective-permute-start.12 = (f32[64,256]{1,0:T(8,128)S(1)}, f32[64,256]{1,0:T(8,128)S(1)}, u32[]{:S(2)}, u32[]{:S(2)}) collective-permute-start(f32[64,256]{1,0:T(8,128)S(1)} %get-tuple-element.50), channel_id=1, source_target_pairs={{0,24},{8,16},{16,8},{24,0},{1,25},{9,17},{17,9},{25,1},{2,26},{10... | collective-permute-start | bytes 196616 | tf_op jit(solution)/shard_map/ppermute | solution.py:390

commit v9 on v8

--- a/solution.py
+++ b/solution.py
@@ -183,11 +183,10 @@
 
 
 def gain_kernel(earlier, last, near_parts, order, longitudes, blocks, flags, values, errors, *refs):
-    cov, left = refs[-1], refs[-10:-1]
-    outs = refs[4 + earlier + len(order) : -10]
+    cov, left = refs[-1], refs[-11:-1]
+    outs = refs[4 + earlier + len(order) : -11]
     before, first_seen, parts = refs[:4], refs[4 : 4 + earlier], refs[4 + earlier : 4 + earlier + len(order)]
     own_cells = outs[0].shape[1]
-    near_rows = left[0].shape[0]
     total = sum(part.shape[0] for part in parts)
     last_seen, last_cells = observe(parts[-last:], longitudes, own_cells, blocks, flags)
     square_sum, cross, seen_mean, _ = moments(last_seen, last_cells, (before[2][...], before[3][...]), total)
@@ -203,17 +202,21 @@
     root = lax.rsqrt(jnp.sum(size, axis=0, keepdims=True))
     root_down = lax.rsqrt(jnp.sum(size, axis=1, keepdims=True))
     cross = split((cross + before[1][...]) * root_down)
-    seen = jnp.concatenate([ref[...] for ref in first_seen] + [last_seen], axis=0)
-    start = ((values[...] - seen_mean) - 0.5 * (seen - seen_mean)) * root
+    seen = jnp.concatenate([ref[...] for ref in first_seen[1:]] + [last_seen], axis=0)
+    start = weights(seen, seen_mean, values, root)
     b1 = (covariance * root_down) * root
     s1 = split(b1)
     b2 = 2.0 * b1 - square(s1)
     s2 = split(b2)
     b4 = 2.0 * b2 - square(s2)
     s4 = split(b4)
-    for out, value in zip(left, (start[:near_rows],) + s4 + s2 + s1 + cross):
+    for out, value in zip(left, (seen_mean, root) + s4 + s2 + s1 + cross):
         out[...] = value
-    finish(start[near_rows:], s4, (s2, s1), cross, parts[near_parts:], order[near_parts:], outs)
+    finish(start, s4, (s2, s1), cross, parts[near_parts:], order[near_parts:], outs)
+
+
+def weights(seen, seen_mean, values, root):
+    return ((values[...] - seen_mean) - 0.5 * (seen - seen_mean)) * root
 
 
 def finish(start, s4, factors, cross, parts, order, outs):
@@ -230,10 +233,11 @@
         at += size
 
 
-def finish_kernel(order, start, *refs):
+def finish_kernel(order, seen, values, seen_mean, root, *refs):
     s4, s2, s1, cross = [(refs[i][...], refs[i + 1][...]) for i in (0, 2, 4, 6)]
     parts, outs = refs[8 : 8 + len(order)], refs[8 + len(order) :]
-    finish(start[...], s4, (s2, s1), cross, parts, order, outs)
+    start = weights(seen[...], seen_mean[...], values, root[...])
+    finish(start, s4, (s2, s1), cross, parts, order, outs)
 
 
 def place_kernel(masks, longitudes, *refs):
@@ -357,17 +361,16 @@
     far_mems = mems - mems // 2
     part_of_product = [jax.ShapeDtypeStruct((observations, observations), BF16)] * 2
     part_of_cross = [jax.ShapeDtypeStruct((observations, own_cells), BF16)] * 2
-    near_rows = local * (mems // 2)
     done = pl.pallas_call(
         functools.partial(
             gain_kernel, len(seen), len(stage), near_parts, near_order + far_order, longitudes
         ),
         out_shape=[to_member] * far_mems
-        + [jax.ShapeDtypeStruct((near_rows, observations), F32)]
+        + [jax.ShapeDtypeStruct((1, observations), F32)] * 2
         + part_of_product * 3
         + part_of_cross,
         in_specs=[SMEM] + [VMEM] * (3 + len(before) + len(seen) + len(flat)),
-        out_specs=[VMEM] * (far_mems + 9),
+        out_specs=[VMEM] * (far_mems + 10),
         scratch_shapes=[pltpu.VMEM((observations, observations), F32)],
         cost_estimate=pl.CostEstimate(flops=5000000000, bytes_accessed=4000000, transcendentals=0),
         compiler_params=pltpu.CompilerParams(vmem_limit_bytes=24 << 20),
@@ -377,12 +380,12 @@
     near_outs = pl.pallas_call(
         functools.partial(finish_kernel, near_order),
         out_shape=[to_member] * (mems // 2),
-        in_specs=[VMEM] * (9 + near_parts),
+        in_specs=[VMEM] * (12 + near_parts),
         out_specs=[VMEM] * (mems // 2),
         cost_estimate=pl.CostEstimate(flops=600000000, bytes_accessed=2000000, transcendentals=0),
         compiler_params=pltpu.CompilerParams(vmem_limit_bytes=16 << 20),
         name="finish",
-    )(*done[far_mems:], *flat[:near_parts])
+    )(seen[0], observed_values[0], *done[far_mems:], *flat[:near_parts])
     outs = list(near_outs) + list(far_outs)
     came = {0: outs[0]}
     for mask in sorted(masks[1:], reverse=True):

time: 38.7 us -> 38.7 us (level)
  no operation moved by 1% of the time
where the time goes in v9:
time: 38.7 us; the launch traced here: 38.6 us
  waiting for transfers between devices  15.1 us (39%)
  starting transfers between devices  11.7 us (30%)
  Pallas kernels  10.5 us (27%)
  local copies, waits for them, and re-layouts  1.05 us (3%)
    ppermute x2, waiting for transfers between devices, body(): near.append(lax.ppermute(own, 'lat', near_pairs))  5.17 us
    pallas_call x1, Pallas kernels, body(): pl.pallas_call(functools.partial(gain_kernel, len(seen), len(stage), near...  4.42 us
    ppermute x3, waiting for transfers between devices, body(): came[mask] = lax.ppermute(outs[masks.index(mask)], 'mem', pairs)  3.92 us
    ppermute x2, waiting for transfers between devices, body(): far_half.append(lax.ppermute(band, 'mem', xor_pairs(mems, top)))  3.47 us
    ppermute x2, starting transfers between devices, body(): near.append(lax.ppermute(own, 'lat', near_pairs))  3.14 us
    ppermute x2, starting transfers between devices, body(): far.append(lax.ppermute(near[k], 'lat', far_pairs))  3.02 us
    ppermute x2, starting transfers between devices, body(): far_half.append(lax.ppermute(band, 'mem', xor_pairs(mems, top)))  2.96 us
    ppermute x2, waiting for transfers between devices, body(): far.append(lax.ppermute(near[k], 'lat', far_pairs))  2.54 us
  transfers between devices with their start and end apart: 13, of which 7 were waited for; matrix products, arithmetic and copies ran while one was open for 0% of the time, Pallas kernels for 9%

profile of v9, /device:TPU:0, one launch (start us, length us, event | category | flops | bytes accessed | tf_op | source)
XLA Modules:
  0.0 38.6 jit_solution(6906674186172924995)
XLA Ops:
  0.0 1.0 %fusion = (f32[32,2,512]{2,1,0:T(2,128)S(1)}, f32[32,2,512]{2,1,0:T(2,128)S(1)}) fusion(f32[64,2,512]{2,1,0:T(2,128)} %own.3), kind=kLoop, calls=%fused_computation.1 | loop fusion | bytes 524288 | tf_op jit(solution)/shard_map/slice | solution.py:297
  1.2 3.1 %collective-permute-start = (f32[34,2,512]{2,1,0:T(2,128)S(1)}, f32[34,2,512]{2,1,0:T(2,128)S(1)}, u32[]{:S(2)}, u32[]{:S(2)}) collective-permute-start(f32[34,2,512]{2,1,0:T(2,128)S(1)} %pad_maximum_fusion), channel_id=1, source_target_pairs={{0,1},{1,0},{2,3},{3,2},{4,5},{5,4},{6,7},{7,6},{8,9},{9,8},{10,11... | collective-permute-start | bytes 417800 | tf_op jit(solution)/shard_map/ppermute | solution.py:300
  4.3 4.4 %collective-permute-done.near.coef_near = f32[34,2,512]{2,1,0:T(2,128)S(1)} collective-permute-done((f32[34,2,512]{2,1,0:T(2,128)S(1)}, f32[34,2,512]{2,1,0:T(2,128)S(1)}, u32[]{:S(2)}, u32[]{:S(2)}) %collective-permute-start) | collective-permute-done | bytes 139296 | tf_op jit(solution)/shard_map/ppermute | solution.py:300
  8.8 2.1 %collective-permute-start.1 = (f32[34,2,512]{2,1,0:T(2,128)S(1)}, f32[34,2,512]{2,1,0:T(2,128)S(1)}, u32[]{:S(2)}, u32[]{:S(2)}) collective-permute-start(f32[34,2,512]{2,1,0:T(2,128)S(1)} %collective-permute-done.near.coef_near), channel_id=1, source_target_pairs={{0,2},{2,4},{4,6},{3,1},{5,3},{7,5},{6,7},{1,0},{8,10},{10,12},{12... | collective-permute-start | bytes 417800 | tf_op jit(solution)/shard_map/ppermute | solution.py:302
  10.8 0.7 %collective-permute-done.3.near = f32[32,2,512]{2,1,0:T(2,128)S(1)} collective-permute-done((f32[32,2,512]{2,1,0:T(2,128)S(1)}, f32[32,2,512]{2,1,0:T(2,128)S(1)}, u32[]{:S(2)}, u32[]{:S(2)}) %collective-permute-start.3) | collective-permute-done | bytes 131104 | tf_op jit(solution)/shard_map/ppermute | solution.py:300
  11.6 0.9 %collective-permute-start.4 = (f32[32,2,512]{2,1,0:T(2,128)S(1)}, f32[32,2,512]{2,1,0:T(2,128)S(1)}, u32[]{:S(2)}, u32[]{:S(2)}) collective-permute-start(f32[32,2,512]{2,1,0:T(2,128)S(1)} %collective-permute-done.3.near), channel_id=1, source_target_pairs={{0,2},{2,4},{4,6},{3,1},{5,3},{7,5},{6,7},{1,0},{8,10},{10,12},{12... | collective-permute-start | bytes 393224 | tf_op jit(solution)/shard_map/ppermute | solution.py:302
  12.5 2.5 %collective-permute-done.1.far.coef_far = f32[34,2,512]{2,1,0:T(2,128)S(1)} collective-permute-done((f32[34,2,512]{2,1,0:T(2,128)S(1)}, f32[34,2,512]{2,1,0:T(2,128)S(1)}, u32[]{:S(2)}, u32[]{:S(2)}) %collective-permute-start.1) | collective-permute-done | bytes 139296 | tf_op jit(solution)/shard_map/ppermute | solution.py:302
  15.1 0.5 %shard_map.73.refs_0_.refs_6_.refs_8_ = f32[32,1024]{1,0:T(8,128)S(1)} custom-call(f32[64,2,512]{2,1,0:T(2,128)S(1)} %copy-done, f32[2,512]{1,0:T(2,128)S(1)} %copy-done.1, f32[2,512]{1,0:T(2,128)S(1)} %copy-done.2, f32[34,2,512]{2,1,0:T(2,128)S(1)} %collective-permute-done.near.coef_near, f32[34,2,512]{2,1,0:T(2,128)S(1)} %collective-permute-done.1.far.coef_far, ...), custom_call_target="tpu_custom_call" | custom-call | flops 2000000 | bytes 2000000 | tf_op jit(solution)/shard_map/pallas_call | solution.py:318
  15.6 1.9 %collective-permute-start.6 = (f32[32,1024]{1,0:T(8,128)S(1)}, f32[32,1024]{1,0:T(8,128)S(1)}, u32[]{:S(2)}, u32[]{:S(2)}) collective-permute-start(f32[32,1024]{1,0:T(8,128)S(1)} %shard_map.73.refs_0_.refs_6_.refs_8_), channel_id=1, source_target_pairs={{0,16},{8,24},{16,0},{24,8},{1,17},{9,25},{17,1},{25,9},{2,18},{10... | collective-permute-start | bytes 393224 | tf_op jit(solution)/shard_map/ppermute | solution.py:326
  17.5 0.5 %shard_map.74.refs_2_.refs_8_.refs_10_ = f32[32,1024]{1,0:T(8,128)S(1)} custom-call(f32[64,2,512]{2,1,0:T(2,128)S(1)} %copy-done, f32[2,512]{1,0:T(2,128)S(1)} %copy-done.1, f32[2,512]{1,0:T(2,128)S(1)} %copy-done.2, f32[32,2,512]{2,1,0:T(2,128)S(1)} %collective-permute-done.3.near, f32[32,2,512]{2,1,0:T(2,128)S(1)} %collective-permute-done.4.far, ...), custom_call_target="tpu_custom_call" | custom-call | flops 2000000 | bytes 2000000 | tf_op jit(solution)/shard_map/pallas_call | solution.py:318
  18.1 1.0 %collective-permute-start.8 = (f32[32,1024]{1,0:T(8,128)S(1)}, f32[32,1024]{1,0:T(8,128)S(1)}, u32[]{:S(2)}, u32[]{:S(2)}) collective-permute-start(f32[32,1024]{1,0:T(8,128)S(1)} %shard_map.74.refs_2_.refs_8_.refs_10_), channel_id=1, source_target_pairs={{0,16},{8,24},{16,0},{24,8},{1,17},{9,25},{17,1},{25,9},{2,18},{10... | collective-permute-start | bytes 393224 | tf_op jit(solution)/shard_map/ppermute | solution.py:326
  19.1 0.5 %collective-permute-start.5 = (f32[32,1024]{1,0:T(8,128)S(1)}, f32[32,1024]{1,0:T(8,128)S(1)}, u32[]{:S(2)}, u32[]{:S(2)}) collective-permute-start(f32[32,1024]{1,0:T(8,128)S(1)} %shard_map.74.refs_2_.refs_8_.refs_10_), channel_id=1, source_target_pairs={{0,8},{8,0},{16,24},{24,16},{1,9},{9,1},{17,25},{25,17},{2,10},{10... | collective-permute-start | bytes 393224 | tf_op jit(solution)/shard_map/ppermute | solution.py:309
  19.6 1.8 %collective-permute-done.6.refs_4_.refs_10_ = f32[32,1024]{1,0:T(8,128)S(1)} collective-permute-done((f32[32,1024]{1,0:T(8,128)S(1)}, f32[32,1024]{1,0:T(8,128)S(1)}, u32[]{:S(2)}, u32[]{:S(2)}) %collective-permute-start.6) | collective-permute-done | bytes 131104 | tf_op jit(solution)/shard_map/ppermute | solution.py:326
  21.4 1.7 %collective-permute-done.8.refs_12_ = f32[32,1024]{1,0:T(8,128)S(1)} collective-permute-done((f32[32,1024]{1,0:T(8,128)S(1)}, f32[32,1024]{1,0:T(8,128)S(1)}, u32[]{:S(2)}, u32[]{:S(2)}) %collective-permute-start.8) | collective-permute-done | bytes 131104 | tf_op jit(solution)/shard_map/ppermute | solution.py:326
  23.1 1.4 %shard_map.75 = (f32[512,512]{1,0:T(8,128)S(1)}, f32[512,256]{1,0:T(8,128)S(1)}, f32[1,512]{1,0:T(1,128)S(1)}, f32[1,256]{1,0:T(1,128)S(1)}, f32[128,512]{1,0:T(8,128)S(1)}) custom-call(s32[4,4]{1,0:T(4,128)S(1)} %bitcast.19, s32[4,512]{1,0:T(4,128)S(1)} %bitcast.10, f32[32,1024]{1,0:T(8,128)S(1)} %shard_map.73.refs_0_.refs_6_.refs_8_, ...), custom_call_target="tpu_custom_call" | custom-call | flops 800000000 | bytes 3000000 | tf_op jit(solution)/shard_map/pallas_call | solution.py:331
  24.5 1.1 %shard_map.76 = (f32[512,512]{1,0:T(8,128)S(1)}, f32[512,256]{1,0:T(8,128)S(1)}, f32[1,512]{1,0:T(1,128)S(1)}, f32[1,256]{1,0:T(1,128)S(1)}, f32[64,512]{1,0:T(8,128)S(1)}) custom-call(s32[4,4]{1,0:T(4,128)S(1)} %bitcast.20, s32[4,512]{1,0:T(4,128)S(1)} %bitcast.11, f32[512,512]{1,0:T(8,128)S(1)} %get-tuple-element.30.refs_0_, ...), custom_call_target="tpu_custom_call" | custom-call | flops 800000000 | bytes 3000000 | tf_op jit(solution)/shard_map/pallas_call | solution.py:331
  25.6 4.4 %gain.1 = (f32[64,256]{1,0:T(8,128)S(1)}, f32[64,256]{1,0:T(8,128)S(1)}, f32[1,512]{1,0:T(1,128)S(1)}, f32[1,512]{1,0:T(1,128)S(1)}, bf16[512,512]{1,0:T(8,128)(...) custom-call(s32[4,4]{1,0:T(4,128)S(1)} %bitcast.21, ...), custom_call_target="tpu_custom_call" | custom-call | flops 5000000000 | bytes 4000000 | tf_op jit(solution)/shard_map/gain/pallas_call | solution.py:364
  30.1 1.8 %finish.1 = (f32[64,256]{1,0:T(8,128)S(1)}, f32[64,256]{1,0:T(8,128)S(1)}) custom-call(f32[128,512]{1,0:T(8,128)S(1)} %get-tuple-element.29.refs_4_.seen, f32[1,512]{1,0:T(1,128)S(1)} %bitcast.16, f32[1,512]{1,0:T(1,128)S(1)} %get-tuple-element.39.seen_mean, f32[1,512]{1,0:T(1,128)S(1)} %get-tuple-element.40.root, ...), custom_call_target="tpu_custom_call" | custom-call | flops 600000000 | bytes 2000000 | tf_op jit(solution)/shard_map/finish/pallas_call | solution.py:380
  31.8 0.6 %collective-permute-start.10 = (f32[64,256]{1,0:T(8,128)S(1)}, f32[64,256]{1,0:T(8,128)S(1)}, u32[]{:S(2)}, u32[]{:S(2)}) collective-permute-start(f32[64,256]{1,0:T(8,128)S(1)} %get-tuple-element.50), channel_id=1, source_target_pairs={{0,8},{8,0},{16,24},{24,16},{1,9},{9,1},{17,25},{25,17},{2,10},{10... | collective-permute-start | bytes 196616 | tf_op jit(solution)/shard_map/ppermute | solution.py:393
  32.4 1.0 %collective-permute-start.11 = (f32[64,256]{1,0:T(8,128)S(1)}, f32[64,256]{1,0:T(8,128)S(1)}, u32[]{:S(2)}, u32[]{:S(2)}) collective-permute-start(f32[64,256]{1,0:T(8,128)S(1)} %get-tuple-element.51), channel_id=1, source_target_pairs={{0,16},{8,24},{16,0},{24,8},{1,17},{9,25},{17,1},{25,9},{2,18},{10... | collective-permute-start | bytes 196616 | tf_op jit(solution)/shard_map/ppermute | solution.py:393
  33.4 0.5 %collective-permute-start.12 = (f32[64,256]{1,0:T(8,128)S(1)}, f32[64,256]{1,0:T(8,128)S(1)}, u32[]{:S(2)}, u32[]{:S(2)}) collective-permute-start(f32[64,256]{1,0:T(8,128)S(1)} %get-tuple-element.52), channel_id=1, source_target_pairs={{0,24},{8,16},{16,8},{24,0},{1,25},{9,17},{17,9},{25,1},{2,26},{10... | collective-permute-start | bytes 196616 | tf_op jit(solution)/shard_map/ppermute | solution.py:393
  33.9 3.2 %collective-permute-done.11.refs_2_ = f32[64,256]{1,0:T(8,128)S(1)} collective-permute-done((f32[64,256]{1,0:T(8,128)S(1)}, f32[64,256]{1,0:T(8,128)S(1)}, u32[]{:S(2)}, u32[]{:S(2)}) %collective-permute-start.11) | collective-permute-done | bytes 65568 | tf_op jit(solution)/shard_map/ppermute | solution.py:393
  37.0 0.8 %collective-permute-done.12.refs_3_ = f32[64,256]{1,0:T(8,128)S(1)} collective-permute-done((f32[64,256]{1,0:T(8,128)S(1)}, f32[64,256]{1,0:T(8,128)S(1)}, u32[]{:S(2)}, u32[]{:S(2)}) %collective-permute-start.12) | collective-permute-done | bytes 65568 | tf_op jit(solution)/shard_map/ppermute | solution.py:393
  37.8 0.8 %place.1 = f32[64,2,512]{2,1,0:T(2,128)} custom-call(f32[64,256]{1,0:T(8,128)S(1)} %get-tuple-element.49.refs_0_, f32[64,256]{1,0:T(8,128)S(1)} %collective-permute-done.10.refs_1_, f32[64,256]{1,0:T(8,128)S(1)} %collective-permute-done.11.refs_2_, f32[64,256]{1,0:T(8,128)S(1)} %collective-permute-done.12.refs_3_), custom_call_target="tpu_custom_call" | custom-call | flops 100000 | bytes 600000 | tf_op jit(solution)/shard_map/place/pallas_call | solution.py:394
  (25 shorter events, 0.2 us)
Async XLA Ops:
  0.0 1.0 %copy-start.1 = (f32[2,512]{1,0:T(2,128)S(1)}, f32[2,512]{1,0:T(2,128)}, u32[]{:S(2)}) copy-start(f32[2,512]{1,0:T(2,128)} %dif.3) | copy-start | bytes 12292
  0.0 1.0 %copy-start.2 = (f32[2,512]{1,0:T(2,128)S(1)}, f32[2,512]{1,0:T(2,128)}, u32[]{:S(2)}) copy-start(f32[2,512]{1,0:T(2,128)} %wind.3) | copy-start | bytes 12292
  1.0 14.0 %copy-start = (f32[64,2,512]{2,1,0:T(2,128)S(1)}, f32[64,2,512]{2,1,0:T(2,128)}, u32[]{:S(2)}) copy-start(f32[64,2,512]{2,1,0:T(2,128)} %own.3) | copy-start | bytes 786436
  1.1 14.0 %copy-start.4 = (f32[1,1,512]{2,1,0:T(1,128)S(1)}, f32[1,1,512]{2,1,0:T(1,128)}, u32[]{:S(2)}) copy-start(f32[1,1,512]{2,1,0:T(1,128)} %param.12) | copy-start | bytes 6148
  1.1 14.0 %copy-start.5 = (s32[1,4,4]{2,1,0:T(4,128)S(1)}, s32[1,4,4]{2,1,0:T(4,128)}, u32[]{:S(2)}) copy-start(s32[1,4,4]{2,1,0:T(4,128)} %param.10) | copy-start | bytes 196
  1.1 14.0 %copy-start.6 = (f32[1,1,512]{2,1,0:T(1,128)S(1)}, f32[1,1,512]{2,1,0:T(1,128)}, u32[]{:S(2)}) copy-start(f32[1,1,512]{2,1,0:T(1,128)} %param.13) | copy-start | bytes 6148
  1.2 13.9 %copy-start.3 = (s32[1,4,512]{2,1,0:T(4,128)S(1)}, s32[1,4,512]{2,1,0:T(4,128)}, u32[]{:S(2)}) copy-start(s32[1,4,512]{2,1,0:T(4,128)} %param.11) | copy-start | bytes 24580
  1.2 7.6 %collective-permute-start = (f32[34,2,512]{2,1,0:T(2,128)S(1)}, f32[34,2,512]{2,1,0:T(2,128)S(1)}, u32[]{:S(2)}, u32[]{:S(2)}) collective-permute-start(f32[34,2,512]{2,1,0:T(2,128)S(1)} %pad_maximum_fusion), channel_id=1, source_target_pairs={{0,1},{1,0},{2,3},{3,2},{4,5},{5,4},{6,7},{7,6},{8,9},{9,8},{10,11... | collective-permute-start | bytes 417800 | tf_op jit(solution)/shard_map/ppermute | solution.py:300
  4.2 7.3 %collective-permute-start.3 = (f32[32,2,512]{2,1,0:T(2,128)S(1)}, f32[32,2,512]{2,1,0:T(2,128)S(1)}, u32[]{:S(2)}, u32[]{:S(2)}) collective-permute-start(f32[32,2,512]{2,1,0:T(2,128)S(1)} %get-tuple-element.53), channel_id=1, source_target_pairs={{0,1},{1,0},{2,3},{3,2},{4,5},{5,4},{6,7},{7,6},{8,9},{9,8},{10,11... | collective-permute-start | bytes 393224 | tf_op jit(solution)/shard_map/ppermute | solution.py:300
  8.8 6.3 %collective-permute-start.1 = (f32[34,2,512]{2,1,0:T(2,128)S(1)}, f32[34,2,512]{2,1,0:T(2,128)S(1)}, u32[]{:S(2)}, u32[]{:S(2)}) collective-permute-start(f32[34,2,512]{2,1,0:T(2,128)S(1)} %collective-permute-done.near.coef_near), channel_id=1, source_target_pairs={{0,2},{2,4},{4,6},{3,1},{5,3},{7,5},{6,7},{1,0},{8,10},{10,12},{12... | collective-permute-start | bytes 417800 | tf_op jit(solution)/shard_map/ppermute | solution.py:302
  11.6 6.0 %collective-permute-start.4 = (f32[32,2,512]{2,1,0:T(2,128)S(1)}, f32[32,2,512]{2,1,0:T(2,128)S(1)}, u32[]{:S(2)}, u32[]{:S(2)}) collective-permute-start(f32[32,2,512]{2,1,0:T(2,128)S(1)} %collective-permute-done.3.near), channel_id=1, source_target_pairs={{0,2},{2,4},{4,6},{3,1},{5,3},{7,5},{6,7},{1,0},{8,10},{10,12},{12... | collective-permute-start | bytes 393224 | tf_op jit(solution)/shard_map/ppermute | solution.py:302
  15.6 5.8 %collective-permute-start.6 = (f32[32,1024]{1,0:T(8,128)S(1)}, f32[32,1024]{1,0:T(8,128)S(1)}, u32[]{:S(2)}, u32[]{:S(2)}) collective-permute-start(f32[32,1024]{1,0:T(8,128)S(1)} %shard_map.73.refs_0_.refs_6_.refs_8_), channel_id=1, source_target_pairs={{0,16},{8,24},{16,0},{24,8},{1,17},{9,25},{17,1},{25,9},{2,18},{10... | collective-permute-start | bytes 393224 | tf_op jit(solution)/shard_map/ppermute | solution.py:326
  18.1 5.0 %collective-permute-start.8 = (f32[32,1024]{1,0:T(8,128)S(1)}, f32[32,1024]{1,0:T(8,128)S(1)}, u32[]{:S(2)}, u32[]{:S(2)}) collective-permute-start(f32[32,1024]{1,0:T(8,128)S(1)} %shard_map.74.refs_2_.refs_8_.refs_10_), channel_id=1, source_target_pairs={{0,16},{8,24},{16,0},{24,8},{1,17},{9,25},{17,1},{25,9},{2,18},{10... | collective-permute-start | bytes 393224 | tf_op jit(solution)/shard_map/ppermute | solution.py:326
  19.1 4.0 %collective-permute-start.2 = (f32[32,1024]{1,0:T(8,128)S(1)}, f32[32,1024]{1,0:T(8,128)S(1)}, u32[]{:S(2)}, u32[]{:S(2)}) collective-permute-start(f32[32,1024]{1,0:T(8,128)S(1)} %shard_map.73.refs_0_.refs_6_.refs_8_), channel_id=1, source_target_pairs={{0,8},{8,0},{16,24},{24,16},{1,9},{9,1},{17,25},{25,17},{2,10},{10... | collective-permute-start | bytes 393224 | tf_op jit(solution)/shard_map/ppermute | solution.py:309
  19.1 4.0 %collective-permute-start.5 = (f32[32,1024]{1,0:T(8,128)S(1)}, f32[32,1024]{1,0:T(8,128)S(1)}, u32[]{:S(2)}, u32[]{:S(2)}) collective-permute-start(f32[32,1024]{1,0:T(8,128)S(1)} %shard_map.74.refs_2_.refs_8_.refs_10_), channel_id=1, source_target_pairs={{0,8},{8,0},{16,24},{24,16},{1,9},{9,1},{17,25},{25,17},{2,10},{10... | collective-permute-start | bytes 393224 | tf_op jit(solution)/shard_map/ppermute | solution.py:309
  21.4 3.1 %collective-permute-start.7 = (f32[32,1024]{1,0:T(8,128)S(1)}, f32[32,1024]{1,0:T(8,128)S(1)}, u32[]{:S(2)}, u32[]{:S(2)}) collective-permute-start(f32[32,1024]{1,0:T(8,128)S(1)} %collective-permute-done.6.refs_4_.refs_10_), channel_id=1, source_target_pairs={{0,8},{8,0},{16,24},{24,16},{1,9},{9,1},{17,25},{25,17},{2,10},{10... | collective-permute-start | bytes 393224 | tf_op jit(solution)/shard_map/ppermute | solution.py:309
  23.1 2.5 %collective-permute-start.9 = (f32[32,1024]{1,0:T(8,128)S(1)}, f32[32,1024]{1,0:T(8,128)S(1)}, u32[]{:S(2)}, u32[]{:S(2)}) collective-permute-start(f32[32,1024]{1,0:T(8,128)S(1)} %collective-permute-done.8.refs_12_), channel_id=1, source_target_pairs={{0,8},{8,0},{16,24},{24,16},{1,9},{9,1},{17,25},{25,17},{2,10},{10... | collective-permute-start | bytes 393224 | tf_op jit(solution)/shard_map/ppermute | solution.py:309
  31.8 2.0 %collective-permute-start.10 = (f32[64,256]{1,0:T(8,128)S(1)}, f32[64,256]{1,0:T(8,128)S(1)}, u32[]{:S(2)}, u32[]{:S(2)}) collective-permute-start(f32[64,256]{1,0:T(8,128)S(1)} %get-tuple-element.50), channel_id=1, source_target_pairs={{0,8},{8,0},{16,24},{24,16},{1,9},{9,1},{17,25},{25,17},{2,10},{10... | collective-permute-start | bytes 196616 | tf_op jit(solution)/shard_map/ppermute | solution.py:393
  32.4 4.6 %collective-permute-start.11 = (f32[64,256]{1,0:T(8,128)S(1)}, f32[64,256]{1,0:T(8,128)S(1)}, u32[]{:S(2)}, u32[]{:S(2)}) collective-permute-start(f32[64,256]{1,0:T(8,128)S(1)} %get-tuple-element.51), channel_id=1, source_target_pairs={{0,16},{8,24},{16,0},{24,8},{1,17},{9,25},{17,1},{25,9},{2,18},{10... | collective-permute-start | bytes 196616 | tf_op jit(solution)/shard_map/ppermute | solution.py:393
  33.4 4.4 %collective-permute-start.12 = (f32[64,256]{1,0:T(8,128)S(1)}, f32[64,256]{1,0:T(8,128)S(1)}, u32[]{:S(2)}, u32[]{:S(2)}) collective-permute-start(f32[64,256]{1,0:T(8,128)S(1)} %get-tuple-element.52), channel_id=1, source_target_pairs={{0,24},{8,16},{16,8},{24,0},{1,25},{9,17},{17,9},{25,1},{2,26},{10... | collective-permute-start | bytes 196616 | tf_op jit(solution)/shard_map/ppermute | solution.py:393
